TPU v7x, 32 devices: a whole 2x2x4 slice. The times are simulated.
32 devices in a mesh: group: 4 (over x, core), replica: 8 (over z, y).
Axes of the slice: x: 2, y: 2, z: 4, core: 2. Of those that a mesh axis runs over, the one named last changes fastest.
Arguments:
- tokens: bfloat16 [8, 8, 196, 768], P('replica', 'group'), may hold values from -6 to 6
- out_grad: bfloat16 [8, 8, 196, 768], P('replica', 'group'), may hold values from -6 to 6
- slot_mask: int32 [8], P('replica'), may hold values 0 or 1
- time_norm_gain: bfloat16 [768], P('group'), may hold values from 0.5 to 1.5
- time_norm_shift: bfloat16 [768], P('group'), may hold values from -2.5 to 2.5
- time_qkv: bfloat16 [768, 2304], P('group'), may hold values from -0.21875 to 0.21875
- time_qv_bias: bfloat16 [1536], P('group'), may hold values from -2.5 to 2.5
- time_proj: bfloat16 [768, 768], P('group'), may hold values from -0.4375 to 0.4375
- time_proj_bias: bfloat16 [768], P('group'), may hold values from -2.5 to 2.5
- time_fc: bfloat16 [768, 768], P('group'), may hold values from -0.21875 to 0.21875
- time_fc_bias: bfloat16 [768], P('group'), may hold values from -2.5 to 2.5
- space_norm_gain: bfloat16 [768], P('group'), may hold values from 0.5 to 1.5
- space_norm_shift: bfloat16 [768], P('group'), may hold values from -2.5 to 2.5
- space_qkv: bfloat16 [768, 2304], P('group'), may hold values from -0.21875 to 0.21875
- space_qv_bias: bfloat16 [1536], P('group'), may hold values from -2.5 to 2.5
- space_proj: bfloat16 [768, 768], P('group'), may hold values from -1.75 to 1.75
- space_proj_bias: bfloat16 [768], P('group'), may hold values from -2.5 to 2.5
- mlp_norm_gain: bfloat16 [768], P('group'), may hold values from 0.5 to 1.5
- mlp_norm_shift: bfloat16 [768], P('group'), may hold values from -2.5 to 2.5
- mlp_in: bfloat16 [768, 3072], P('group'), may hold values from -0.21875 to 0.21875
- mlp_in_bias: bfloat16 [3072], P('group'), may hold values from -2.5 to 2.5
- mlp_out: bfloat16 [3072, 768], P('group'), may hold values from -0.15625 to 0.15625
- mlp_out_bias: bfloat16 [768], P('group'), may hold values from -2.5 to 2.5
Outputs:
- layer_out: bfloat16 [8, 8, 196, 768], P('replica', 'group')
- tokens_grad: float32 [8, 8, 196, 768], P('replica', 'group')
- time_norm_gain_grad: float32 [768], P('group')
- time_norm_shift_grad: float32 [768], P('group')
- time_qkv_grad: float32 [768, 2304], P('group')
- time_qv_bias_grad: float32 [1536], P('group')
- time_proj_grad: float32 [768, 768], P('group')
- time_proj_bias_grad: float32 [768], P('group')
- time_fc_grad: float32 [768, 768], P('group')
- time_fc_bias_grad: float32 [768], P('group')
- space_norm_gain_grad: float32 [768], P('group')
- space_norm_shift_grad: float32 [768], P('group')
- space_qkv_grad: float32 [768, 2304], P('group')
- space_qv_bias_grad: float32 [1536], P('group')
- space_proj_grad: float32 [768, 768], P('group')
- space_proj_bias_grad: float32 [768], P('group')
- mlp_norm_gain_grad: float32 [768], P('group')
- mlp_norm_shift_grad: float32 [768], P('group')
- mlp_in_grad: float32 [768, 3072], P('group')
- mlp_in_bias_grad: float32 [3072], P('group')
- mlp_out_grad: float32 [3072, 768], P('group')
- mlp_out_bias_grad: float32 [768], P('group')
All inputs are finite; a program needn't handle non-finite values. No bound on the sum of `slot_mask` on one device may be relied on, other than what follows from the above.
Results may differ from a plain program's by a relative error of at most 0.02.
Values may be sent and summed in bfloat16 or wider, within the bound.
No kernel may reach another device: no remote copies, remote signals or barrier semaphores. Data moves between devices by JAX's collectives and lax.ppermute only.
A program may use at most 192 MiB of HBM per device.

v0:
```python
import jax
import jax.numpy as jnp
from jax import lax
from jax.sharding import PartitionSpec as P

D = 768
HEADS = 12
HEAD_DIM = 64
PLACES = 196


epsilon = 1e-06
time_forms = ("sfphd,sgphd->sphfg", "sphfg,sgphd->sfphd", "sphfg,sfphd->sgphd")
space_forms = ("sfphd,sfqhd->sfhpq", "sfhpq,sfqhd->sfphd", "sfhpq,sfphd->sfqhd")


def matmul(left, right):
    return jnp.dot(left, right, preferred_element_type=jnp.float32)


def times_trans(left, right):
    return lax.dot_general(
        left, right, (((1,), (1,)), ((), ())), preferred_element_type=jnp.float32
    )


def outer_sum(left, right):
    return lax.dot_general(
        left, right, (((0,), (0,)), ((), ())), preferred_element_type=jnp.float32
    )


def to_float(vector):
    return vector.astype(jnp.float32)


def column_sums(values):
    return jnp.sum(values.astype(jnp.float32), axis=0)


def layer_norm(values, gain, shift):
    average = jnp.mean(values, axis=-1, keepdims=True)
    centred = values - average
    variance = jnp.mean(centred * centred, axis=-1, keepdims=True)
    return centred * lax.rsqrt(variance + epsilon) * gain + shift


def norm_back(values, gain, shift, grad_normed):
    unused_out, pullback = jax.vjp(layer_norm, values, gain, shift)
    return pullback(grad_normed)


def gelu_exact(values):
    return jax.nn.gelu(values, approximate=False)


def qkv_rows(normed, weight, qv_bias):
    qv_float = to_float(qv_bias)
    bias_full = jnp.concatenate([qv_float[:D], jnp.zeros_like(qv_float[:D]), qv_float[D:]])
    return (matmul(normed, weight) + bias_full).astype(jnp.bfloat16)


def qv_sums(grad_packed):
    totals = column_sums(grad_packed)
    return jnp.concatenate([totals[:D], totals[2 * D :]])


def split_heads(packed, member):
    leading = packed.shape[:-1]
    return packed[..., member * D : (member + 1) * D].reshape(leading + (HEADS, HEAD_DIM))


def merge_heads(values):
    return values.reshape(values.shape[:-2] + (D,))


def attend(packed, forms):
    score_form, mix_form, back_form = forms
    query = split_heads(packed, 0)
    key_part = split_heads(packed, 1)
    value_part = split_heads(packed, 2)
    scores = jnp.einsum(
        score_form, query, key_part, preferred_element_type=jnp.float32
    ) * HEAD_DIM ** (-0.5)
    maximum = jnp.max(scores, axis=-1, keepdims=True)
    log_total = maximum + jnp.log(jnp.sum(jnp.exp(scores - maximum), axis=-1, keepdims=True))
    probs = jnp.exp(scores - log_total).astype(jnp.bfloat16)
    mixed = jnp.einsum(mix_form, probs, value_part, preferred_element_type=jnp.float32)
    return (merge_heads(mixed).astype(jnp.bfloat16), log_total)


def attend_back(packed, log_total, grad_mixed, forms):
    score_form, mix_form, back_form = forms
    score_scale = HEAD_DIM ** (-0.5)
    query = split_heads(packed, 0)
    key_part = split_heads(packed, 1)
    value_part = split_heads(packed, 2)
    grad_heads = grad_mixed.reshape(grad_mixed.shape[:-1] + (HEADS, HEAD_DIM))
    scores = (
        jnp.einsum(score_form, query, key_part, preferred_element_type=jnp.float32) * score_scale
    )
    probs = jnp.exp(scores - log_total)
    grad_value = jnp.einsum(
        back_form, probs.astype(jnp.bfloat16), grad_heads, preferred_element_type=jnp.float32
    )
    grad_probs = jnp.einsum(score_form, grad_heads, value_part, preferred_element_type=jnp.float32)
    centre = jnp.sum(grad_probs * probs, axis=-1, keepdims=True)
    grad_scores = (probs * (grad_probs - centre)).astype(jnp.bfloat16)
    grad_query = (
        jnp.einsum(mix_form, grad_scores, key_part, preferred_element_type=jnp.float32)
        * score_scale
    )
    grad_key = (
        jnp.einsum(back_form, grad_scores, query, preferred_element_type=jnp.float32) * score_scale
    )
    return jnp.concatenate(
        [merge_heads(grad_query), merge_heads(grad_key), merge_heads(grad_value)], axis=-1
    ).astype(jnp.bfloat16)


def on_device(
    tokens,
    out_grad,
    slot_mask,
    time_norm_gain,
    time_norm_shift,
    time_qkv,
    time_qv_bias,
    time_proj,
    time_proj_bias,
    time_fc,
    time_fc_bias,
    space_norm_gain,
    space_norm_shift,
    space_qkv,
    space_qv_bias,
    space_proj,
    space_proj_bias,
    mlp_norm_gain,
    mlp_norm_shift,
    mlp_in,
    mlp_in_bias,
    mlp_out,
    mlp_out_bias,
):
    shards = (
        time_norm_gain,
        time_norm_shift,
        time_qkv,
        time_qv_bias,
        time_proj,
        time_proj_bias,
        time_fc,
        time_fc_bias,
        space_norm_gain,
        space_norm_shift,
        space_qkv,
        space_qv_bias,
        space_proj,
        space_proj_bias,
        mlp_norm_gain,
        mlp_norm_shift,
        mlp_in,
        mlp_in_bias,
        mlp_out,
        mlp_out_bias,
    )
    slots_here = tokens.shape[0]
    frames_here = tokens.shape[1]
    row_count = slots_here * frames_here * PLACES
    frame_shape = (slots_here, frames_here, PLACES)
    gathered = (
        lax.all_gather(shards[0], "group", axis=0, tiled=True),
        lax.all_gather(shards[1], "group", axis=0, tiled=True),
        lax.all_gather(shards[2], "group", axis=0, tiled=True),
        lax.all_gather(shards[3], "group", axis=0, tiled=True),
        lax.all_gather(shards[4], "group", axis=0, tiled=True),
        lax.all_gather(shards[5], "group", axis=0, tiled=True),
        lax.all_gather(shards[6], "group", axis=0, tiled=True),
        lax.all_gather(shards[7], "group", axis=0, tiled=True),
        lax.all_gather(shards[8], "group", axis=0, tiled=True),
        lax.all_gather(shards[9], "group", axis=0, tiled=True),
        lax.all_gather(shards[10], "group", axis=0, tiled=True),
        lax.all_gather(shards[11], "group", axis=0, tiled=True),
        lax.all_gather(shards[12], "group", axis=0, tiled=True),
        lax.all_gather(shards[13], "group", axis=0, tiled=True),
        lax.all_gather(shards[14], "group", axis=0, tiled=True),
        lax.all_gather(shards[15], "group", axis=0, tiled=True),
        lax.all_gather(shards[16], "group", axis=0, tiled=True),
        lax.all_gather(shards[17], "group", axis=0, tiled=True),
        lax.all_gather(shards[18], "group", axis=0, tiled=True),
        lax.all_gather(shards[19], "group", axis=0, tiled=True),
    )
    tokens_flat = tokens.astype(jnp.float32).reshape(row_count, D)
    slot_live = jnp.repeat(slot_mask.astype(jnp.float32), frames_here * PLACES)[:, None]
    time_normed = layer_norm(tokens_flat, to_float(gathered[0]), to_float(gathered[1])).astype(
        jnp.bfloat16
    )
    time_packed = qkv_rows(time_normed, gathered[2], gathered[3]).reshape(frame_shape + (3 * D,))
    place_packed = lax.all_to_all(time_packed, "group", split_axis=2, concat_axis=1, tiled=True)
    place_mixed, time_total = attend(place_packed, time_forms)
    time_mixed = lax.all_to_all(
        place_mixed, "group", split_axis=1, concat_axis=2, tiled=True
    ).reshape(row_count, D)
    time_projected = (matmul(time_mixed, gathered[4]) + to_float(gathered[5])).astype(jnp.bfloat16)
    time_branch = matmul(time_projected, gathered[6]) + to_float(gathered[7])
    after_time = tokens_flat + time_branch
    space_normed = layer_norm(after_time, to_float(gathered[8]), to_float(gathered[9])).astype(
        jnp.bfloat16
    )
    space_packed = qkv_rows(space_normed, gathered[10], gathered[11]).reshape(
        frame_shape + (3 * D,)
    )
    space_mixed, space_total = attend(space_packed, space_forms)
    space_rows = space_mixed.reshape(row_count, D)
    after_space = after_time + (matmul(space_rows, gathered[12]) + to_float(gathered[13]))
    mlp_normed = layer_norm(after_space, to_float(gathered[14]), to_float(gathered[15])).astype(
        jnp.bfloat16
    )
    pre_act = matmul(mlp_normed, gathered[16]) + to_float(gathered[17])
    activated = gelu_exact(pre_act).astype(jnp.bfloat16)
    after_mlp = after_space + (matmul(activated, gathered[18]) + to_float(gathered[19]))
    layer_out = (slot_live * after_mlp).astype(jnp.bfloat16).reshape(tokens.shape)
    weights = (
        lax.all_gather(shards[0], "group", axis=0, tiled=True),
        lax.all_gather(shards[1], "group", axis=0, tiled=True),
        lax.all_gather(shards[2], "group", axis=0, tiled=True),
        lax.all_gather(shards[3], "group", axis=0, tiled=True),
        lax.all_gather(shards[4], "group", axis=0, tiled=True),
        lax.all_gather(shards[5], "group", axis=0, tiled=True),
        lax.all_gather(shards[6], "group", axis=0, tiled=True),
        lax.all_gather(shards[7], "group", axis=0, tiled=True),
        lax.all_gather(shards[8], "group", axis=0, tiled=True),
        lax.all_gather(shards[9], "group", axis=0, tiled=True),
        lax.all_gather(shards[10], "group", axis=0, tiled=True),
        lax.all_gather(shards[11], "group", axis=0, tiled=True),
        lax.all_gather(shards[12], "group", axis=0, tiled=True),
        lax.all_gather(shards[13], "group", axis=0, tiled=True),
        lax.all_gather(shards[14], "group", axis=0, tiled=True),
        lax.all_gather(shards[15], "group", axis=0, tiled=True),
        lax.all_gather(shards[16], "group", axis=0, tiled=True),
        lax.all_gather(shards[17], "group", axis=0, tiled=True),
        lax.all_gather(shards[18], "group", axis=0, tiled=True),
        lax.all_gather(shards[19], "group", axis=0, tiled=True),
    )
    grad_out = slot_live * out_grad.astype(jnp.float32).reshape(row_count, D)
    grad_branch = grad_out.astype(jnp.bfloat16)
    grad_mlp_out = outer_sum(activated, grad_branch)
    grad_mlp_out_bias = column_sums(grad_branch)
    unused_act, gelu_pull = jax.vjp(gelu_exact, pre_act)
    grad_pre = gelu_pull(times_trans(grad_branch, weights[18]))[0].astype(jnp.bfloat16)
    grad_mlp_in = outer_sum(mlp_normed, grad_pre)
    grad_mlp_in_bias = column_sums(grad_pre)
    grad_mlp_normed = times_trans(grad_pre, weights[16])
    grad_space_in, grad_mlp_gain, grad_mlp_shift = norm_back(
        after_space, to_float(weights[14]), to_float(weights[15]), grad_mlp_normed
    )
    grad_after_space = grad_out + grad_space_in
    grad_space_branch = grad_after_space.astype(jnp.bfloat16)
    grad_space_proj = outer_sum(space_rows, grad_space_branch)
    grad_space_proj_bias = column_sums(grad_space_branch)
    grad_space_mixed = (
        times_trans(grad_space_branch, weights[12]).astype(jnp.bfloat16).reshape(frame_shape + (D,))
    )
    grad_space_packed = attend_back(
        space_packed, space_total, grad_space_mixed, space_forms
    ).reshape(row_count, 3 * D)
    grad_space_qkv = outer_sum(space_normed, grad_space_packed)
    grad_space_qv = qv_sums(grad_space_packed)
    grad_space_normed = times_trans(grad_space_packed, weights[10])
    grad_time_in, grad_space_gain, grad_space_shift = norm_back(
        after_time, to_float(weights[8]), to_float(weights[9]), grad_space_normed
    )
    grad_after_time = grad_after_space + grad_time_in
    grad_time_branch = grad_after_time.astype(jnp.bfloat16)
    grad_time_fc = outer_sum(time_projected, grad_time_branch)
    grad_time_fc_bias = column_sums(grad_time_branch)
    grad_projected = times_trans(grad_time_branch, weights[6]).astype(jnp.bfloat16)
    grad_time_proj = outer_sum(time_mixed, grad_projected)
    grad_time_proj_bias = column_sums(grad_projected)
    grad_mixed = (
        times_trans(grad_projected, weights[4]).astype(jnp.bfloat16).reshape(frame_shape + (D,))
    )
    grad_place_mixed = lax.all_to_all(grad_mixed, "group", split_axis=2, concat_axis=1, tiled=True)
    grad_place_packed = attend_back(place_packed, time_total, grad_place_mixed, time_forms)
    grad_time_packed = lax.all_to_all(
        grad_place_packed, "group", split_axis=1, concat_axis=2, tiled=True
    ).reshape(row_count, 3 * D)
    grad_time_qkv = outer_sum(time_normed, grad_time_packed)
    grad_time_qv = qv_sums(grad_time_packed)
    grad_time_normed = times_trans(grad_time_packed, weights[2])
    grad_tokens_in, grad_time_gain, grad_time_shift = norm_back(
        tokens_flat, to_float(weights[0]), to_float(weights[1]), grad_time_normed
    )
    tokens_grad = (grad_after_time + grad_tokens_in).reshape(tokens.shape)
    local_grads = (
        grad_time_gain,
        grad_time_shift,
        grad_time_qkv,
        grad_time_qv,
        grad_time_proj,
        grad_time_proj_bias,
        grad_time_fc,
        grad_time_fc_bias,
        grad_space_gain,
        grad_space_shift,
        grad_space_qkv,
        grad_space_qv,
        grad_space_proj,
        grad_space_proj_bias,
        grad_mlp_gain,
        grad_mlp_shift,
        grad_mlp_in,
        grad_mlp_in_bias,
        grad_mlp_out,
        grad_mlp_out_bias,
    )
    owned = (
        lax.psum_scatter(
            local_grads[0].astype(jnp.bfloat16), "group", scatter_dimension=0, tiled=True
        ).astype(jnp.float32),
        lax.psum_scatter(
            local_grads[1].astype(jnp.bfloat16), "group", scatter_dimension=0, tiled=True
        ).astype(jnp.float32),
        lax.psum_scatter(
            local_grads[2].astype(jnp.bfloat16), "group", scatter_dimension=0, tiled=True
        ).astype(jnp.float32),
        lax.psum_scatter(
            local_grads[3].astype(jnp.bfloat16), "group", scatter_dimension=0, tiled=True
        ).astype(jnp.float32),
        lax.psum_scatter(
            local_grads[4].astype(jnp.bfloat16), "group", scatter_dimension=0, tiled=True
        ).astype(jnp.float32),
        lax.psum_scatter(
            local_grads[5].astype(jnp.bfloat16), "group", scatter_dimension=0, tiled=True
        ).astype(jnp.float32),
        lax.psum_scatter(
            local_grads[6].astype(jnp.bfloat16), "group", scatter_dimension=0, tiled=True
        ).astype(jnp.float32),
        lax.psum_scatter(
            local_grads[7].astype(jnp.bfloat16), "group", scatter_dimension=0, tiled=True
        ).astype(jnp.float32),
        lax.psum_scatter(
            local_grads[8].astype(jnp.bfloat16), "group", scatter_dimension=0, tiled=True
        ).astype(jnp.float32),
        lax.psum_scatter(
            local_grads[9].astype(jnp.bfloat16), "group", scatter_dimension=0, tiled=True
        ).astype(jnp.float32),
        lax.psum_scatter(
            local_grads[10].astype(jnp.bfloat16), "group", scatter_dimension=0, tiled=True
        ).astype(jnp.float32),
        lax.psum_scatter(
            local_grads[11].astype(jnp.bfloat16), "group", scatter_dimension=0, tiled=True
        ).astype(jnp.float32),
        lax.psum_scatter(
            local_grads[12].astype(jnp.bfloat16), "group", scatter_dimension=0, tiled=True
        ).astype(jnp.float32),
        lax.psum_scatter(
            local_grads[13].astype(jnp.bfloat16), "group", scatter_dimension=0, tiled=True
        ).astype(jnp.float32),
        lax.psum_scatter(
            local_grads[14].astype(jnp.bfloat16), "group", scatter_dimension=0, tiled=True
        ).astype(jnp.float32),
        lax.psum_scatter(
            local_grads[15].astype(jnp.bfloat16), "group", scatter_dimension=0, tiled=True
        ).astype(jnp.float32),
        lax.psum_scatter(
            local_grads[16].astype(jnp.bfloat16), "group", scatter_dimension=0, tiled=True
        ).astype(jnp.float32),
        lax.psum_scatter(
            local_grads[17].astype(jnp.bfloat16), "group", scatter_dimension=0, tiled=True
        ).astype(jnp.float32),
        lax.psum_scatter(
            local_grads[18].astype(jnp.bfloat16), "group", scatter_dimension=0, tiled=True
        ).astype(jnp.float32),
        lax.psum_scatter(
            local_grads[19].astype(jnp.bfloat16), "group", scatter_dimension=0, tiled=True
        ).astype(jnp.float32),
    )
    summed = lax.psum(
        (
            owned[0],
            owned[1],
            owned[2],
            owned[3],
            owned[4],
            owned[5],
            owned[6],
            owned[7],
            owned[8],
            owned[9],
            owned[10],
            owned[11],
            owned[12],
            owned[13],
            owned[14],
            owned[15],
            owned[16],
            owned[17],
            owned[18],
            owned[19],
        ),
        "replica",
    )
    return (layer_out, tokens_grad) + tuple(summed)


def solution(mesh):
    placed = (
        P("replica", "group", None, None),
        P("replica", "group", None, None),
        P("replica"),
        P("group"),
        P("group"),
        P("group", None),
        P("group"),
        P("group", None),
        P("group"),
        P("group", None),
        P("group"),
        P("group"),
        P("group"),
        P("group", None),
        P("group"),
        P("group", None),
        P("group"),
        P("group"),
        P("group"),
        P("group", None),
        P("group"),
        P("group", None),
        P("group"),
    )
    return jax.shard_map(
        on_device,
        mesh=mesh,
        in_specs=placed,
        out_specs=(
            P("replica", "group", None, None),
            P("replica", "group", None, None),
            P("group"),
            P("group"),
            P("group", None),
            P("group"),
            P("group", None),
            P("group"),
            P("group", None),
            P("group"),
            P("group"),
            P("group"),
            P("group", None),
            P("group"),
            P("group", None),
            P("group"),
            P("group"),
            P("group"),
            P("group", None),
            P("group"),
            P("group", None),
            P("group"),
        ),
        check_vma=False,
    )
```

profile of v0, /device:TPU:0, one launch (start us, length us, event | category | flops | bytes accessed | tf_op | source)
XLA Modules:
  0.0 957.7 jit_solution(8965359546983486648)
XLA Ops:
  14.7 14.1 %all-reduce.25 = (bf16[768]{0:T(1024)(128)(2,1)S(1)}, bf16[768]{0:T(1024)(128)(2,1)S(1)}, bf16[768]{0:T(1024)(128)(2,1)}, bf16[768]{0:T(1024)(128)(2,1)}, bf16[7...) all-reduce(bf16[768]{0:T(1024)(128)(2,1)S(1)} %dynamic-update-slice, ...), channel_id=1, replica_groups=mesh['group'=4,'replica'=8] {'group'}, use_global_device_ids=true, to_apply=%add.1 | all-reduce | flops 6912 | bytes 27648
  32.0 5.1 all-gather
  37.3 5.2 all-gather.1
  43.6 4.9 fusion.6
  54.6 31.9 %all_to_all.63 = bf16[1,2,196,2304]{3,1,0,2:T(2,128)(2,1)S(1)} all-to-all(bf16[1,2,196,2304]{3,1,0,2:T(2,128)(2,1)S(1)} %copy.148), channel_id=1, replica_groups=mesh['group'=4,'replica'=8] {'group'}, dimensions={2} | all-to-all | bytes 3612672 | tf_op jit(solution)/shard_map/all_to_all | solution.py:200
  118.3 9.0 all-gather.2
  144.4 5.3 fusion.7
  179.0 16.3 %multiply_convert_fusion.1 = (bf16[392,3072]{1,0:T(8,128)(2,1)}, f32[392,3072]{1,0:T(8,128)}, f32[392,3072]{1,0:T(8,128)}) fusion(f32[3072]{0:T(1024)} %bitcast.145, bf16[768,3072]{1,0:T(8,128)(2,1)} %all-gather.21.cloned.1.call-done, f32[392,768]{1,0:T(8,128)} %copy-done.5, f32[768]{0:T(1024)} %convert_element_type.318, f32[768]{0:T(1024)} %convert_element_type.317, ...), kind=kOutput, calls=%fused_computation.11 | convolution fusion | flops 1930672128 | bytes 17986624 | tf_op jit(solution)/shard_map/dot_general | solution.py:18
  195.4 22.7 %all-gather.23.cloned.1.call-done = bf16[3072,768]{1,0:T(8,128)(2,1)} async-done(((bf16[768,768]{1,0:T(8,128)(2,1)}), bf16[3072,768]{1,0:T(8,128)(2,1)}) %all-gather.23.cloned.1.call-update) | async-done | bytes 4718608 | tf_op jit(solution)/shard_map/all_gather | solution.py:191
  218.1 9.5 fusion.72
  273.6 5.8 multiply_reduce_fusion.5
  292.7 6.2 convolution_convert_fusion.2
  305.4 12.3 %all_to_all.64 = bf16[1,2,196,768]{3,1,0,2:T(2,128)(2,1)S(1)} all-to-all(bf16[1,2,196,768]{3,1,0,2:T(2,128)(2,1)S(1)} %copy.172), channel_id=1, replica_groups=mesh['group'=4,'replica'=8] {'group'}, dimensions={2} | all-to-all | bytes 1204224 | tf_op jit(solution)/shard_map/all_to_all | solution.py:284
  353.3 29.8 %all-to-all-done.3 = bf16[1,8,49,2304]{3,2,0,1:T(8,128)(2,1)S(1)} async-done(((bf16[1,8,49,2304]{3,2,0,1:T(8,128)(2,1)}), bf16[1,8,49,2304]{3,2,0,1:T(8,128)(2,1)S(1)}, u32[]{:S(2)}, u32[]{:S(2)}) %all-to-all-start.3) | async-done | bytes 1806368 | tf_op jit(solution)/shard_map/all_to_all | solution.py:286
  388.1 5.4 convolution_convert_fusion.3
  395.2 6.2 convolution_convert_fusion.1
  401.5 7.0 convolution_convert_fusion
  415.1 4.9 multiply_reduce_fusion.6
  428.4 10.9 %all-reduce.24 = (bf16[768]{0:T(1024)(128)(2,1)S(1)}, bf16[768]{0:T(1024)(128)(2,1)S(1)}, bf16[768]{0:T(1024)(128)(2,1)S(1)}, bf16[1536]{0:T(1024)(128)(2,1)S(1)...) all-reduce(bf16[768]{0:T(1024)(128)(2,1)S(1)} %dynamic-update-slice, ...), channel_id=1, replica_groups=mesh['group'=4,'replica'=8] {'group'}, use_global_device_ids=true, to_apply=%add.9 | all-reduce | flops 14592 | bytes 58368
  439.4 5.1 fusion.18
  446.5 12.9 %reduce-scatter.8.cloned.1.call-done = bf16[192,2304]{1,0:T(8,128)(2,1)} async-done(((bf16[768,2304]{1,0:T(8,128)(2,1)}), bf16[192,2304]{1,0:T(8,128)(2,1)}) %reduce-scatter.8.cloned.1.call-update) | async-done | bytes 884752 | tf_op jit(solution)/shard_map/reduce_scatter | solution.py:325
  459.4 50.6 %reduce-scatter.18.cloned.1.call-done = bf16[192,3072]{1,0:T(8,128)(2,1)} async-done(((bf16[768,3072]{1,0:T(8,128)(2,1)}), bf16[192,3072]{1,0:T(8,128)(2,1)}) %reduce-scatter.18.cloned.1.call-update) | async-done | bytes 1179664 | tf_op jit(solution)/shard_map/reduce_scatter | solution.py:367
  510.0 50.3 %reduce-scatter.20.cloned.1.call-done = bf16[768,768]{1,0:T(8,128)(2,1)} async-done(((bf16[3072,768]{1,0:T(8,128)(2,1)}), bf16[768,768]{1,0:T(8,128)(2,1)}) %reduce-scatter.20.cloned.1.call-update) | async-done | bytes 1179664 | tf_op jit(solution)/shard_map/reduce_scatter | solution.py:373
  560.2 390.8 %all-reduce.27 = (f32[192]{0:T(256)}, f32[192]{0:T(256)}, f32[192,2304]{1,0:T(8,128)}, f32[384]{0:T(512)}, f32[192,768]{1,0:T(8,128)}, /*index=5*/f32[192]{0:T(2...) all-reduce(f32[192]{0:T(256)S(1)} %get-tuple-element.225, ...), channel_id=1, replica_groups=mesh['group'=4,'replica'=8] {'replica'}, use_global_device_ids=true, to_apply=%region_20.0 | all-reduce | flops 2510208 | bytes 15068160 | tf_op jit(solution)/shard_map/psum | solution.py:380
  (397 shorter events, 216.9 us)
Async XLA Ops:
  7.3 21.4 %copy-start.17 = (bf16[1,2,196,768]{3,1,2,0:T(2,128)(2,1)S(1)}, bf16[1,2,196,768]{3,1,2,0:T(2,128)(2,1)}, u32[]{:S(2)}) copy-start(bf16[1,2,196,768]{3,1,2,0:T(2,128)(2,1)} %param.23) | copy-start | bytes 1806340
  7.3 36.3 %all-gather.11.cloned.1.call-start = ((), (), s32[]{:S(2)}) async-start(), calls=%async_computation.11 | async-start | bytes 4423680 | tf_op jit(solution)/shard_map/all_gather | solution.py:175
  8.0 129.4 %all-gather.13.cloned.1.call-start = ((), (), s32[]{:S(2)}) async-start(), calls=%async_computation.12 | async-start | bytes 1474560 | tf_op jit(solution)/shard_map/all_gather | solution.py:177
  8.8 131.6 %all-gather.15.cloned.1.call-start = ((), (), s32[]{:S(2)}) async-start(), calls=%async_computation.13 | async-start | bytes 1474560 | tf_op jit(solution)/shard_map/all_gather | solution.py:179
  9.5 134.8 %all-gather.17.cloned.1.call-start = ((), (), s32[]{:S(2)}) async-start(), calls=%async_computation.14 | async-start | bytes 4423680 | tf_op jit(solution)/shard_map/all_gather | solution.py:183
  10.1 163.0 %all-gather.19.cloned.1.call-start = ((), (), s32[]{:S(2)}) async-start(), calls=%async_computation.15 | async-start | bytes 1474560 | tf_op jit(solution)/shard_map/all_gather | solution.py:185
  10.7 168.3 %all-gather.21.cloned.1.call-start = ((), (), s32[]{:S(2)}) async-start(), calls=%async_computation.16 | async-start | bytes 5898240 | tf_op jit(solution)/shard_map/all_gather | solution.py:189
  28.7 14.9 %copy-start.44 = (f32[768]{0:T(1024)}, f32[768]{0:T(1024)S(1)}, u32[]{:S(2)}) copy-start(f32[768]{0:T(1024)S(1)} %convert_element_type.294) | copy-start | bytes 9220
  31.5 17.1 %copy-start.51 = (f32[392]{0:T(512)}, f32[392]{0:T(512)S(1)}, u32[]{:S(2)}) copy-start(f32[392]{0:T(512)S(1)} %rsqrt.36) | copy-start | bytes 4708
  111.2 22.1 %all-to-all-start.1 = ((bf16[1,8,49,768]{3,2,0,1:T(8,128)(2,1)}), bf16[1,8,49,768]{3,2,0,1:T(8,128)(2,1)}, u32[]{:S(2)}, u32[]{:S(2)}) async-start(bf16[1,8,49,768]{3,2,0,1:T(8,128)(2,1)} %reshape.584), calls=%async_computation.1 | async-start | bytes 1376256 | tf_op jit(solution)/shard_map/all_to_all | solution.py:202
  115.5 102.6 %all-gather.23.cloned.1.call-start = ((), (), s32[]{:S(2)}) async-start(), calls=%async_computation.17 | async-start | bytes 5898240 | tf_op jit(solution)/shard_map/all_gather | solution.py:191
  116.3 330.2 %reduce-scatter.12.cloned.1.call-start = ((), (), s32[]{:S(2)}) async-start(), calls=%async_computation.20 | async-start | bytes 1474560 | tf_op jit(solution)/shard_map/reduce_scatter | solution.py:337
  116.4 28.0 %copy-start.48 = (f32[768]{0:T(1024)}, f32[768]{0:T(1024)S(1)}, u32[]{:S(2)}) copy-start(f32[768]{0:T(1024)S(1)} %convert_element_type.306) | copy-start | bytes 9220
  116.4 28.0 %copy-start.63 = (f32[768]{0:T(1024)}, f32[768]{0:T(1024)S(1)}, u32[]{:S(2)}) copy-start(f32[768]{0:T(1024)S(1)} %convert_element_type.307) | copy-start | bytes 9220
  175.8 54.7 %copy-start.34 = (f32[392]{0:T(512)}, f32[392]{0:T(512)S(1)}, u32[]{:S(2)}) copy-start(f32[392]{0:T(512)S(1)} %broadcast_multiply_fusion.1) | copy-start | bytes 4708
  218.1 9.5 copy-start.55
  218.1 9.5 copy-start.78
  284.3 162.2 %reduce-scatter.10.cloned.1.call-start = ((), (), s32[]{:S(2)}) async-start(), calls=%async_computation.19 | async-start | bytes 1474560 | tf_op jit(solution)/shard_map/reduce_scatter | solution.py:331
  289.4 157.0 %reduce-scatter.16.cloned.1.call-start = ((), (), s32[]{:S(2)}) async-start(), calls=%async_computation.22 | async-start | bytes 1474560 | tf_op jit(solution)/shard_map/reduce_scatter | solution.py:355
  292.6 153.9 %reduce-scatter.14.cloned.1.call-start = ((), (), s32[]{:S(2)}) async-start(), calls=%async_computation.21 | async-start | bytes 4423680 | tf_op jit(solution)/shard_map/reduce_scatter | solution.py:349
  347.7 35.4 %all-to-all-start.3 = ((bf16[1,8,49,2304]{3,2,0,1:T(8,128)(2,1)}), bf16[1,8,49,2304]{3,2,0,1:T(8,128)(2,1)S(1)}, u32[]{:S(2)}, u32[]{:S(2)}) async-start(bf16[1,8,49,2304]{3,2,0,1:T(8,128)(2,1)} %copy.183), calls=%async_computation.3 | async-start | bytes 4128768 | tf_op jit(solution)/shard_map/all_to_all | solution.py:286
  351.4 108.0 %reduce-scatter.8.cloned.1.call-start = ((), (), s32[]{:S(2)}) async-start(), calls=%async_computation.18 | async-start | bytes 4423680 | tf_op jit(solution)/shard_map/reduce_scatter | solution.py:325
  393.6 116.4 %reduce-scatter.18.cloned.1.call-start = ((), (), s32[]{:S(2)}) async-start(), calls=%async_computation.23 | async-start | bytes 5898240 | tf_op jit(solution)/shard_map/reduce_scatter | solution.py:367
  401.4 158.8 %reduce-scatter.20.cloned.1.call-start = ((), (), s32[]{:S(2)}) async-start(), calls=%async_computation.24 | async-start | bytes 5898240 | tf_op jit(solution)/shard_map/reduce_scatter | solution.py:373
  (84 other events, 303.6 us)
Sparse Core Ops, SparseCore 0:
  9.7 33.8 all-gather.10
  45.2 17.8 all-gather.12
  64.6 23.6 all-gather.14
  89.8 31.0 all-gather.16
  122.2 17.8 all-gather.18
  141.5 37.4 all-gather.20
  180.6 37.4 all-gather.22
  284.4 25.7 reduce-scatter.11
  312.9 25.7 reduce-scatter.9
  341.1 32.1 reduce-scatter.15
  376.0 40.3 reduce-scatter.13
  418.8 40.5 reduce-scatter.7
  462.1 47.8 reduce-scatter.17
  512.4 47.8 reduce-scatter.19
where the time goes:
time: 967 us; the launch traced here: 958 us
  blocking collectives  479 us (50%)
  waiting for transfers between devices  172 us (18%)
  matrix products  129 us (13%)
  local copies, waits for them, and re-layouts  128 us (13%)
  other arithmetic  22.9 us (2%)
  between operations  18.6 us (2%)
    psum x1, blocking collectives, on_device(): lax.psum((owned[0], owned[1], owned[2], owned[3], owned[4], owned[5], own...  391 us
    reduce_scatter x1, waiting for transfers between devices, on_device(): lax.psum_scatter(local_grads[16].astype(jnp.bfloat16), 'group', scatter_d...  50.6 us
    reduce_scatter x1, waiting for transfers between devices, on_device(): lax.psum_scatter(local_grads[18].astype(jnp.bfloat16), 'group', scatter_d...  50.3 us
    dot_general x7, matrix products, matmul(): return jnp.dot(left, right, preferred_element_type=jnp.float32)  39.8 us
    all_to_all x1, blocking collectives, on_device(): lax.all_to_all(time_packed, 'group', split_axis=2, concat_axis=1, tiled=T...  31.9 us
    dot_general x7, matrix products, outer_sum(): lax.dot_general(left, right, (((0,), (0,)), ((), ())), preferred_element_...  31.6 us
    dot_general x7, matrix products, times_trans(): lax.dot_general(left, right, (((1,), (1,)), ((), ())), preferred_element_...  30 us
    all_to_all x1, waiting for transfers between devices, on_device(): lax.all_to_all(grad_place_packed, 'group', split_axis=1, concat_axis=2, t...  29.8 us
  transfers between devices with their start and end apart: 16, of which 7 were waited for; matrix products, arithmetic and copies ran while one was open for 21% of the time, Pallas kernels for 0%

commit v1 on v0

v1 whole, which is shorter than its diff:
```python
import jax
import jax.numpy as jnp
from jax import lax
from jax.sharding import PartitionSpec as P

D = 768
HEADS = 12
HEAD_DIM = 64
PLACES = 196
BLOCK = 192
CHUNK = 104
PLACE_ROWS = 392
FRAME_PAD = 208
FRAME_ROWS = 416
epsilon = 1e-06
bf16 = jnp.bfloat16
f32 = jnp.float32


def matmul(left, right):
    return jnp.dot(left, right, preferred_element_type=f32)


def times_trans(left, right):
    return lax.dot_general(left, right, (((1,), (1,)), ((), ())), preferred_element_type=f32)


def outer_sum(left, right):
    return lax.dot_general(left, right, (((0,), (0,)), ((), ())), preferred_element_type=f32)


def column_sums(values):
    return jnp.sum(values.astype(f32), axis=0)


def norm_parts(values):
    centred = values - jnp.mean(values, axis=-1, keepdims=True)
    inverse = lax.rsqrt(jnp.mean(centred * centred, axis=-1, keepdims=True) + epsilon)
    return centred * inverse, inverse


def norm_back(values, gain, grad_normed):
    normal, inverse = norm_parts(values)
    scaled = grad_normed * gain
    grad = inverse * (
        scaled
        - jnp.mean(scaled, axis=-1, keepdims=True)
        - normal * jnp.mean(scaled * normal, axis=-1, keepdims=True)
    )
    return grad, jnp.sum(grad_normed * normal, axis=0), jnp.sum(grad_normed, axis=0)


def flip(array, axis, bit, size):
    return lax.ppermute(array, axis, [(at, at ^ bit) for at in range(size)])


def pick(array, at):
    return lax.dynamic_index_in_dim(array, at, 0, keepdims=False)


def add_rounded(left, right):
    return (left.astype(f32) + right.astype(f32)).astype(bf16)


def gather_shard(own, place):
    group_at, ring_bit, ring_size = place
    rows = own.shape[0]
    partner = flip(own, "group", 1, 4)
    if ring_size > 1:
        half = rows // 2
        sent = lax.dynamic_slice_in_dim(own, ring_bit * half, half, 0)
        direct = flip(sent, "group", 2, 4)
        relayed = flip(direct, "replica", 1, ring_size)
        remote = jnp.where(
            ring_bit == 0,
            jnp.concatenate([direct, relayed], 0),
            jnp.concatenate([relayed, direct], 0),
        )
    else:
        remote = flip(own, "group", 2, 4)
    across = flip(remote, "group", 1, 4)
    held = jnp.stack([own, partner, remote, across])
    return jnp.stack([pick(held, group_at ^ shard) for shard in range(4)])


def reduce_chunk(packed, place, replica_at, ring_size):
    group_at = place[0]
    chip_at = group_at // 2
    core_at = group_at % 2
    rows = packed.shape[1]
    halves = packed.reshape(2, 2, rows, D).transpose(1, 0, 2, 3)
    current = add_rounded(pick(halves, core_at), flip(pick(halves, 1 - core_at), "group", 1, 4))
    current = add_rounded(
        pick(current, chip_at), flip(pick(current, 1 - chip_at), "group", 2, 4)
    )
    bits = [1 << at for at in range(ring_size.bit_length() - 1)]
    for bit in bits:
        mine = (replica_at // bit) % 2
        split = current.reshape(2, current.shape[0] // 2, D)
        current = add_rounded(
            pick(split, mine), flip(pick(split, 1 - mine), "replica", bit, ring_size)
        )
    for bit in reversed(bits):
        mine = (replica_at // bit) % 2
        other = flip(current, "replica", bit, ring_size)
        current = jnp.where(
            mine == 0,
            jnp.concatenate([current, other], 0),
            jnp.concatenate([other, current], 0),
        )
    return current.astype(f32)


def pack_weight(shard):
    rows, width = shard.shape
    return shard.reshape(rows, width // D, D).transpose(1, 0, 2).reshape(-1, D)


def unpack_weight(full, start, blocks):
    part = full[:, start * BLOCK : (start + blocks) * BLOCK]
    return part.reshape(4, blocks, BLOCK, D).transpose(0, 2, 1, 3).reshape(4 * BLOCK, blocks * D)


def pack_grad(grad):
    rounded = grad.astype(bf16)
    blocks = grad.shape[1] // D
    return (
        rounded.reshape(4, BLOCK, blocks, D).transpose(0, 2, 1, 3).reshape(4, blocks * BLOCK, D)
    )


def unpack_grad(summed, start, blocks):
    part = summed[start * BLOCK : (start + blocks) * BLOCK]
    return part.reshape(blocks, BLOCK, D).transpose(1, 0, 2).reshape(BLOCK, blocks * D)


def bias_row(qv_bias):
    qv_float = qv_bias.astype(f32)
    return jnp.concatenate([qv_float[:D], jnp.zeros((D,), f32), qv_float[D:]])


def split_heads(packed, member):
    leading = packed.shape[:-1]
    return packed[..., member * D : (member + 1) * D].reshape(leading + (HEADS, HEAD_DIM))


def attend(packed, live_keys):
    query, key_part, value_part = (split_heads(packed, member) for member in range(3))
    scores = jnp.einsum("bqhd,bkhd->bhqk", query, key_part, preferred_element_type=f32)
    scores = scores * HEAD_DIM ** (-0.5)
    if live_keys is not None:
        scores = jnp.where(live_keys, scores, -1e30)
    maximum = jnp.max(scores, axis=-1, keepdims=True)
    weights = jnp.exp(scores - maximum)
    probs = weights / jnp.sum(weights, axis=-1, keepdims=True)
    mixed = jnp.einsum(
        "bhqk,bkhd->bqhd", probs.astype(bf16), value_part, preferred_element_type=f32
    )
    return mixed.reshape(packed.shape[:-1] + (D,)).astype(bf16), probs


def attend_back(packed, probs, grad_mixed):
    query, key_part, value_part = (split_heads(packed, member) for member in range(3))
    score_scale = HEAD_DIM ** (-0.5)
    grad_heads = grad_mixed.reshape(grad_mixed.shape[:-1] + (HEADS, HEAD_DIM))
    grad_value = jnp.einsum(
        "bhqk,bqhd->bkhd", probs.astype(bf16), grad_heads, preferred_element_type=f32
    )
    grad_probs = jnp.einsum("bqhd,bkhd->bhqk", grad_heads, value_part, preferred_element_type=f32)
    centre = jnp.sum(grad_probs * probs, axis=-1, keepdims=True)
    grad_scores = (probs * (grad_probs - centre)).astype(bf16)
    grad_query = (
        jnp.einsum("bhqk,bkhd->bqhd", grad_scores, key_part, preferred_element_type=f32)
        * score_scale
    )
    grad_key = (
        jnp.einsum("bhqk,bqhd->bkhd", grad_scores, query, preferred_element_type=f32) * score_scale
    )
    flat = packed.shape[:-1] + (D,)
    return jnp.concatenate(
        [grad_query.reshape(flat), grad_key.reshape(flat), grad_value.reshape(flat)], axis=-1
    ).astype(bf16)


def place_to_send():
    row = lax.broadcasted_iota(jnp.int32, (FRAME_ROWS, PLACE_ROWS), 0)
    col = lax.broadcasted_iota(jnp.int32, (FRAME_ROWS, PLACE_ROWS), 1)
    dest = row // CHUNK
    local = row % CHUNK
    source = (local // 2) * 8 + dest * 2 + local % 2
    return ((col == source) & (local < 98)).astype(bf16)


def recv_to_frame(group_at):
    row = lax.broadcasted_iota(jnp.int32, (FRAME_ROWS, FRAME_ROWS), 0)
    col = lax.broadcasted_iota(jnp.int32, (FRAME_ROWS, FRAME_ROWS), 1)
    frame = row // FRAME_PAD
    spot = row % FRAME_PAD
    source = ((spot // 49) ^ group_at) * CHUNK + (spot % 49) * 2 + frame
    return ((col == source) & (spot < PLACES)).astype(bf16)


def exchange(chunks):
    return [chunks[0]] + [flip(chunks[d], "group", d, 4) for d in range(1, 4)]


def permuted(matrix, rows):
    return matmul(matrix, rows).astype(bf16)


def permuted_back(matrix, rows):
    return outer_sum(matrix, rows).astype(bf16)


def chunks_of(rows):
    return [rows[d * CHUNK : (d + 1) * CHUNK] for d in range(4)]


def build(mesh):
    ring_size = mesh.shape["replica"]

    def on_device(tokens, out_grad, slot_mask, *shards):
        (
            time_norm_gain, time_norm_shift, time_qkv, time_qv_bias, time_proj, time_proj_bias,
            time_fc, time_fc_bias, space_norm_gain, space_norm_shift, space_qkv, space_qv_bias,
            space_proj, space_proj_bias, mlp_norm_gain, mlp_norm_shift, mlp_in, mlp_in_bias,
            mlp_out, mlp_out_bias,
        ) = shards
        group_at = lax.axis_index("group")
        replica_at = lax.axis_index("replica")
        place = (group_at, replica_at % 2, ring_size)
        vectors = [
            time_norm_gain, time_norm_shift, time_qv_bias, time_proj_bias, time_fc_bias,
            space_norm_gain, space_norm_shift, space_qv_bias, space_proj_bias, mlp_norm_gain,
            mlp_norm_shift, mlp_in_bias, mlp_out_bias,
        ]
        widths = [v.shape[0] for v in vectors]
        flat = jnp.concatenate(vectors)
        extra = jnp.pad(flat, (0, 16 * D - flat.shape[0])).reshape(16, D)

        token_pieces = tokens[0].transpose(1, 0, 2).reshape(4, 49, 2, D)
        got = exchange([pick(token_pieces, group_at ^ d) for d in range(4)])
        place_tokens = jnp.concatenate(got, axis=1).reshape(PLACE_ROWS, D)

        full_a = gather_shard(
            jnp.concatenate([pack_weight(time_qkv), time_proj, time_fc, extra], 0), place
        )
        full_b = gather_shard(jnp.concatenate([pack_weight(space_qkv), space_proj], 0), place)
        full_c = gather_shard(jnp.concatenate([pack_weight(mlp_in), mlp_out], 0), place)
        w_time_qkv = unpack_weight(full_a, 0, 3)
        w_time_proj = unpack_weight(full_a, 3, 1)
        w_time_fc = unpack_weight(full_a, 4, 1)
        w_space_qkv = unpack_weight(full_b, 0, 3)
        w_space_proj = unpack_weight(full_b, 3, 1)
        w_mlp_in = unpack_weight(full_c, 0, 4)
        w_mlp_out = full_c[:, 4 * BLOCK :].reshape(4 * D, D)
        flat_full = full_a[:, 5 * BLOCK :].reshape(4, 16 * D)
        vecs = []
        start = 0
        for width in widths:
            vecs.append(flat_full[:, start : start + width].reshape(-1).astype(f32))
            start += width
        (
            g_time_norm, s_time_norm, b_time_qv, b_time_proj, b_time_fc, g_space_norm,
            s_space_norm, b_space_qv, b_space_proj, g_mlp_norm, s_mlp_norm, b_mlp_in, b_mlp_out,
        ) = vecs

        live = slot_mask.astype(f32)[0]
        pads = ((0, 0), (0, FRAME_PAD - PLACES), (0, 0))
        frame_tokens = jnp.pad(tokens[0], pads).reshape(FRAME_ROWS, D)
        frame_grad = jnp.pad(out_grad[0], pads).reshape(FRAME_ROWS, D)
        to_send = place_to_send()
        to_frame = recv_to_frame(group_at)
        live_keys = (lax.broadcasted_iota(jnp.int32, (1, 1, 1, FRAME_PAD), 3) < PLACES)

        place_x = place_tokens.astype(f32)
        normal1, unused = norm_parts(place_x)
        h1 = (normal1 * g_time_norm + s_time_norm).astype(bf16)
        qkv1 = (matmul(h1, w_time_qkv) + bias_row(b_time_qv)).astype(bf16)
        a1, probs1 = attend(qkv1.reshape(49, 8, 3 * D), None)
        a1 = a1.reshape(PLACE_ROWS, D)
        o1 = (matmul(a1, w_time_proj) + b_time_proj).astype(bf16)
        frame_o1 = permuted(
            to_frame, jnp.concatenate(exchange(chunks_of(permuted(to_send, o1))), 0)
        )
        x1 = frame_tokens.astype(f32) + (matmul(frame_o1, w_time_fc) + b_time_fc)
        normal2, unused = norm_parts(x1)
        h2 = (normal2 * g_space_norm + s_space_norm).astype(bf16)
        qkv2 = (matmul(h2, w_space_qkv) + bias_row(b_space_qv)).astype(bf16)
        a2, probs2 = attend(qkv2.reshape(2, FRAME_PAD, 3 * D), live_keys)
        a2 = a2.reshape(FRAME_ROWS, D)
        x2 = x1 + (matmul(a2, w_space_proj) + b_space_proj)
        normal3, unused = norm_parts(x2)
        h3 = (normal3 * g_mlp_norm + s_mlp_norm).astype(bf16)
        pre_act = matmul(h3, w_mlp_in) + b_mlp_in
        cdf = 0.5 * (1.0 + lax.erf(pre_act * (0.5**0.5)))
        act = (pre_act * cdf).astype(bf16)
        x3 = x2 + (matmul(act, w_mlp_out) + b_mlp_out)
        layer_out = (live * x3).astype(bf16).reshape(2, FRAME_PAD, D)[None, :, :PLACES]
        e3 = live * frame_grad.astype(f32)
        dm = e3.astype(bf16)
        d_mlp_out = outer_sum(act, dm)
        slope = cdf + pre_act * jnp.exp(-0.5 * pre_act * pre_act) * 0.3989422804014327
        du = (slope * times_trans(dm, w_mlp_out)).astype(bf16)
        d_mlp_in = outer_sum(h3, du)
        grad_c = jnp.concatenate(
            [pack_grad(d_mlp_in), d_mlp_out.astype(bf16).reshape(4, D, D)], 1
        )
        sum_c = reduce_chunk(grad_c, place, replica_at, ring_size)
        d_v3, dg3, ds3 = norm_back(x2, g_mlp_norm, times_trans(du, w_mlp_in))
        e2 = e3 + d_v3
        dt2 = e2.astype(bf16)
        d_space_proj = outer_sum(a2, dt2)
        da2 = times_trans(dt2, w_space_proj).astype(bf16)
        dqkv2 = attend_back(
            qkv2.reshape(2, FRAME_PAD, 3 * D), probs2, da2.reshape(2, FRAME_PAD, D)
        ).reshape(FRAME_ROWS, 3 * D)
        d_space_qkv = outer_sum(h2, dqkv2)
        sum_b = reduce_chunk(
            jnp.concatenate([pack_grad(d_space_qkv), pack_grad(d_space_proj)], 1),
            place, replica_at, ring_size,
        )
        d_v2, dg2, ds2 = norm_back(x1, g_space_norm, times_trans(dqkv2, w_space_qkv))
        e1 = e2 + d_v2
        dt1 = e1.astype(bf16)
        dt1_place = permuted_back(
            to_send, jnp.concatenate(exchange(chunks_of(permuted_back(to_frame, dt1))), 0)
        )
        d_time_fc = outer_sum(o1, dt1_place)
        do1 = times_trans(dt1_place, w_time_fc).astype(bf16)
        d_time_proj = outer_sum(a1, do1)
        da1 = times_trans(do1, w_time_proj).astype(bf16)
        dqkv1 = attend_back(
            qkv1.reshape(49, 8, 3 * D), probs1, da1.reshape(49, 8, D)
        ).reshape(PLACE_ROWS, 3 * D)
        d_time_qkv = outer_sum(h1, dqkv1)
        d_v1, dg1, ds1 = norm_back(place_x, g_time_norm, times_trans(dqkv1, w_time_qkv))
        sums1 = column_sums(dqkv1)
        sums2 = column_sums(dqkv2)
        grads = [
            dg1, ds1, jnp.concatenate([sums1[:D], sums1[2 * D :]]), column_sums(do1),
            column_sums(dt1_place), dg2, ds2, jnp.concatenate([sums2[:D], sums2[2 * D :]]),
            column_sums(dt2), dg3, ds3, column_sums(du), column_sums(dm),
        ]
        flat_grads = jnp.concatenate([v.astype(bf16).reshape(4, -1) for v in grads], 1)
        extra_rows = max(16, ring_size)
        extra_grads = jnp.pad(
            flat_grads, ((0, 0), (0, extra_rows * D - flat_grads.shape[1]))
        ).reshape(4, extra_rows, D)
        sum_a = reduce_chunk(
            jnp.concatenate(
                [pack_grad(d_time_qkv), pack_grad(d_time_proj), pack_grad(d_time_fc), extra_grads],
                1,
            ),
            place, replica_at, ring_size,
        )
        back = permuted(
            to_frame,
            jnp.concatenate(exchange(chunks_of(permuted(to_send, d_v1.astype(bf16)))), 0),
        )
        tokens_grad = (e1 + back.astype(f32)).reshape(2, FRAME_PAD, D)[None, :, :PLACES]
        flat_sums = sum_a[5 * BLOCK :].reshape(-1)
        outs = []
        start = 0
        for width in widths:
            outs.append(flat_sums[start : start + width])
            start += width
        (
            o_dg1, o_ds1, o_qv1, o_pb, o_fb, o_dg2, o_ds2, o_qv2, o_sb, o_dg3, o_ds3, o_ib, o_ob,
        ) = outs
        return (
            layer_out, tokens_grad, o_dg1, o_ds1, unpack_grad(sum_a, 0, 3), o_qv1,
            unpack_grad(sum_a, 3, 1), o_pb, unpack_grad(sum_a, 4, 1), o_fb, o_dg2, o_ds2,
            unpack_grad(sum_b, 0, 3), o_qv2, unpack_grad(sum_b, 3, 1), o_sb, o_dg3, o_ds3,
            unpack_grad(sum_c, 0, 4), o_ib, sum_c[4 * BLOCK :], o_ob,
        )

    return on_device


def solution(mesh):
    rows = P("group", None)
    vector = P("group")
    batch = P("replica", "group", None, None)
    params = (
        vector, vector, rows, vector, rows, vector, rows, vector, vector, vector, rows, vector,
        rows, vector, vector, vector, rows, vector, rows, vector,
    )
    return jax.shard_map(
        build(mesh),
        mesh=mesh,
        in_specs=(batch, batch, P("replica")) + params,
        out_specs=(batch, batch) + params,
        check_vma=False,
    )
```

time: 967 us -> 748 us (0.77)
  blocking collectives: 479 us -> 0 us
  waiting for transfers between devices: 172 us -> 286 us
  other arithmetic: 22.9 us -> 116 us
  local copies, waits for them, and re-layouts: 128 us -> 192 us
  starting transfers between devices: 8.63 us -> 43.6 us
  matrix products: 129 us -> 96.1 us
  between operations: 18.6 us -> 4.21 us
    psum x1 -> x0, blocking collectives: 391 us -> none  [on_device(): lax.psum((owned[0], owned[1], owned[2], owned[3], owned[4], owned[5], own...]
    ppermute x0 -> x48, waiting for transfers between devices: none -> 286 us  [flip(): return lax.ppermute(array, axis, [(at, at ^ bit) for at in range(size)])]
    reduce_scatter x7 -> x0, waiting for transfers between devices: 114 us -> none  [the longest x1 50.6 us: on_device(): lax.psum_scatter(local_grads[16].astype(jnp.bfloat16), 'group', scatter_d...]
    all_to_all x2 -> x0, blocking collectives: 44.2 us -> none  [the longest x1 31.9 us: on_device(): lax.all_to_all(time_packed, 'group', split_axis=2, concat_axis=1, tiled=T...]
    ppermute x0 -> x48, starting transfers between devices: none -> 43.6 us  [flip(): return lax.ppermute(array, axis, [(at, at ^ bit) for at in range(size)])]
    reshape x10 -> x25, local copies, waits for them, and re-layouts: 21.4 us -> 61.2 us  [the longest x4 26 us: pack_grad(): rounded.reshape(4, BLOCK, blocks, D).transpose(0, 2, 1, 3)]
    all_to_all x2 -> x0, waiting for transfers between devices: 29.8 us -> none  [the longest x1 29.8 us: on_device(): lax.all_to_all(grad_place_packed, 'group', split_axis=1, concat_axis=2, t...]
    convert_element_type x23 -> x24, other arithmetic: 5.9 us -> 34.5 us  [the longest x15 27.4 us: add_rounded(): return (left.astype(f32) + right.astype(f32)).astype(bf16)]
  transfers between devices with their start and end apart: 16 -> 48, of which waited for: 7 -> 20; matrix products, arithmetic and copies ran while one was open for 21% -> 36% of each run, Pallas kernels for 0% -> 0%
where the time goes in v1:
time: 748 us; the launch traced here: 737 us
  waiting for transfers between devices  286 us (38%)
  local copies, waits for them, and re-layouts  192 us (26%)
  other arithmetic  116 us (16%)
  matrix products  96.1 us (13%)
  starting transfers between devices  43.6 us (6%)
    ppermute x48, waiting for transfers between devices, flip(): return lax.ppermute(array, axis, [(at, at ^ bit) for at in range(size)])  286 us
    ppermute x48, starting transfers between devices, flip(): return lax.ppermute(array, axis, [(at, at ^ bit) for at in range(size)])  43.6 us
    unnamed x343, local copies, waits for them, and re-layouts  32.8 us
    convert_element_type x15, other arithmetic, add_rounded(): return (left.astype(f32) + right.astype(f32)).astype(bf16)  27.4 us
    dot_general x9, matrix products, outer_sum(): lax.dot_general(left, right, (((0,), (0,)), ((), ())), preferred_element_...  26.2 us
    reshape x4, local copies, waits for them, and re-layouts, pack_grad(): rounded.reshape(4, BLOCK, blocks, D).transpose(0, 2, 1, 3)  26 us
    dot_general x10, matrix products, matmul(): return jnp.dot(left, right, preferred_element_type=f32)  23.8 us
    dot_general x7, matrix products, times_trans(): lax.dot_general(left, right, (((1,), (1,)), ((), ())), preferred_element_...  19.5 us
  transfers between devices with their start and end apart: 48, of which 20 were waited for; matrix products, arithmetic and copies ran while one was open for 36% of the time, Pallas kernels for 0%

profile of v1, /device:TPU:0, one launch (start us, length us, event | category | flops | bytes accessed | tf_op | source)
XLA Modules:
  0.0 737.2 jit_solution(14164439854193056746)
XLA Ops:
  37.9 9.1 %collective-permute-done.12 = bf16[384,768]{1,0:T(8,128)(2,1)} collective-permute-done((bf16[384,768]{1,0:T(8,128)(2,1)}, bf16[384,768]{1,0:T(8,128)(2,1)}, u32[]{:S(2)}, u32[]{:S(2)}) %collective-permute-start.12) | collective-permute-done | bytes 589856 | tf_op jit(solution)/shard_map/ppermute | solution.py:54
  54.5 13.4 %collective-permute-done.4 = bf16[488,768]{1,0:T(8,128)(2,1)} collective-permute-done((bf16[488,768]{1,0:T(8,128)(2,1)}, bf16[488,768]{1,0:T(8,128)(2,1)}, u32[]{:S(2)}, u32[]{:S(2)}) %collective-permute-start.4) | collective-permute-done | bytes 749600 | tf_op jit(solution)/shard_map/ppermute | solution.py:54
  75.6 11.9 %collective-permute-done.5 = bf16[488,768]{1,0:T(8,128)(2,1)S(1)} collective-permute-done((bf16[488,768]{1,0:T(8,128)(2,1)}, bf16[488,768]{1,0:T(8,128)(2,1)S(1)}, u32[]{:S(2)}, u32[]{:S(2)}) %collective-permute-start.5) | collective-permute-done | bytes 749600 | tf_op jit(solution)/shard_map/ppermute | solution.py:54
  102.4 12.7 %collective-permute-done.16 = bf16[768,768]{1,0:T(8,128)(2,1)S(1)} collective-permute-done((bf16[768,768]{1,0:T(8,128)(2,1)}, bf16[768,768]{1,0:T(8,128)(2,1)S(1)}, u32[]{:S(2)}, u32[]{:S(2)}) %collective-permute-start.16) | collective-permute-done | bytes 1179680 | tf_op jit(solution)/shard_map/ppermute | solution.py:54
  149.6 17.2 %fusion.216 = (f32[49,12,8]{2,1,0:T(8,128)S(1)}, f32[49,12,8,8]{2,3,1,0:T(8,128)S(1)}) fusion(f32[49,12,8,8]{2,3,1,0:T(8,128)S(1)} %fusion.88), kind=kOutput, calls=%fused_computation.409 | output fusion | flops 150535 | bytes 319872 | tf_op jit(solution)/shard_map/sub | solution.py:154
  200.2 5.5 fusion.222
  234.6 6.0 copy.218
  298.6 5.7 convolution_convert_fusion.2
  306.4 9.7 %reshape.860 = bf16[4,192,4,768]{3,2,1,0:T(4,128)(2,1)} reshape(bf16[768,3072]{1,0:T(8,128)(2,1)} %convolution_convert_fusion.1) | data formatting | bytes 9437184 | tf_op jit(solution)/shard_map/reshape | solution.py:128
  329.0 5.4 reshape.854
  393.4 5.5 reshape.842
  411.4 7.6 %fusion.2 = bf16[2,1536,768]{2,1,0:T(8,128)(2,1)} fusion(bf16[2,1536,768]{2,1,0:T(8,128)(2,1)} %collective-permute-done.40, s32[]{:T(128)S(6)} %select_n.391, bf16[2,2,768,768]{3,2,1,0:T(8,128)(2,1)S(1)} %bitcast.314, bf16[2,2,768,768]{3,2,1,0:T(8,128)(2,1)} %bitcast.328), kind=kLoop, calls=%fused_computation.9 | loop fusion | flops 18874368 | bytes 18874372 | tf_op jit(solution)/shard_map/convert_element_type | solution.py:62
  430.7 71.3 %collective-permute-done.33 = bf16[768,768]{1,0:T(8,128)(2,1)} collective-permute-done((bf16[768,768]{1,0:T(8,128)(2,1)}, bf16[768,768]{1,0:T(8,128)(2,1)}, u32[]{:S(2)}, u32[]{:S(2)}) %collective-permute-start.33) | collective-permute-done | bytes 1179680 | tf_op jit(solution)/shard_map/ppermute | solution.py:54
  506.2 27.0 %collective-permute-done.25 = bf16[976,768]{1,0:T(8,128)(2,1)} collective-permute-done((bf16[976,768]{1,0:T(8,128)(2,1)}, bf16[976,768]{1,0:T(8,128)(2,1)}, u32[]{:S(2)}, u32[]{:S(2)}) %collective-permute-start.25) | collective-permute-done | bytes 1499168 | tf_op jit(solution)/shard_map/ppermute | solution.py:54
  545.8 36.7 %collective-permute-done.26 = bf16[488,768]{1,0:T(8,128)(2,1)} collective-permute-done((bf16[488,768]{1,0:T(8,128)(2,1)}, bf16[488,768]{1,0:T(8,128)(2,1)}, u32[]{:S(2)}, u32[]{:S(2)}) %collective-permute-start.26) | collective-permute-done | bytes 749600 | tf_op jit(solution)/shard_map/ppermute | solution.py:54
  596.4 8.5 %collective-permute-done.27 = bf16[244,768]{1,0:T(8,128)(2,1)S(1)} collective-permute-done((bf16[244,768]{1,0:T(8,128)(2,1)S(1)}, bf16[244,768]{1,0:T(8,128)(2,1)S(1)}, u32[]{:S(2)}, u32[]{:S(2)}) %collective-permute-start.27) | collective-permute-done | bytes 374816 | tf_op jit(solution)/shard_map/ppermute | solution.py:54
  607.0 10.1 %collective-permute-done.43 = bf16[384,768]{1,0:T(8,128)(2,1)} collective-permute-done((bf16[384,768]{1,0:T(8,128)(2,1)S(1)}, bf16[384,768]{1,0:T(8,128)(2,1)}, u32[]{:S(2)}, u32[]{:S(2)}) %collective-permute-start.43) | collective-permute-done | bytes 589856 | tf_op jit(solution)/shard_map/ppermute | solution.py:54
  622.7 17.3 %collective-permute-done.44 = bf16[192,768]{1,0:T(8,128)(2,1)S(1)} collective-permute-done((bf16[192,768]{1,0:T(8,128)(2,1)S(1)}, bf16[192,768]{1,0:T(8,128)(2,1)S(1)}, u32[]{:S(2)}, u32[]{:S(2)}) %collective-permute-start.44) | collective-permute-done | bytes 294944 | tf_op jit(solution)/shard_map/ppermute | solution.py:54
  640.2 9.3 %collective-permute-done.37 = bf16[96,768]{1,0:T(8,128)(2,1)S(1)} collective-permute-done((bf16[96,768]{1,0:T(8,128)(2,1)S(1)}, bf16[96,768]{1,0:T(8,128)(2,1)S(1)}, u32[]{:S(2)}, u32[]{:S(2)}) %collective-permute-start.37) | collective-permute-done | bytes 147488 | tf_op jit(solution)/shard_map/ppermute | solution.py:54
  654.0 5.5 collective-permute-done.45
  666.1 8.0 %collective-permute-done.30 = bf16[244,768]{1,0:T(8,128)(2,1)S(1)} collective-permute-done((bf16[244,768]{1,0:T(8,128)(2,1)S(1)}, bf16[244,768]{1,0:T(8,128)(2,1)S(1)}, u32[]{:S(2)}, u32[]{:S(2)}) %collective-permute-start.30) | collective-permute-done | bytes 374816 | tf_op jit(solution)/shard_map/ppermute | solution.py:54
  675.9 10.7 %collective-permute-done.46 = bf16[384,768]{1,0:T(8,128)(2,1)S(1)} collective-permute-done((bf16[384,768]{1,0:T(8,128)(2,1)S(1)}, bf16[384,768]{1,0:T(8,128)(2,1)S(1)}, u32[]{:S(2)}, u32[]{:S(2)}) %collective-permute-start.46) | collective-permute-done | bytes 589856 | tf_op jit(solution)/shard_map/ppermute | solution.py:54
  700.5 5.7 collective-permute-done.31
  715.1 15.5 %collective-permute-done.47 = bf16[768,768]{1,0:T(8,128)(2,1)} collective-permute-done((bf16[768,768]{1,0:T(8,128)(2,1)}, bf16[768,768]{1,0:T(8,128)(2,1)}, u32[]{:S(2)}, u32[]{:S(2)}) %collective-permute-start.47) | collective-permute-done | bytes 1179680 | tf_op jit(solution)/shard_map/ppermute | solution.py:54
  (674 shorter events, 397.5 us)
Async XLA Ops:
  3.6 46.4 %collective-permute-start.2 = (bf16[49,2,768]{2,1,0:T(2,128)(2,1)}, bf16[49,2,768]{2,1,0:T(2,128)(2,1)}, u32[]{:S(2)}, u32[]{:S(2)}) collective-permute-start(bf16[49,2,768]{2,1,0:T(2,128)(2,1)} %get-tuple-element.83), channel_id=1, source_target_pairs={{0,24},{8,16},{16,8},{24,0},{1,25},{9,17},{17,9},{25,1},{2,26},{10... | collective-permute-start | bytes 451592 | tf_op jit(solution)/shard_map/ppermute | solution.py:54
  5.9 44.6 %collective-permute-start.1 = (bf16[49,2,768]{2,1,0:T(2,128)(2,1)}, bf16[49,2,768]{2,1,0:T(2,128)(2,1)}, u32[]{:S(2)}, u32[]{:S(2)}) collective-permute-start(bf16[49,2,768]{2,1,0:T(2,128)(2,1)} %get-tuple-element.84), channel_id=1, source_target_pairs={{0,16},{8,24},{16,0},{24,8},{1,17},{9,25},{17,1},{25,9},{2,18},{10... | collective-permute-start | bytes 451592 | tf_op jit(solution)/shard_map/ppermute | solution.py:54
  14.1 61.4 %collective-permute-start.15 = (bf16[768,768]{1,0:T(8,128)(2,1)}, bf16[768,768]{1,0:T(8,128)(2,1)}, u32[]{:S(2)}, u32[]{:S(2)}) collective-permute-start(bf16[768,768]{1,0:T(8,128)(2,1)} %fusion.78), channel_id=1, source_target_pairs={{0,16},{8,24},{16,0},{24,8},{1,17},{9,25},{17,1},{25,9},{2,18},{10... | collective-permute-start | bytes 3538952 | tf_op jit(solution)/shard_map/ppermute | solution.py:54
  25.5 42.4 %collective-permute-start.4 = (bf16[488,768]{1,0:T(8,128)(2,1)}, bf16[488,768]{1,0:T(8,128)(2,1)}, u32[]{:S(2)}, u32[]{:S(2)}) collective-permute-start(bf16[488,768]{1,0:T(8,128)(2,1)} %constant_dynamic-slice_fusion.12), channel_id=1, source_target_pairs={{0,16},{8,24},{16,0},{24,8},{1,17},{9,25},{17,1},{25,9},{2,18},{10... | collective-permute-start | bytes 2248712 | tf_op jit(solution)/shard_map/ppermute | solution.py:54
  50.0 43.0 %collective-permute-start.10 = (bf16[768,768]{1,0:T(8,128)(2,1)S(1)}, bf16[768,768]{1,0:T(8,128)(2,1)}, u32[]{:S(2)}, u32[]{:S(2)}) collective-permute-start(bf16[768,768]{1,0:T(8,128)(2,1)S(1)} %copy-done.51), channel_id=1, source_target_pairs={{0,8},{8,0},{16,24},{24,16},{1,9},{9,1},{17,25},{25,17},{2,10},{10... | collective-permute-start | bytes 3538952 | tf_op jit(solution)/shard_map/ppermute | solution.py:54
  50.5 42.6 %collective-permute-start.13 = (bf16[768,768]{1,0:T(8,128)(2,1)}, bf16[768,768]{1,0:T(8,128)(2,1)}, u32[]{:S(2)}, u32[]{:S(2)}) collective-permute-start(bf16[768,768]{1,0:T(8,128)(2,1)} %maximum_select_fusion.7), channel_id=1, source_target_pairs={{0,8},{8,0},{16,24},{24,16},{1,9},{9,1},{17,25},{25,17},{2,10},{10... | collective-permute-start | bytes 3538952 | tf_op jit(solution)/shard_map/ppermute | solution.py:54
  52.3 69.3 %collective-permute-start.3 = (bf16[976,768]{1,0:T(8,128)(2,1)}, bf16[976,768]{1,0:T(8,128)(2,1)}, u32[]{:S(2)}, u32[]{:S(2)}) collective-permute-start(bf16[976,768]{1,0:T(8,128)(2,1)} %get-tuple-element.65), channel_id=1, source_target_pairs={{0,8},{8,0},{16,24},{24,16},{1,9},{9,1},{17,25},{25,17},{2,10},{10... | collective-permute-start | bytes 4497416 | tf_op jit(solution)/shard_map/ppermute | solution.py:54
  75.5 138.9 %collective-permute-start.14 = (bf16[1536,768]{1,0:T(8,128)(2,1)}, bf16[1536,768]{1,0:T(8,128)(2,1)}, u32[]{:S(2)}, u32[]{:S(2)}) collective-permute-start(bf16[1536,768]{1,0:T(8,128)(2,1)} %get-tuple-element.57), channel_id=1, source_target_pairs={{0,8},{8,0},{16,24},{24,16},{1,9},{9,1},{17,25},{25,17},{2,10},{10... | collective-permute-start | bytes 7077896 | tf_op jit(solution)/shard_map/ppermute | solution.py:54
  93.0 28.6 %collective-permute-start.6 = (bf16[976,768]{1,0:T(8,128)(2,1)S(1)}, bf16[976,768]{1,0:T(8,128)(2,1)S(1)}, u32[]{:S(2)}, u32[]{:S(2)}) collective-permute-start(bf16[976,768]{1,0:T(8,128)(2,1)S(1)} %maximum_select_fusion.4), channel_id=1, source_target_pairs={{0,8},{8,0},{16,24},{24,16},{1,9},{9,1},{17,25},{25,17},{2,10},{10... | collective-permute-start | bytes 4497416 | tf_op jit(solution)/shard_map/ppermute | solution.py:54
  118.1 96.3 %collective-permute-start.17 = (bf16[1536,768]{1,0:T(8,128)(2,1)}, bf16[1536,768]{1,0:T(8,128)(2,1)}, u32[]{:S(2)}, u32[]{:S(2)}) collective-permute-start(bf16[1536,768]{1,0:T(8,128)(2,1)} %maximum_select_fusion.1), channel_id=1, source_target_pairs={{0,8},{8,0},{16,24},{24,16},{1,9},{9,1},{17,25},{25,17},{2,10},{10... | collective-permute-start | bytes 7077896 | tf_op jit(solution)/shard_map/ppermute | solution.py:54
  340.5 67.3 %collective-permute-start.32 = (bf16[2,768,768]{2,1,0:T(8,128)(2,1)}, bf16[2,768,768]{2,1,0:T(8,128)(2,1)}, u32[]{:S(2)}, u32[]{:S(2)}) collective-permute-start(bf16[2,768,768]{2,1,0:T(8,128)(2,1)} %fusion.25), channel_id=1, source_target_pairs={{0,8},{8,0},{16,24},{24,16},{1,9},{9,1},{17,25},{25,17},{2,10},{10... | collective-permute-start | bytes 7077896 | tf_op jit(solution)/shard_map/ppermute | solution.py:54
  348.2 62.6 %collective-permute-start.40 = (bf16[2,1536,768]{2,1,0:T(8,128)(2,1)}, bf16[2,1536,768]{2,1,0:T(8,128)(2,1)}, u32[]{:S(2)}, u32[]{:S(2)}) collective-permute-start(bf16[2,1536,768]{2,1,0:T(8,128)(2,1)} %fusion.11), channel_id=1, source_target_pairs={{0,8},{8,0},{16,24},{24,16},{1,9},{9,1},{17,25},{25,17},{2,10},{10... | collective-permute-start | bytes 14155784 | tf_op jit(solution)/shard_map/ppermute | solution.py:54
  422.2 112.8 %collective-permute-start.41 = (bf16[1536,768]{1,0:T(8,128)(2,1)}, bf16[1536,768]{1,0:T(8,128)(2,1)}, u32[]{:S(2)}, u32[]{:S(2)}) collective-permute-start(bf16[1536,768]{1,0:T(8,128)(2,1)} %dynamic-slice_bitcast_fusion.1), channel_id=1, source_target_pairs={{0,16},{8,24},{16,0},{24,8},{1,17},{9,25},{17,1},{25,9},{2,18},{10... | collective-permute-start | bytes 7077896 | tf_op jit(solution)/shard_map/ppermute | solution.py:54
  424.8 77.2 %collective-permute-start.33 = (bf16[768,768]{1,0:T(8,128)(2,1)}, bf16[768,768]{1,0:T(8,128)(2,1)}, u32[]{:S(2)}, u32[]{:S(2)}) collective-permute-start(bf16[768,768]{1,0:T(8,128)(2,1)} %dynamic-slice_bitcast_fusion.4), channel_id=1, source_target_pairs={{0,16},{8,24},{16,0},{24,8},{1,17},{9,25},{17,1},{25,9},{2,18},{10... | collective-permute-start | bytes 3538952 | tf_op jit(solution)/shard_map/ppermute | solution.py:54
  429.2 104.0 %collective-permute-start.25 = (bf16[976,768]{1,0:T(8,128)(2,1)}, bf16[976,768]{1,0:T(8,128)(2,1)}, u32[]{:S(2)}, u32[]{:S(2)}) collective-permute-start(bf16[976,768]{1,0:T(8,128)(2,1)} %dynamic-slice_bitcast_fusion.2), channel_id=1, source_target_pairs={{0,16},{8,24},{16,0},{24,8},{1,17},{9,25},{17,1},{25,9},{2,18},{10... | collective-permute-start | bytes 4497416 | tf_op jit(solution)/shard_map/ppermute | solution.py:54
  504.8 37.2 %collective-permute-start.34 = (bf16[384,768]{1,0:T(8,128)(2,1)}, bf16[384,768]{1,0:T(8,128)(2,1)}, u32[]{:S(2)}, u32[]{:S(2)}) collective-permute-start(bf16[384,768]{1,0:T(8,128)(2,1)} %dynamic-slice_bitcast_fusion.7), channel_id=1, source_target_pairs={{0,1},{1,0},{2,3},{3,2},{4,5},{5,4},{6,7},{7,6},{8,9},{9,8},{10,11... | collective-permute-start | bytes 1769480 | tf_op jit(solution)/shard_map/ppermute | solution.py:54
  538.9 50.6 %collective-permute-start.42 = (bf16[768,768]{1,0:T(8,128)(2,1)}, bf16[768,768]{1,0:T(8,128)(2,1)}, u32[]{:S(2)}, u32[]{:S(2)}) collective-permute-start(bf16[768,768]{1,0:T(8,128)(2,1)} %dynamic-slice_bitcast_fusion.3), channel_id=1, source_target_pairs={{0,1},{1,0},{2,3},{3,2},{4,5},{5,4},{6,7},{7,6},{8,9},{9,8},{10,11... | collective-permute-start | bytes 3538952 | tf_op jit(solution)/shard_map/ppermute | solution.py:54
  541.4 41.1 %collective-permute-start.26 = (bf16[488,768]{1,0:T(8,128)(2,1)}, bf16[488,768]{1,0:T(8,128)(2,1)}, u32[]{:S(2)}, u32[]{:S(2)}) collective-permute-start(bf16[488,768]{1,0:T(8,128)(2,1)} %dynamic-slice_bitcast_fusion.5), channel_id=1, source_target_pairs={{0,1},{1,0},{2,3},{3,2},{4,5},{5,4},{6,7},{7,6},{8,9},{9,8},{10,11... | collective-permute-start | bytes 2248712 | tf_op jit(solution)/shard_map/ppermute | solution.py:54
  544.2 48.4 %collective-permute-start.35 = (bf16[192,768]{1,0:T(8,128)(2,1)}, bf16[192,768]{1,0:T(8,128)(2,1)}, u32[]{:S(2)}, u32[]{:S(2)}) collective-permute-start(bf16[192,768]{1,0:T(8,128)(2,1)} %dynamic-slice_bitcast_fusion.10), channel_id=1, source_target_pairs={{0,2},{1,3},{2,0},{3,1},{4,6},{5,7},{6,4},{7,5},{8,10},{9,11},{10,... | collective-permute-start | bytes 884744 | tf_op jit(solution)/shard_map/ppermute | solution.py:54
  619.5 30.1 %collective-permute-start.37 = (bf16[96,768]{1,0:T(8,128)(2,1)S(1)}, bf16[96,768]{1,0:T(8,128)(2,1)S(1)}, u32[]{:S(2)}, u32[]{:S(2)}) collective-permute-start(bf16[96,768]{1,0:T(8,128)(2,1)S(1)} %fusion.166), channel_id=1, source_target_pairs={{0,4},{1,5},{2,6},{3,7},{4,0},{5,1},{6,2},{7,3},{8,12},{9,13},{10,... | collective-permute-start | bytes 442376 | tf_op jit(solution)/shard_map/ppermute | solution.py:54
  621.7 32.1 %collective-permute-start.29 = (bf16[122,768]{1,0:T(8,128)(2,1)S(1)}, bf16[122,768]{1,0:T(8,128)(2,1)S(1)}, u32[]{:S(2)}, u32[]{:S(2)}) collective-permute-start(bf16[122,768]{1,0:T(8,128)(2,1)S(1)} %fusion.165), channel_id=1, source_target_pairs={{0,4},{1,5},{2,6},{3,7},{4,0},{5,1},{6,2},{7,3},{8,12},{9,13},{10,... | collective-permute-start | bytes 562184 | tf_op jit(solution)/shard_map/ppermute | solution.py:54
  662.9 28.9 %collective-permute-start.23 = (bf16[104,768]{1,0:T(8,128)(2,1)S(1)}, bf16[104,768]{1,0:T(8,128)(2,1)S(1)}, u32[]{:S(2)}, u32[]{:S(2)}) collective-permute-start(bf16[104,768]{1,0:T(8,128)(2,1)S(1)} %get-tuple-element.69), channel_id=1, source_target_pairs={{0,24},{8,16},{16,8},{24,0},{1,25},{9,17},{17,9},{25,1},{2,26},{10... | collective-permute-start | bytes 479240 | tf_op jit(solution)/shard_map/ppermute | solution.py:54
  663.4 30.5 %collective-permute-start.22 = (bf16[104,768]{1,0:T(8,128)(2,1)S(1)}, bf16[104,768]{1,0:T(8,128)(2,1)S(1)}, u32[]{:S(2)}, u32[]{:S(2)}) collective-permute-start(bf16[104,768]{1,0:T(8,128)(2,1)S(1)} %get-tuple-element.70), channel_id=1, source_target_pairs={{0,16},{8,24},{16,0},{24,8},{1,17},{9,25},{17,1},{25,9},{2,18},{10... | collective-permute-start | bytes 479240 | tf_op jit(solution)/shard_map/ppermute | solution.py:54
  691.9 38.8 %collective-permute-start.47 = (bf16[768,768]{1,0:T(8,128)(2,1)}, bf16[768,768]{1,0:T(8,128)(2,1)}, u32[]{:S(2)}, u32[]{:S(2)}) collective-permute-start(bf16[768,768]{1,0:T(8,128)(2,1)} %maximum_select_fusion.9), channel_id=1, source_target_pairs={{0,1},{1,0},{2,3},{3,2},{4,5},{5,4},{6,7},{7,6},{8,9},{9,8},{10,11... | collective-permute-start | bytes 3538952 | tf_op jit(solution)/shard_map/ppermute | solution.py:54
  (189 other events, 3964.8 us)

commit v2 on v1

v2 whole, which is shorter than its diff:
```python
import functools

import jax
import jax.numpy as jnp
from jax import lax
from jax.experimental import pallas as pl
from jax.experimental.pallas import tpu as pltpu
from jax.sharding import PartitionSpec as P

D = 768
FF = 3072
HEADS = 12
HEAD_DIM = 64
PLACES = 196
BLOCK = 192
CHUNK = 104
HALF = 208
ROWS = 416
epsilon = 1e-06
bf16 = jnp.bfloat16
f32 = jnp.float32

TIME_GAIN, TIME_SHIFT, TIME_PROJ_B, TIME_FC_B, SPACE_GAIN, SPACE_SHIFT, SPACE_PROJ_B = range(7)
MLP_GAIN, MLP_SHIFT, MLP_OUT_B = 7, 8, 9
TIME_QV, SPACE_QV, MLP_IN_B = 10, 12, 14
VECTOR_ROWS = 18
EXTRA = 64

TIME_QKV_PARTS = ((0, 0, 192, 0, 0), (0, 192, 192, 0, 1), (1, 0, 192, 0, 2))
TIME_PROJ_PARTS = ((1, 192, 192, 0, 0),)
SPACE_QKV_PARTS = ((0, 0, 192, 0, 0), (0, 192, 192, 0, 1), (1, 96, 192, 0, 2))
SPACE_PROJ_PARTS = ((1, 288, 192, 0, 0),)
TIME_FC_PARTS = ((0, 384, 96, 0, 0), (1, 0, 96, 96, 0))
MLP_IN_PARTS = ((0, 0, 192, 0, 0), (0, 192, 192, 0, 1), (1, 0, 192, 0, 2), (1, 192, 192, 0, 3))
MLP_OUT_PARTS = ((0, 0, 384, 0, 0), (1, 0, 384, 384, 0))
TIME_CHUNK, SPACE_CHUNK, IN_CHUNK, OUT_CHUNK = (0, 768), (768, 960), (1728, 768), (2496, 768)
VECTOR_AT = 3264


def nn(left, right):
    return lax.dot_general(left, right, (((1,), (0,)), ((), ())), preferred_element_type=f32)


def nt(left, right):
    return lax.dot_general(left, right, (((1,), (1,)), ((), ())), preferred_element_type=f32)


def tn(left, right):
    return lax.dot_general(left, right, (((0,), (0,)), ((), ())), preferred_element_type=f32)


def norm_parts(values):
    centred = values - jnp.mean(values, axis=-1, keepdims=True)
    inverse = lax.rsqrt(jnp.mean(centred * centred, axis=-1, keepdims=True) + epsilon)
    return centred * inverse, inverse


class Weights:
    def __init__(self, scalars, own, pieces, parts, chunk, target, sems):
        self.scalars, self.own, self.pieces, self.parts = scalars, own, pieces, parts
        self.chunk, self.target, self.sems = chunk, target, sems
        self.shard_rows = own.shape[0]

    def base(self, flipped):
        at = (self.scalars[0] ^ flipped) * self.shard_rows
        return pl.multiple_of(at, self.shard_rows)

    def copy(self, source, part, flipped, at):
        half, row, rows, block_row, column = part
        return pltpu.make_async_copy(
            source.at[pl.ds(row, rows), :],
            self.target.at[pl.ds(self.base(flipped) + block_row, rows), pl.ds(column * D, D)],
            self.sems.at[at],
        )

    def own_copy(self):
        target = self.target.at[pl.ds(self.base(0), self.shard_rows), :]
        return pltpu.make_async_copy(self.own, target, self.sems.at[0])

    def start(self):
        packed, direct, relayed, across, across_relayed = self.pieces
        self.own_copy().start()
        y = self.scalars[1]
        first, chunk_rows = self.chunk
        at = 1
        for part in self.parts:
            half, row, rows, block_row, column = part
            whole = (half, first + row + half * (chunk_rows // 2), rows, block_row, column)
            self.copy(packed, whole, 1, at).start()

            @pl.when(y == half)
            def _():
                self.copy(direct, part, 2, at + 1).start()
                self.copy(across, part, 3, at + 2).start()

            @pl.when(y != half)
            def _():
                self.copy(relayed, part, 2, at + 1).start()
                self.copy(across_relayed, part, 3, at + 2).start()

            at += 3

    def wait(self):
        direct, across = self.pieces[1], self.pieces[3]
        self.own_copy().wait()
        at = 1
        for part in self.parts:
            self.copy(direct, part, 1, at).wait()
            self.copy(direct, part, 2, at + 1).wait()
            self.copy(across, part, 3, at + 2).wait()
            at += 3


def lane_half(second):
    lane = lax.broadcasted_iota(jnp.int32, (HALF, 128), 1)
    return (lane >= 64) if second else (lane < 64)


def masked(values, second):
    return jnp.where(lane_half(second), values, jnp.zeros_like(values))


def key_mask(same_place):
    key = lax.broadcasted_iota(jnp.int32, (HALF, HALF), 0)
    query = lax.broadcasted_iota(jnp.int32, (HALF, HALF), 1)
    allowed = (key // 8 == query // 8) if same_place else (key < PLACES)
    return jnp.where(allowed, 0.0, -1e30).astype(f32)


def probs_of(key_pair, query_pair, mask, second):
    scores = nt(masked(key_pair, second), query_pair) + mask
    weights = jnp.exp(scores - jnp.max(scores, axis=0, keepdims=True))
    return weights * (1.0 / jnp.sum(weights, axis=0, keepdims=True))


def merged_rows(first, second):
    return jnp.concatenate([first[:64], second[64:]], axis=0)


def attend(qkv_ref, mask, out_ref):
    def pair_step(pair, carry):
        column = pl.multiple_of(pair * 128, 128)
        for part in range(2):
            rows = pl.ds(part * HALF, HALF)
            query = qkv_ref[rows, pl.ds(column, 128)] * bf16(HEAD_DIM**-0.5)
            key_part = qkv_ref[rows, pl.ds(D + column, 128)]
            value_part = qkv_ref[rows, pl.ds(2 * D + column, 128)]
            mixed = [
                tn(value_part, probs_of(key_part, query, mask, second).astype(bf16))
                for second in (False, True)
            ]
            out_ref[rows, pl.ds(column, 128)] = merged_rows(*mixed).T.astype(bf16)
        return carry

    lax.fori_loop(0, HEADS // 2, pair_step, 0)


def attend_back(qkv_ref, mask, grad_ref, out_ref):
    def pair_step(pair, carry):
        column = pl.multiple_of(pair * 128, 128)
        for part in range(2):
            rows = pl.ds(part * HALF, HALF)
            query = qkv_ref[rows, pl.ds(column, 128)] * bf16(HEAD_DIM**-0.5)
            key_part = qkv_ref[rows, pl.ds(D + column, 128)]
            value_part = qkv_ref[rows, pl.ds(2 * D + column, 128)]
            grad = grad_ref[rows, pl.ds(column, 128)]
            grads = ([], [], [])
            for second in (False, True):
                probs = probs_of(key_part, query, mask, second)
                grad_probs = nt(masked(value_part, second), grad)
                centre = jnp.sum(grad_probs * probs, axis=0, keepdims=True)
                grad_scores = (probs * (grad_probs - centre)).astype(bf16)
                grads[0].append(tn(key_part, grad_scores))
                grads[1].append(nn(grad_scores, query))
                grads[2].append(nn(probs.astype(bf16), grad))
            grad_query = merged_rows(*grads[0]).T * HEAD_DIM**-0.5
            out_ref[rows, pl.ds(column, 128)] = grad_query.astype(bf16)
            first = lane_half(False)
            out_ref[rows, pl.ds(D + column, 128)] = jnp.where(first, *grads[1]).astype(bf16)
            out_ref[rows, pl.ds(2 * D + column, 128)] = jnp.where(first, *grads[2]).astype(bf16)
        return carry

    lax.fori_loop(0, HEADS // 2, pair_step, 0)


def project_qkv(normed, weight, vec, qv_row, out_ref):
    for member in range(3):
        packed = nn(normed, weight[:, member * D : (member + 1) * D])
        if member != 1:
            row = qv_row + member // 2
            packed = packed + vec[row : row + 1, :]
        out_ref[:, member * D : (member + 1) * D] = packed.astype(bf16)


def place_to_send(dest):
    local = lax.broadcasted_iota(jnp.int32, (CHUNK, ROWS), 0)
    col = lax.broadcasted_iota(jnp.int32, (CHUNK, ROWS), 1)
    source = (local // 2) * 8 + dest * 2 + local % 2
    return ((col == source) & (local < 98)).astype(bf16)


def recv_to_frame(group_at, source):
    row = lax.broadcasted_iota(jnp.int32, (ROWS, CHUNK), 0)
    col = lax.broadcasted_iota(jnp.int32, (ROWS, CHUNK), 1)
    second = (row >= HALF).astype(jnp.int32)
    spot = row - second * HALF
    local = (spot - (group_at ^ source) * 49) * 2 + second
    inside = (spot >= (group_at ^ source) * 49) & (spot < ((group_at ^ source) + 1) * 49)
    return ((col == local) & inside).astype(bf16)


def place_forward_kernel(
    scalars, tokens, vec, *refs
):
    own_qkv, own_proj, *pieces = refs[:7]
    h1, qkv, mixed, o1, *rest = refs[7:]
    sends, (w_qkv, w_proj, sem_a, sem_b) = rest[:4], rest[4:]
    qkv_copy = Weights(scalars, own_qkv, pieces, TIME_QKV_PARTS, TIME_CHUNK, w_qkv, sem_a)
    proj_copy = Weights(scalars, own_proj, pieces, TIME_PROJ_PARTS, TIME_CHUNK, w_proj, sem_b)
    qkv_copy.start()
    proj_copy.start()
    normal, unused = norm_parts(tokens[...].astype(f32))
    normed = (normal * vec[TIME_GAIN : TIME_GAIN + 1, :] + vec[TIME_SHIFT : TIME_SHIFT + 1, :])
    normed = normed.astype(bf16)
    h1[...] = normed
    qkv_copy.wait()
    project_qkv(normed, w_qkv, vec, TIME_QV, qkv)
    attend(qkv, key_mask(True), mixed)
    proj_copy.wait()
    out = (nn(mixed[...], w_proj[...]) + vec[TIME_PROJ_B : TIME_PROJ_B + 1, :]).astype(bf16)
    o1[...] = out
    for dest in range(4):
        sends[dest][...] = nn(place_to_send(dest), out).astype(bf16)


def frame_forward_kernel(scalars, tokens, vec, r0, r1, r2, r3, *refs):
    own_fc, own_qkv, own_proj, *pieces = refs[:8]
    x1, h2, qkv, mixed, x2, h3 = refs[8:14]
    w_fc, w_qkv, w_proj, sem_a, sem_b, sem_c = refs[14:]
    fc_copy = Weights(scalars, own_fc, pieces, TIME_FC_PARTS, SPACE_CHUNK, w_fc, sem_a)
    qkv_copy = Weights(scalars, own_qkv, pieces, SPACE_QKV_PARTS, SPACE_CHUNK, w_qkv, sem_b)
    proj_copy = Weights(scalars, own_proj, pieces, SPACE_PROJ_PARTS, SPACE_CHUNK, w_proj, sem_c)
    fc_copy.start()
    qkv_copy.start()
    proj_copy.start()
    group_at = scalars[0]
    received = sum(
        nn(recv_to_frame(group_at, source), ref[...]) for source, ref in enumerate((r0, r1, r2, r3))
    ).astype(bf16)
    fc_copy.wait()
    branch = nn(received, w_fc[...]) + vec[TIME_FC_B : TIME_FC_B + 1, :]
    after = tokens[...].astype(f32) + branch
    x1[...] = after
    normal, unused = norm_parts(after)
    normed = normal * vec[SPACE_GAIN : SPACE_GAIN + 1, :] + vec[SPACE_SHIFT : SPACE_SHIFT + 1, :]
    normed = normed.astype(bf16)
    h2[...] = normed
    qkv_copy.wait()
    project_qkv(normed, w_qkv, vec, SPACE_QV, qkv)
    attend(qkv, key_mask(False), mixed)
    proj_copy.wait()
    after = x1[...] + (nn(mixed[...], w_proj[...]) + vec[SPACE_PROJ_B : SPACE_PROJ_B + 1, :])
    x2[...] = after
    normal, unused = norm_parts(after)
    normed = normal * vec[MLP_GAIN : MLP_GAIN + 1, :] + vec[MLP_SHIFT : MLP_SHIFT + 1, :]
    h3[...] = normed.astype(bf16)


def norm_back(values, gain, grad_normed):
    normal, inverse = norm_parts(values)
    scaled = grad_normed * gain
    mean = jnp.mean(scaled, axis=-1, keepdims=True)
    along = jnp.mean(scaled * normal, axis=-1, keepdims=True)
    grad = inverse * (scaled - mean - normal * along)
    return (
        grad,
        jnp.sum(grad_normed * normal, axis=0, keepdims=True),
        jnp.sum(grad_normed, axis=0, keepdims=True),
    )


def column_sum(values):
    return jnp.sum(values.astype(f32), axis=0, keepdims=True)


def mlp_kernel(scalars, live, vec, x2, h3, out_grad, *refs):
    own_in, own_out, *pieces = refs[:11]
    in_pieces, out_pieces = [pieces[0]] + pieces[1:5], [pieces[0]] + pieces[5:9]
    layer_out, acts, du, dm, e2, sums, w_in, w_out, sem_a, sem_b = refs[11:]
    in_copy = Weights(scalars, own_in, in_pieces, MLP_IN_PARTS, IN_CHUNK, w_in, sem_a)
    out_copy = Weights(scalars, own_out, out_pieces, MLP_OUT_PARTS, OUT_CHUNK, w_out, sem_b)
    in_copy.start()
    out_copy.start()
    e3 = live[0, 0] * out_grad[...].astype(f32)
    grad_branch = e3.astype(bf16)
    dm[...] = grad_branch
    sums[3:4, :] = column_sum(grad_branch)
    sums[4:8, :] = jnp.zeros((4, D), f32)
    normed = h3[...]
    in_copy.wait()
    out_copy.wait()
    x3 = x2[...] + vec[MLP_OUT_B : MLP_OUT_B + 1, :]
    e2[...] = x3
    back = None
    for part in range(4):
        columns = slice(part * D, (part + 1) * D)
        pre = nn(normed, w_in[:, columns]) + vec[MLP_IN_B + part : MLP_IN_B + part + 1, :]
        cdf = 0.5 * (1.0 + lax.erf(pre * (0.5**0.5)))
        act = (pre * cdf).astype(bf16)
        slope = cdf + pre * jnp.exp(-0.5 * pre * pre) * 0.3989422804014327
        acts[:, columns] = act
        grad = (slope * nt(grad_branch, w_out[columns, :])).astype(bf16)
        du[:, columns] = grad
        sums[4 + part : 5 + part, :] = column_sum(grad)
        e2[...] += nn(act, w_out[columns, :])
        piece = nt(grad, w_in[:, columns])
        back = piece if back is None else back + piece
    layer_out[...] = (live[0, 0] * e2[...]).astype(bf16)
    grad, gain_grad, shift_grad = norm_back(x2[...], vec[MLP_GAIN : MLP_GAIN + 1, :], back)
    sums[0:1, :] = gain_grad
    sums[1:2, :] = shift_grad
    sums[2:3, :] = jnp.zeros((1, D), f32)
    e2[...] = e3 + grad


def space_back_kernel(scalars, vec, e2, x1, qkv, *refs):
    own_proj, own_qkv, *pieces = refs[:7]
    dqkv, e1, dt2, sums, s0, s1, s2, s3, w_qkv, w_proj, da, sem_a, sem_b = refs[7:]
    proj_copy = Weights(scalars, own_proj, pieces, SPACE_PROJ_PARTS, SPACE_CHUNK, w_proj, sem_a)
    qkv_copy = Weights(scalars, own_qkv, pieces, SPACE_QKV_PARTS, SPACE_CHUNK, w_qkv, sem_b)
    proj_copy.start()
    qkv_copy.start()
    branch = e2[...].astype(bf16)
    dt2[...] = branch
    proj_copy.wait()
    da[...] = nt(branch, w_proj[...]).astype(bf16)
    attend_back(qkv, key_mask(False), da, dqkv)
    qkv_copy.wait()
    back = nt(dqkv[...], w_qkv[...])
    grad, gain_grad, shift_grad = norm_back(x1[...], vec[SPACE_GAIN : SPACE_GAIN + 1, :], back)
    total = e2[...] + grad
    e1[...] = total
    rounded = total.astype(bf16)
    for source, ref in enumerate((s0, s1, s2, s3)):
        ref[...] = tn(recv_to_frame(scalars[0], source), rounded).astype(bf16)
    sums[0:1, :] = gain_grad
    sums[1:2, :] = shift_grad
    sums[2:3, :] = column_sum(branch)
    sums[3:4, :] = column_sum(dqkv[:, :D])
    sums[4:5, :] = column_sum(dqkv[:, 2 * D :])
    sums[5:8, :] = jnp.zeros((3, D), f32)


def time_back_kernel(scalars, vec, tokens, qkv, r0, r1, r2, r3, *refs):
    own_fc, own_proj, own_qkv, packed, *pieces = refs[:12]
    fc_pieces, pieces = [packed] + pieces[:4], [packed] + pieces[4:]
    (
        dqkv, dt1, do1, sums, s0, s1, s2, s3, w_fc, w_proj, w_qkv, da, sem_a, sem_b, sem_c,
    ) = refs[12:]
    fc_copy = Weights(scalars, own_fc, fc_pieces, TIME_FC_PARTS, SPACE_CHUNK, w_fc, sem_a)
    proj_copy = Weights(scalars, own_proj, pieces, TIME_PROJ_PARTS, TIME_CHUNK, w_proj, sem_b)
    qkv_copy = Weights(scalars, own_qkv, pieces, TIME_QKV_PARTS, TIME_CHUNK, w_qkv, sem_c)
    fc_copy.start()
    proj_copy.start()
    qkv_copy.start()
    branch = sum(
        tn(place_to_send(source), ref[...]) for source, ref in enumerate((r0, r1, r2, r3))
    ).astype(bf16)
    dt1[...] = branch
    fc_copy.wait()
    projected = nt(branch, w_fc[...]).astype(bf16)
    do1[...] = projected
    proj_copy.wait()
    da[...] = nt(projected, w_proj[...]).astype(bf16)
    attend_back(qkv, key_mask(True), da, dqkv)
    qkv_copy.wait()
    back = nt(dqkv[...], w_qkv[...])
    grad, gain_grad, shift_grad = norm_back(
        tokens[...].astype(f32), vec[TIME_GAIN : TIME_GAIN + 1, :], back
    )
    rounded = grad.astype(bf16)
    for dest, ref in enumerate((s0, s1, s2, s3)):
        ref[...] = nn(place_to_send(dest), rounded).astype(bf16)
    sums[0:1, :] = gain_grad
    sums[1:2, :] = shift_grad
    sums[2:3, :] = column_sum(projected)
    sums[3:4, :] = column_sum(branch)
    sums[4:5, :] = column_sum(dqkv[:, :D])
    sums[5:6, :] = column_sum(dqkv[:, 2 * D :])
    sums[6:8, :] = jnp.zeros((2, D), f32)


def weight_grad_kernel(scalars, *refs, count, tables):
    inputs, (kept, sent) = refs[:-2], refs[-2:]
    core = scalars[0] % 2

    def store(shard, rows, columns, values):
        @pl.when(core == shard % 2)
        def _():
            kept[shard // 2, rows, columns] = values

        @pl.when(core != shard % 2)
        def _():
            sent[shard // 2, rows, columns] = values

    at = 0
    for index in range(count):
        left, right = inputs[2 * index : 2 * index + 2]
        shard_rows = left.shape[1] // 4
        for block in range(right.shape[1] // D):
            columns = slice(block * D, (block + 1) * D)
            total = tn(left[...], right[:, columns]).astype(bf16)
            for shard in range(4):
                values = total[shard * shard_rows : (shard + 1) * shard_rows, :]
                store(shard, slice(at, at + shard_rows), slice(0, D), values)
            at += shard_rows
    if tables:
        time, space, mlp = (ref[...] for ref in inputs[2 * count :])
        singles = jnp.concatenate([time[0:4], space[0:3], mlp[0:2], mlp[3:4]], axis=0)
        for ref in (kept, sent):
            for chip in range(2):
                ref[chip, at : at + EXTRA, :] = jnp.zeros((EXTRA, D), bf16)
        for shard in range(4):
            lanes = slice(shard * BLOCK, (shard + 1) * BLOCK)
            store(shard, slice(at, at + 10), slice(0, BLOCK), singles[:, lanes].astype(bf16))
            half = slice((shard % 2) * (D // 2), (shard % 2 + 1) * (D // 2))
            for row, pair in ((10, time[4:6]), (11, space[3:5])):
                values = pair[shard // 2 : shard // 2 + 1, half].astype(bf16)
                store(shard, slice(at + row, at + row + 1), slice(0, D // 2), values)
            values = mlp[4 + shard : 5 + shard, :].astype(bf16)
            store(shard, slice(at + 12, at + 13), slice(0, D), values)


def last_kernel(scalars, e1, r0, r1, r2, r3, out):
    total = e1[...]
    for source, ref in enumerate((r0, r1, r2, r3)):
        total = total + nn(recv_to_frame(scalars[0], source), ref[...])
    out[...] = total


def shape(rows, columns, kind):
    return jax.ShapeDtypeStruct((rows, columns), kind)


VMEM = pl.BlockSpec(memory_space=pltpu.MemorySpace.VMEM)
SMEM = pl.BlockSpec(memory_space=pltpu.MemorySpace.SMEM)
ANY = pl.BlockSpec(memory_space=pl.ANY)


def call(kernel, name, outs, specs, scratch, operands, microseconds, limit=48):
    return pl.pallas_call(
        kernel,
        name=name,
        out_shape=outs,
        in_specs=specs,
        out_specs=[VMEM] * len(outs),
        scratch_shapes=scratch,
        compiler_params=pltpu.CompilerParams(vmem_limit_bytes=limit << 20),
        cost_estimate=pl.CostEstimate(
            flops=int(microseconds * 1.1e9), transcendentals=0, bytes_accessed=1 << 20
        ),
    )(*operands)


def dma_sems(parts):
    return pltpu.SemaphoreType.DMA((1 + 3 * len(parts),))


def vmem(rows, columns, kind=bf16):
    return pltpu.VMEM((rows, columns), kind)


def place_forward(scalars, tokens, vec, owns, pieces):
    outs = [shape(ROWS, D, bf16), shape(ROWS, 3 * D, bf16), shape(ROWS, D, bf16)]
    outs += [shape(ROWS, D, bf16)] + [shape(CHUNK, D, bf16)] * 4
    return call(
        place_forward_kernel, "place_forward", outs, [SMEM, VMEM, VMEM] + [ANY] * 7,
        [vmem(D, 3 * D), vmem(D, D), dma_sems(TIME_QKV_PARTS), dma_sems(TIME_PROJ_PARTS)],
        (scalars, tokens, vec, *owns, *pieces), 11,
    )


def frame_forward(scalars, tokens, vec, received, owns, pieces):
    outs = [shape(ROWS, D, f32), shape(ROWS, D, bf16), shape(ROWS, 3 * D, bf16)]
    outs += [shape(ROWS, D, bf16), shape(ROWS, D, f32), shape(ROWS, D, bf16)]
    return call(
        frame_forward_kernel, "frame_forward", outs, [SMEM] + [VMEM] * 6 + [ANY] * 8,
        [
            vmem(D, D), vmem(D, 3 * D), vmem(D, D),
            dma_sems(TIME_FC_PARTS), dma_sems(SPACE_QKV_PARTS), dma_sems(SPACE_PROJ_PARTS),
        ],
        (scalars, tokens, vec, *received, *owns, *pieces), 13,
    )


def mlp_both(scalars, live, vec, x2, h3, out_grad, owns, in_pieces, out_pieces):
    outs = [
        shape(ROWS, D, bf16), shape(ROWS, FF, bf16), shape(ROWS, FF, bf16),
        shape(ROWS, D, bf16), shape(ROWS, D, f32), shape(8, D, f32),
    ]
    return call(
        mlp_kernel, "mlp_both", outs, [SMEM, SMEM] + [VMEM] * 4 + [ANY] * 11,
        [vmem(D, FF), vmem(FF, D), dma_sems(MLP_IN_PARTS), dma_sems(MLP_OUT_PARTS)],
        (scalars, live, vec, x2, h3, out_grad, *owns, *in_pieces, *out_pieces[1:]), 18, 56,
    )


def space_back(scalars, vec, e2, x1, qkv, owns, pieces):
    outs = [shape(ROWS, 3 * D, bf16), shape(ROWS, D, f32), shape(ROWS, D, bf16)]
    outs += [shape(8, D, f32)] + [shape(CHUNK, D, bf16)] * 4
    return call(
        space_back_kernel, "space_back", outs, [SMEM] + [VMEM] * 4 + [ANY] * 7,
        [
            vmem(D, 3 * D), vmem(D, D), vmem(ROWS, D),
            dma_sems(SPACE_PROJ_PARTS), dma_sems(SPACE_QKV_PARTS),
        ],
        (scalars, vec, e2, x1, qkv, *owns, *pieces), 20,
    )


def time_back(scalars, vec, tokens, qkv, received, owns, fc_pieces, pieces):
    outs = [shape(ROWS, 3 * D, bf16), shape(ROWS, D, bf16), shape(ROWS, D, bf16)]
    outs += [shape(8, D, f32)] + [shape(CHUNK, D, bf16)] * 4
    return call(
        time_back_kernel, "time_back", outs, [SMEM] + [VMEM] * 7 + [ANY] * 12,
        [
            vmem(D, D), vmem(D, D), vmem(D, 3 * D), vmem(ROWS, D),
            dma_sems(TIME_FC_PARTS), dma_sems(TIME_PROJ_PARTS), dma_sems(TIME_QKV_PARTS),
        ],
        (scalars, vec, tokens, qkv, *received, *owns, *fc_pieces, *pieces[1:]), 21,
    )


def weight_grads(name, scalars, groups, tables=()):
    rows = sum(g[0].shape[1] // 4 * (g[1].shape[1] // D) for g in groups)
    flat = [array for group in groups for array in group] + list(tables)
    rows += EXTRA if tables else 0
    kernel = functools.partial(weight_grad_kernel, count=len(groups), tables=len(tables))
    return call(
        kernel, name, [jax.ShapeDtypeStruct((2, rows, D), bf16)] * 2, [SMEM] + [VMEM] * len(flat),
        [], (scalars, *flat), rows / 128,
    )


def last_sum(scalars, e1, received):
    return call(
        last_kernel, "last_sum", [shape(ROWS, D, f32)], [SMEM] + [VMEM] * 5, [],
        (scalars, e1, *received), 2,
    )[0]


def flip(array, axis, bit, size):
    return lax.ppermute(array, axis, [(at, at ^ bit) for at in range(size)])


def pick(array, at):
    return lax.dynamic_index_in_dim(array, at, 0, keepdims=False)


def add_rounded(left, right):
    return (left.astype(f32) + right.astype(f32)).astype(bf16)


def after(value, *others):
    return lax.optimization_barrier((value,) + others)[0]


def halves_of(own, half_at):
    return lax.dynamic_slice_in_dim(own, half_at * (own.shape[0] // 2), own.shape[0] // 2, 0)


class Reduce:
    def __init__(self, parts, order, group_at, replica_at, ring_size):
        self.kept, sent = parts
        self.group_at, self.replica_at = group_at, replica_at
        self.ring_size = ring_size
        self.steps = [("sum", -1)] + [("sum", bit) for bit in order]
        self.steps += [("gather", bit) for bit in reversed(order) if bit]
        self.flying = flip(sent, "group", 1, 4)

    def place(self, bit):
        return (self.replica_at // bit) % 2

    def start(self, *others):
        kind, bit = self.steps[0]
        if kind == "gather":
            sent = self.current
        elif bit == 0:
            chip = self.group_at // 2
            sent, self.kept = pick(self.current, 1 - chip), pick(self.current, chip)
        else:
            rows = self.current.shape[-2] // 2
            mine = self.place(bit)
            sent = lax.dynamic_slice_in_dim(self.current, (1 - mine) * rows, rows, -2 % self.current.ndim)
            self.kept = lax.dynamic_slice_in_dim(self.current, mine * rows, rows, -2 % self.current.ndim)
        if others:
            sent = after(sent, *others)
        axis = ("group", 2, 4) if bit == 0 else ("replica", bit, self.ring_size)
        self.flying = flip(sent, *axis)

    def finish(self, *others):
        kind, bit = self.steps.pop(0)
        got = after(self.flying, *others) if others else self.flying
        if kind == "sum":
            self.current = add_rounded(self.kept, got)
        else:
            mine = self.place(bit)
            self.current = jnp.where(
                mine == 0,
                jnp.concatenate([self.current, got], 0),
                jnp.concatenate([got, self.current], 0),
            )
        return self.current

    def advance(self, *others):
        result = self.finish(*others)
        if self.steps:
            self.start()
        return result


def block(array, at):
    return array[:, at * D : (at + 1) * D]


def unpack_grad(summed, blocks):
    return summed.reshape(blocks, BLOCK, D).transpose(1, 0, 2).reshape(BLOCK, blocks * D).astype(f32)


def exchange(chunks):
    return [chunks[0]] + [flip(chunks[d], "group", d, 4) for d in range(1, 4)]


def build(mesh):
    ring_size = mesh.shape["replica"]

    def on_device(tokens, out_grad, slot_mask, *shards):
        (
            time_norm_gain, time_norm_shift, time_qkv, time_qv_bias, time_proj, time_proj_bias,
            time_fc, time_fc_bias, space_norm_gain, space_norm_shift, space_qkv, space_qv_bias,
            space_proj, space_proj_bias, mlp_norm_gain, mlp_norm_shift, mlp_in, mlp_in_bias,
            mlp_out, mlp_out_bias,
        ) = shards
        group_at = lax.axis_index("group")
        replica_at = lax.axis_index("replica")
        half_at = replica_at % 2
        scalars = jnp.stack([group_at, half_at]).astype(jnp.int32)
        live = slot_mask.astype(f32).reshape(1, 1)
        vectors = [
            time_norm_gain, time_norm_shift, time_proj_bias, time_fc_bias, space_norm_gain,
            space_norm_shift, space_proj_bias, mlp_norm_gain, mlp_norm_shift, mlp_out_bias,
            time_qv_bias, space_qv_bias, mlp_in_bias,
        ]
        cross = functools.partial(flip, axis="group", bit=2, size=4)
        near = functools.partial(flip, axis="group", bit=1, size=4)
        relay = functools.partial(flip, axis="replica", bit=1, size=ring_size)
        flat = jnp.pad(jnp.concatenate(vectors), (0, 8 * D - VECTOR_ROWS * BLOCK)).reshape(8, D)
        time_half = jnp.where(
            half_at == 0,
            jnp.concatenate([block(time_qkv, 0), block(time_qkv, 1), flat]),
            jnp.concatenate([block(time_qkv, 2), time_proj, flat]),
        )
        time_direct = cross(time_half)
        token_pieces = tokens[0].transpose(1, 0, 2).reshape(4, 49, 2, D)
        got = exchange([pick(token_pieces, group_at ^ d) for d in range(4)])
        place_tokens = jnp.pad(jnp.concatenate(got, axis=1), ((0, 3), (0, 0), (0, 0)))
        place_tokens = place_tokens.reshape(ROWS, D)

        packed = jnp.concatenate(
            [
                block(time_qkv, 0), block(time_qkv, 1), block(time_qkv, 2), time_proj,
                block(space_qkv, 0), block(space_qkv, 1), time_fc, block(space_qkv, 2), space_proj,
                block(mlp_in, 0), block(mlp_in, 1), block(mlp_in, 2), block(mlp_in, 3), mlp_out,
                flat,
            ]
        )

        def half_of(chunk):
            first, rows = chunk
            return lax.dynamic_slice_in_dim(packed, first + half_at * (rows // 2), rows // 2, 0)

        partner = near(packed)
        time_across = near(time_direct)
        time_relayed = relay(time_direct)
        time_pieces = (partner, time_direct, time_relayed, time_across, near(time_relayed))
        space_direct = cross(after(half_of(SPACE_CHUNK), time_direct, got[2], got[3]))
        in_direct = cross(after(half_of(IN_CHUNK), space_direct))
        out_direct = cross(after(half_of(OUT_CHUNK), in_direct))

        held = [flat, partner[VECTOR_AT:], time_direct[384:], time_across[384:]]
        held = jnp.stack(held).reshape(4, 8 * D)[:, : VECTOR_ROWS * BLOCK]
        tables = jnp.stack([pick(held, group_at ^ shard) for shard in range(4)]).astype(f32)
        tables = tables.reshape(4, VECTOR_ROWS, BLOCK)
        vec = jnp.concatenate(
            [
                tables[:, :10].transpose(1, 0, 2).reshape(10, D),
                tables[:, 10:12].reshape(2, D),
                tables[:, 12:14].reshape(2, D),
                tables[:, 14:18].reshape(4, D),
                jnp.zeros((6, D), f32),
            ]
        )
        pads = ((0, 0), (0, HALF - PLACES), (0, 0))
        frame_tokens = jnp.pad(tokens[0], pads).reshape(ROWS, D)
        frame_grad = jnp.pad(out_grad[0], pads).reshape(ROWS, D)

        h1, qkv1, a1, o1, *sends = place_forward(
            scalars, after(place_tokens, space_direct), vec, (time_qkv, time_proj), time_pieces
        )
        received = exchange(sends)
        space_relayed = relay(space_direct)
        space_pieces = (
            partner, space_direct, space_relayed, near(space_direct),
            near(after(space_relayed, o1)),
        )
        x1, h2, qkv2, a2, x2, h3 = frame_forward(
            scalars, after(frame_tokens, in_direct), vec, received,
            (time_fc, space_qkv, space_proj), space_pieces,
        )
        in_relayed = relay(in_direct)
        in_pieces = (
            partner, in_direct, in_relayed, near(after(in_direct, x2)), near(after(in_relayed, x2)),
        )
        out_direct = after(out_direct, x2)
        out_relayed = relay(out_direct)
        out_pieces = (partner, out_direct, out_relayed, near(out_direct), near(out_relayed))
        layer_out, act, du, dm, e2, sums3 = mlp_both(
            scalars, live, vec, x2, h3, frame_grad, (mlp_in, mlp_out), in_pieces, out_pieces
        )
        layer_out = layer_out.reshape(2, HALF, D)[None, :, :PLACES]

        chunk = functools.partial(
            Reduce, group_at=group_at, replica_at=replica_at, ring_size=ring_size
        )
        bits = [1 << at for at in range(ring_size.bit_length() - 1)]
        along = [0] + bits
        first_y = bits[:1] + [0] + bits[1:]
        first_z = bits[1:2] + [0] + bits[:1] + bits[2:]

        way_out = chunk(weight_grads("mlp_out_grad", scalars, [(act, dm)]), along)
        way_in = chunk(
            weight_grads("mlp_in_grad", scalars, [(h3, after(du, way_out.kept))]), first_y
        )
        one = way_out.advance(way_in.kept)
        two = way_in.advance(one)
        dqkv2, e1, dt2, sums2, *sends = space_back(
            scalars, vec, after(e2, one, two), x1, qkv2, (space_proj, space_qkv), space_pieces
        )
        received = exchange(sends)
        one = way_out.advance(e1)
        two = way_in.advance(one)
        way_space = chunk(
            weight_grads("space_grad", scalars, [(h2, after(dqkv2, two)), (a2, dt2)]), first_z
        )
        three = way_space.advance(two)
        dqkv1, dt1, do1, sums1, *sends = time_back(
            scalars, vec, after(place_tokens, three), qkv1, received,
            (time_fc, time_proj, time_qkv), space_pieces, time_pieces,
        )
        received = exchange(sends)
        one = way_out.advance(dqkv1)
        two = way_in.advance(one)
        three = way_space.advance(two)
        way_time = chunk(weight_grads("time_grad", scalars, [(h1, after(dqkv1, three))]), along)
        way_small = chunk(
            weight_grads(
                "time_small_grad", scalars, [(a1, after(do1, way_time.kept)), (o1, dt1)],
                (sums1, sums2, sums3),
            ),
            first_y,
        )
        last = way_time.advance(way_small.kept)
        last = way_small.advance(last)
        tokens_grad = last_sum(scalars, after(e1, last), received)
        last = tokens_grad
        tokens_grad = tokens_grad.reshape(2, HALF, D)[None, :, :PLACES]
        ways = [way_out, way_in, way_space, way_time, way_small]
        while any(way.steps for way in ways):
            for way in ways:
                if way.steps:
                    last = way.advance(last)
        sum_out, sum_in, sum_space, sum_time, sum_small = (way.current for way in ways)
        vectors = sum_small[384:].astype(f32)
        ones = vectors[:10, :BLOCK]
        return (
            layer_out, tokens_grad, ones[0], ones[1], unpack_grad(sum_time, 3),
            vectors[10, : D // 2], sum_small[:192].astype(f32), ones[2],
            sum_small[192:384].astype(f32), ones[3],
            ones[4], ones[5], unpack_grad(sum_space[:576], 3), vectors[11, : D // 2],
            sum_space[576:768].astype(f32), ones[6], ones[7], ones[8], unpack_grad(sum_in, 4),
            vectors[12], sum_out.astype(f32), ones[9],
        )

    return on_device


def solution(mesh):
    rows = P("group", None)
    vector = P("group")
    batch = P("replica", "group", None, None)
    params = (
        vector, vector, rows, vector, rows, vector, rows, vector, vector, vector, rows, vector,
        rows, vector, vector, vector, rows, vector, rows, vector,
    )
    return jax.shard_map(
        build(mesh),
        mesh=mesh,
        in_specs=(batch, batch, P("replica")) + params,
        out_specs=(batch, batch) + params,
        check_vma=False,
    )
```

time: 748 us -> 407 us (0.54)
  local copies, waits for them, and re-layouts: 192 us -> 44.5 us
  waiting for transfers between devices: 286 us -> 150 us
  Pallas kernels: 0 us -> 110 us
  matrix products: 96.1 us -> 0 us
  other arithmetic: 116 us -> 28.9 us
  starting transfers between devices: 43.6 us -> 66.4 us
    ppermute x48 -> x69, waiting for transfers between devices: 286 us -> 150 us  [flip(): return lax.ppermute(array, axis, [(at, at ^ bit) for at in range(size)])]
    pallas_call x0 -> x11, Pallas kernels: none -> 110 us  [call(): pl.pallas_call(kernel, name=name, out_shape=outs, in_specs=specs, out_spe...]
    dot_general x37 -> x0, matrix products: 90.6 us -> none  [the longest x9 26.2 us: outer_sum(): lax.dot_general(left, right, (((0,), (0,)), ((), ())), preferred_element_...]
    reshape x25 -> x5, local copies, waits for them, and re-layouts: 61.2 us -> 0.39 us  [the longest x1 0.09 us: on_device(): tables[:, :10].transpose(1, 0, 2).reshape(10, D)]
    another operation x9 -> x2, other arithmetic: 26.3 us -> 0.15 us  [the longest x1 0.07 us: on_device(): scalars = jnp.stack([group_at, half_at]).astype(jnp.int32)]
    ppermute x48 -> x69, starting transfers between devices: 43.6 us -> 66.4 us  [flip(): return lax.ppermute(array, axis, [(at, at ^ bit) for at in range(size)])]
    slice x34 -> x6, local copies, waits for them, and re-layouts: 23.9 us -> 3.21 us  [the longest x1 1.27 us: on_device(): layer_out = layer_out.reshape(2, HALF, D)[None, :, :PLACES]]
    sub x1 -> x0, other arithmetic: 17.2 us -> none  [attend(): weights = jnp.exp(scores - maximum)]
  transfers between devices with their start and end apart: 48 -> 69, of which waited for: 20 -> 29; matrix products, arithmetic and copies ran while one was open for 36% -> 11% of each run, Pallas kernels for 0% -> 19%
where the time goes in v2:
time: 407 us; the launch traced here: 402 us
  waiting for transfers between devices  150 us (37%)
  Pallas kernels  110 us (27%)
  starting transfers between devices  66.4 us (16%)
  local copies, waits for them, and re-layouts  44.5 us (11%)
  other arithmetic  28.9 us (7%)
    ppermute x69, waiting for transfers between devices, flip(): return lax.ppermute(array, axis, [(at, at ^ bit) for at in range(size)])  150 us
    pallas_call x11, Pallas kernels, call(): pl.pallas_call(kernel, name=name, out_shape=outs, in_specs=specs, out_spe...  110 us
    ppermute x69, starting transfers between devices, flip(): return lax.ppermute(array, axis, [(at, at ^ bit) for at in range(size)])  66.4 us
    unnamed x192, local copies, waits for them, and re-layouts  27.7 us
    convert_element_type x25, other arithmetic, add_rounded(): return (left.astype(f32) + right.astype(f32)).astype(bf16)  19.9 us
  transfers between devices with their start and end apart: 69, of which 29 were waited for; matrix products, arithmetic and copies ran while one was open for 11% of the time, Pallas kernels for 19%

profile of v2, /device:TPU:0, one launch (start us, length us, event | category | flops | bytes accessed | tf_op | source)
XLA Modules:
  0.0 402.5 jit_solution(13050544710264665475)
XLA Ops:
  23.9 14.0 %collective-permute-done.3 = bf16[49,2,768]{2,1,0:T(2,128)(2,1)S(1)} collective-permute-done((bf16[49,2,768]{2,1,0:T(2,128)(2,1)S(1)}, bf16[49,2,768]{2,1,0:T(2,128)(2,1)S(1)}, u32[]{:S(2)}, u32[]{:S(2)}) %collective-permute-start.3) | collective-permute-done | bytes 150560 | tf_op jit(solution)/shard_map/ppermute | solution.py:553
  48.6 12.1 %collective-permute-done.8.refs_4_.refs_9_ = bf16[392,768]{1,0:T(8,128)(2,1)} collective-permute-done((bf16[392,768]{1,0:T(8,128)(2,1)S(1)}, bf16[392,768]{1,0:T(8,128)(2,1)}, u32[]{:S(2)}, u32[]{:S(2)}) %collective-permute-start.8) | collective-permute-done | bytes 602144 | tf_op jit(solution)/shard_map/ppermute | solution.py:553
  64.8 11.0 %place_forward.1 = (bf16[416,768]{1,0:T(8,128)(2,1)S(1)}, bf16[416,2304]{1,0:T(8,128)(2,1)}, bf16[416,768]{1,0:T(8,128)(2,1)S(1)}, bf16[416,768]{1,0:T(8,128)(2,...) custom-call(s32[2]{0:T(128)S(1)} %pad_add_fusion.scalars, ...), custom_call_target="tpu_custom_call" | custom-call | flops 12099999744 | bytes 1048576 | tf_op jit(solution)/shard_map/place_forward/pallas_call | solution.py:451
  75.9 4.3 %collective-permute-done.13.refs_5_.refs_4_ = bf16[480,768]{1,0:T(8,128)(2,1)} collective-permute-done((bf16[480,768]{1,0:T(8,128)(2,1)}, bf16[480,768]{1,0:T(8,128)(2,1)}, u32[]{:S(2)}, u32[]{:S(2)}) %collective-permute-start.13) | collective-permute-done | bytes 737312 | tf_op jit(solution)/shard_map/ppermute | solution.py:553
  91.1 12.8 %frame_forward.1 = (f32[416,768]{1,0:T(8,128)}, bf16[416,768]{1,0:T(8,128)(2,1)S(1)}, bf16[416,2304]{1,0:T(8,128)(2,1)}, bf16[416,768]{1,0:T(8,128)(2,1)S(1)}, f...) custom-call(s32[2]{0:T(128)S(1)} %pad_add_fusion.scalars, bf16[416,768]{1,0:T(8,128)(2,1)S(1)} %bitcast.95, ...), custom_call_target="tpu_custom_call" | custom-call | flops 14300000256 | bytes 1048576 | tf_op jit(solution)/shard_map/frame_forward/pallas_call | solution.py:451
  106.8 13.4 %collective-permute-done.20.refs_8_ = bf16[384,768]{1,0:T(8,128)(2,1)S(1)} collective-permute-done((bf16[384,768]{1,0:T(8,128)(2,1)S(1)}, bf16[384,768]{1,0:T(8,128)(2,1)S(1)}, u32[]{:S(2)}, u32[]{:S(2)}) %collective-permute-start.20) | collective-permute-done | bytes 589856 | tf_op jit(solution)/shard_map/ppermute | solution.py:553
  123.3 16.3 %mlp_both.1 = (bf16[416,768]{1,0:T(8,128)(2,1)}, bf16[416,3072]{1,0:T(8,128)(2,1)}, bf16[416,3072]{1,0:T(8,128)(2,1)}, bf16[416,768]{1,0:T(8,128)(2,1)}, f32[416,768]{1,0:T(8,128)}, /*index=5*/f32[8,768]{1,0:T(8,128)}) custom-call(s32[2]{0:T(128)} %copy-done.26, f32[1,1]{1,0:T(1,128)} %bitcast.2.live, f32[24,768]{1,0:T(8,128)} %copy-done.10, ...), custom_call_target="tpu_custom_call" | custom-call | flops 19800000512 | bytes 1048576 | tf_op jit(solution)/shard_map/mlp_both/pallas_call | solution.py:451
  140.7 6.9 %mlp_out_grad.1 = (bf16[2,768,768]{2,1,0:T(8,128)(2,1)S(1)}, bf16[2,768,768]{2,1,0:T(8,128)(2,1)}) custom-call(s32[2]{0:T(128)S(1)} %copy-done.27, bf16[416,3072]{1,0:T(8,128)(2,1)} %get-tuple-element.140.refs_0_, bf16[416,768]{1,0:T(8,128)(2,1)S(1)} %copy-done.45), custom_call_target="tpu_custom_call" | custom-call | flops 6600000000 | bytes 1048576 | tf_op jit(solution)/shard_map/mlp_out_grad/pallas_call | solution.py:451
  148.0 7.7 %mlp_in_grad.1 = (bf16[2,768,768]{2,1,0:T(8,128)(2,1)S(1)}, bf16[2,768,768]{2,1,0:T(8,128)(2,1)}) custom-call(s32[2]{0:T(128)S(1)} %copy-done.27, bf16[416,768]{1,0:T(8,128)(2,1)S(1)} %copy-done.44, bf16[416,3072]{1,0:T(8,128)(2,1)} %get-tuple-element.145.refs_1_), custom_call_target="tpu_custom_call" | custom-call | flops 6600000000 | bytes 1048576 | tf_op jit(solution)/shard_map/mlp_in_grad/pallas_call | solution.py:451
  166.0 19.0 %space_back.1 = (bf16[416,2304]{1,0:T(8,128)(2,1)}, f32[416,768]{1,0:T(8,128)}, bf16[416,768]{1,0:T(8,128)(2,1)S(1)}, f32[8,768]{1,0:T(8,128)S(1)}, bf16[104,768...) custom-call(s32[2]{0:T(128)S(1)} %copy-done.27, ...), custom_call_target="tpu_custom_call" | custom-call | flops 22000001024 | bytes 1048576 | tf_op jit(solution)/shard_map/space_back/pallas_call | solution.py:451
  185.1 7.3 %collective-permute-done.26 = bf16[768,768]{1,0:T(8,128)(2,1)S(1)} collective-permute-done((bf16[768,768]{1,0:T(8,128)(2,1)S(1)}, bf16[768,768]{1,0:T(8,128)(2,1)S(1)}, u32[]{:S(2)}, u32[]{:S(2)}) %collective-permute-start.26) | collective-permute-done | bytes 1179680 | tf_op jit(solution)/shard_map/ppermute | solution.py:553
  196.0 6.5 %space_grad.1 = (bf16[2,768,768]{2,1,0:T(8,128)(2,1)S(1)}, bf16[2,768,768]{2,1,0:T(8,128)(2,1)}) custom-call(s32[2]{0:T(128)S(1)} %copy-done.27, bf16[416,768]{1,0:T(8,128)(2,1)S(1)} %copy-done.40, bf16[416,2304]{1,0:T(8,128)(2,1)S(1)} %copy-done.36, bf16[416,768]{1,0:T(8,128)(2,1)S(1)} %copy-done.42, bf16[416,768]{1,0:T(8,128)(2,1)S(1)} %get-tuple-element.161.refs_3_), custom_call_target="tpu_custom_call" | custom-call | flops 6600000000 | bytes 1048576 | tf_op jit(solution)/shard_map/space_grad/pallas_call | solution.py:451
  213.6 18.9 %time_back.1 = (bf16[416,2304]{1,0:T(8,128)(2,1)}, bf16[416,768]{1,0:T(8,128)(2,1)S(1)}, bf16[416,768]{1,0:T(8,128)(2,1)S(1)}, f32[8,768]{1,0:T(8,128)S(1)}, bf1...) custom-call(s32[2]{0:T(128)S(1)} %copy-done.27, ...), custom_call_target="tpu_custom_call" | custom-call | flops 23100000256 | bytes 1048576 | tf_op jit(solution)/shard_map/time_back/pallas_call | solution.py:451
  241.1 5.0 %time_grad.1 = (bf16[2,576,768]{2,1,0:T(8,128)(2,1)S(1)}, bf16[2,576,768]{2,1,0:T(8,128)(2,1)}) custom-call(s32[2]{0:T(128)S(1)} %copy-done.27, bf16[416,768]{1,0:T(8,128)(2,1)S(1)} %copy-done.38, bf16[416,2304]{1,0:T(8,128)(2,1)S(1)} %copy-done.29), custom_call_target="tpu_custom_call" | custom-call | flops 4950000128 | bytes 1048576 | tf_op jit(solution)/shard_map/time_grad/pallas_call | solution.py:451
  246.1 4.4 %time_small_grad.1 = (bf16[2,448,768]{2,1,0:T(8,128)(2,1)S(1)}, bf16[2,448,768]{2,1,0:T(8,128)(2,1)}) custom-call(s32[2]{0:T(128)S(1)} %copy-done.27, bf16[416,768]{1,0:T(8,128)(2,1)S(1)} %copy-done.33, bf16[416,768]{1,0:T(8,128)(2,1)S(1)} %get-tuple-element.179.refs_1_, bf16[416,768]{1,0:T(8,128)(2,1)S(1)} %copy-done.35, ...), custom_call_target="tpu_custom_call" | custom-call | flops 3849999872 | bytes 1048576 | tf_op jit(solution)/shard_map/time_small_grad/pallas_call | solution.py:451
  269.9 4.4 %collective-permute-done.42 = bf16[192,768]{1,0:T(8,128)(2,1)S(1)} collective-permute-done((bf16[192,768]{1,0:T(8,128)(2,1)S(1)}, bf16[192,768]{1,0:T(8,128)(2,1)S(1)}, u32[]{:S(2)}, u32[]{:S(2)}) %collective-permute-start.42) | collective-permute-done | bytes 294944 | tf_op jit(solution)/shard_map/ppermute | solution.py:553
  282.9 12.5 %collective-permute-done.40 = bf16[576,768]{1,0:T(8,128)(2,1)S(1)} collective-permute-done((bf16[576,768]{1,0:T(8,128)(2,1)S(1)}, bf16[576,768]{1,0:T(8,128)(2,1)S(1)}, u32[]{:S(2)}, u32[]{:S(2)}) %collective-permute-start.40) | collective-permute-done | bytes 884768 | tf_op jit(solution)/shard_map/ppermute | solution.py:553
  304.2 5.3 %collective-permute-done.45 = bf16[288,768]{1,0:T(8,128)(2,1)S(1)} collective-permute-done((bf16[288,768]{1,0:T(8,128)(2,1)S(1)}, bf16[288,768]{1,0:T(8,128)(2,1)S(1)}, u32[]{:S(2)}, u32[]{:S(2)}) %collective-permute-start.45) | collective-permute-done | bytes 442400 | tf_op jit(solution)/shard_map/ppermute | solution.py:553
  321.7 16.2 %collective-permute-done.50 = bf16[144,768]{1,0:T(8,128)(2,1)S(1)} collective-permute-done((bf16[144,768]{1,0:T(8,128)(2,1)S(1)}, bf16[144,768]{1,0:T(8,128)(2,1)S(1)}, u32[]{:S(2)}, u32[]{:S(2)}) %collective-permute-start.50) | collective-permute-done | bytes 221216 | tf_op jit(solution)/shard_map/ppermute | solution.py:553
  338.0 3.5 collective-permute-done.49
  347.7 4.9 %collective-permute-done.55 = bf16[72,768]{1,0:T(8,128)(2,1)S(1)} collective-permute-done((bf16[72,768]{1,0:T(8,128)(2,1)S(1)}, bf16[72,768]{1,0:T(8,128)(2,1)S(1)}, u32[]{:S(2)}, u32[]{:S(2)}) %collective-permute-start.55) | collective-permute-done | bytes 110624 | tf_op jit(solution)/shard_map/ppermute | solution.py:553
  360.6 11.4 %collective-permute-done.59 = bf16[56,768]{1,0:T(8,128)(2,1)S(1)} collective-permute-done((bf16[56,768]{1,0:T(8,128)(2,1)S(1)}, bf16[56,768]{1,0:T(8,128)(2,1)S(1)}, u32[]{:S(2)}, u32[]{:S(2)}) %collective-permute-start.59) | collective-permute-done | bytes 86048 | tf_op jit(solution)/shard_map/ppermute | solution.py:553
  388.2 3.9 collective-permute-done.65
  395.3 4.1 %collective-permute-done.66 = bf16[288,768]{1,0:T(8,128)(2,1)S(1)} collective-permute-done((bf16[288,768]{1,0:T(8,128)(2,1)S(1)}, bf16[288,768]{1,0:T(8,128)(2,1)S(1)}, u32[]{:S(2)}, u32[]{:S(2)}) %collective-permute-start.66) | collective-permute-done | bytes 442400 | tf_op jit(solution)/shard_map/ppermute | solution.py:553
  (420 shorter events, 173.6 us)
Async XLA Ops:
  16.1 46.7 %collective-permute-start = (bf16[3272,768]{1,0:T(8,128)(2,1)}, bf16[3272,768]{1,0:T(8,128)(2,1)}, u32[]{:S(2)}, u32[]{:S(2)}) collective-permute-start(bf16[3272,768]{1,0:T(8,128)(2,1)} %constant_dynamic-update-slice_fusion), channel_id=1, source_target_pairs={{0,8},{8,0},{16,24},{24,16},{1,9},{9,1},{17,25},{25,17},{2,10},{10... | collective-permute-start | bytes 15077384 | tf_op jit(solution)/shard_map/ppermute | solution.py:553
  17.5 23.2 %collective-permute-start.1 = (bf16[392,768]{1,0:T(8,128)(2,1)}, bf16[392,768]{1,0:T(8,128)(2,1)S(1)}, u32[]{:S(2)}, u32[]{:S(2)}) collective-permute-start(bf16[392,768]{1,0:T(8,128)(2,1)} %fusion.13), channel_id=1, source_target_pairs={{0,16},{8,24},{16,0},{24,8},{1,17},{9,25},{17,1},{25,9},{2,18},{10... | collective-permute-start | bytes 1806344 | tf_op jit(solution)/shard_map/ppermute | solution.py:553
  20.6 20.2 %collective-permute-start.4 = (bf16[49,2,768]{2,1,0:T(2,128)(2,1)S(1)}, bf16[49,2,768]{2,1,0:T(2,128)(2,1)S(1)}, u32[]{:S(2)}, u32[]{:S(2)}) collective-permute-start(bf16[49,2,768]{2,1,0:T(2,128)(2,1)S(1)} %get-tuple-element.240), channel_id=1, source_target_pairs={{0,24},{8,16},{16,8},{24,0},{1,25},{9,17},{17,9},{25,1},{2,26},{10... | collective-permute-start | bytes 451592 | tf_op jit(solution)/shard_map/ppermute | solution.py:553
  22.1 24.2 %collective-permute-start.7 = (bf16[49,2,768]{2,1,0:T(2,128)(2,1)S(1)}, bf16[49,2,768]{2,1,0:T(2,128)(2,1)S(1)}, u32[]{:S(2)}, u32[]{:S(2)}) collective-permute-start(bf16[49,2,768]{2,1,0:T(2,128)(2,1)S(1)} %get-tuple-element.239), channel_id=1, source_target_pairs={{0,8},{8,0},{16,24},{24,16},{1,9},{9,1},{17,25},{25,17},{2,10},{10... | collective-permute-start | bytes 451592 | tf_op jit(solution)/shard_map/ppermute | solution.py:553
  60.7 21.5 %collective-permute-start.6 = (bf16[384,768]{1,0:T(8,128)(2,1)}, bf16[384,768]{1,0:T(8,128)(2,1)}, u32[]{:S(2)}, u32[]{:S(2)}) collective-permute-start(bf16[384,768]{1,0:T(8,128)(2,1)} %get-tuple-element.123), channel_id=1, source_target_pairs={{0,16},{8,24},{16,0},{24,8},{1,17},{9,25},{17,1},{25,9},{2,18},{10... | collective-permute-start | bytes 1769480 | tf_op jit(solution)/shard_map/ppermute | solution.py:553
  82.4 21.6 %collective-permute-start.19 = (bf16[384,768]{1,0:T(8,128)(2,1)S(1)}, bf16[384,768]{1,0:T(8,128)(2,1)S(1)}, u32[]{:S(2)}, u32[]{:S(2)}) collective-permute-start(bf16[384,768]{1,0:T(8,128)(2,1)S(1)} %copy-done.61), channel_id=1, source_target_pairs={{0,16},{8,24},{16,0},{24,8},{1,17},{9,25},{17,1},{25,9},{2,18},{10... | collective-permute-start | bytes 1769480 | tf_op jit(solution)/shard_map/ppermute | solution.py:553
  83.8 22.5 %collective-permute-start.16 = (bf16[384,768]{1,0:T(8,128)(2,1)}, bf16[384,768]{1,0:T(8,128)(2,1)S(1)}, u32[]{:S(2)}, u32[]{:S(2)}) collective-permute-start(bf16[384,768]{1,0:T(8,128)(2,1)} %collective-permute-done.6.refs_3_), channel_id=1, source_target_pairs={{0,1},{1,0},{2,3},{3,2},{4,5},{5,4},{6,7},{7,6},{8,9},{9,8},{10,11... | collective-permute-start | bytes 1769480 | tf_op jit(solution)/shard_map/ppermute | solution.py:553
  164.3 28.1 %collective-permute-start.26 = (bf16[768,768]{1,0:T(8,128)(2,1)S(1)}, bf16[768,768]{1,0:T(8,128)(2,1)S(1)}, u32[]{:S(2)}, u32[]{:S(2)}) collective-permute-start(bf16[768,768]{1,0:T(8,128)(2,1)S(1)} %dynamic-slice_bitcast_fusion), channel_id=1, source_target_pairs={{0,16},{8,24},{16,0},{24,8},{1,17},{9,25},{17,1},{25,9},{2,18},{10... | collective-permute-start | bytes 3538952 | tf_op jit(solution)/shard_map/ppermute | solution.py:553
  164.6 29.2 %collective-permute-start.25 = (bf16[2,384,768]{2,1,0:T(8,128)(2,1)S(1)}, bf16[2,384,768]{2,1,0:T(8,128)(2,1)S(1)}, u32[]{:S(2)}, u32[]{:S(2)}) collective-permute-start(bf16[2,384,768]{2,1,0:T(8,128)(2,1)S(1)} %constant_dynamic-slice_fusion.14), channel_id=1, source_target_pairs={{0,1},{1,0},{2,3},{3,2},{4,5},{5,4},{6,7},{7,6},{8,9},{9,8},{10,11... | collective-permute-start | bytes 3538952 | tf_op jit(solution)/shard_map/ppermute | solution.py:553
  206.4 26.2 %collective-permute-start.33 = (bf16[384,768]{1,0:T(8,128)(2,1)}, bf16[384,768]{1,0:T(8,128)(2,1)}, u32[]{:S(2)}, u32[]{:S(2)}) collective-permute-start(bf16[384,768]{1,0:T(8,128)(2,1)} %constant_dynamic-slice_fusion.12), channel_id=1, source_target_pairs={{0,1},{1,0},{2,3},{3,2},{4,5},{5,4},{6,7},{7,6},{8,9},{9,8},{10,11... | collective-permute-start | bytes 1769480 | tf_op jit(solution)/shard_map/ppermute | solution.py:553
  208.8 25.9 %collective-permute-start.32 = (bf16[384,768]{1,0:T(8,128)(2,1)S(1)}, bf16[384,768]{1,0:T(8,128)(2,1)}, u32[]{:S(2)}, u32[]{:S(2)}) collective-permute-start(bf16[384,768]{1,0:T(8,128)(2,1)S(1)} %dynamic-slice_bitcast_fusion.3), channel_id=1, source_target_pairs={{0,16},{8,24},{16,0},{24,8},{1,17},{9,25},{17,1},{25,9},{2,18},{10... | collective-permute-start | bytes 1769480 | tf_op jit(solution)/shard_map/ppermute | solution.py:553
  211.9 27.9 %collective-permute-start.31 = (bf16[2,384,768]{2,1,0:T(8,128)(2,1)S(1)}, bf16[2,384,768]{2,1,0:T(8,128)(2,1)S(1)}, u32[]{:S(2)}, u32[]{:S(2)}) collective-permute-start(bf16[2,384,768]{2,1,0:T(8,128)(2,1)S(1)} %constant_dynamic-slice_fusion.13), channel_id=1, source_target_pairs={{0,2},{1,3},{2,0},{3,1},{4,6},{5,7},{6,4},{7,5},{8,10},{9,11},{10,... | collective-permute-start | bytes 3538952 | tf_op jit(solution)/shard_map/ppermute | solution.py:553
  265.5 29.9 %collective-permute-start.40 = (bf16[576,768]{1,0:T(8,128)(2,1)S(1)}, bf16[576,768]{1,0:T(8,128)(2,1)S(1)}, u32[]{:S(2)}, u32[]{:S(2)}) collective-permute-start(bf16[576,768]{1,0:T(8,128)(2,1)S(1)} %dynamic-slice_bitcast_fusion.1), channel_id=1, source_target_pairs={{0,16},{8,24},{16,0},{24,8},{1,17},{9,25},{17,1},{25,9},{2,18},{10... | collective-permute-start | bytes 2654216 | tf_op jit(solution)/shard_map/ppermute | solution.py:553
  267.2 28.6 %collective-permute-start.48 = (bf16[96,768]{1,0:T(8,128)(2,1)S(1)}, bf16[96,768]{1,0:T(8,128)(2,1)S(1)}, u32[]{:S(2)}, u32[]{:S(2)}) collective-permute-start(bf16[96,768]{1,0:T(8,128)(2,1)S(1)} %constant_dynamic-slice_fusion.5), channel_id=1, source_target_pairs={{0,4},{1,5},{2,6},{3,7},{4,0},{5,1},{6,2},{7,3},{8,12},{9,13},{10,... | collective-permute-start | bytes 442376 | tf_op jit(solution)/shard_map/ppermute | solution.py:553
  274.4 21.3 %collective-permute-start.39 = (bf16[2,224,768]{2,1,0:T(8,128)(2,1)S(1)}, bf16[2,224,768]{2,1,0:T(8,128)(2,1)S(1)}, u32[]{:S(2)}, u32[]{:S(2)}) collective-permute-start(bf16[2,224,768]{2,1,0:T(8,128)(2,1)S(1)} %constant_dynamic-slice_fusion.11), channel_id=1, source_target_pairs={{0,1},{1,0},{2,3},{3,2},{4,5},{5,4},{6,7},{7,6},{8,9},{9,8},{10,11... | collective-permute-start | bytes 2064392 | tf_op jit(solution)/shard_map/ppermute | solution.py:553
  277.7 20.9 %collective-permute-start.47 = (bf16[96,768]{1,0:T(8,128)(2,1)S(1)}, bf16[96,768]{1,0:T(8,128)(2,1)S(1)}, u32[]{:S(2)}, u32[]{:S(2)}) collective-permute-start(bf16[96,768]{1,0:T(8,128)(2,1)S(1)} %constant_dynamic-slice_fusion.6), channel_id=1, source_target_pairs={{0,4},{1,5},{2,6},{3,7},{4,0},{5,1},{6,2},{7,3},{8,12},{9,13},{10,... | collective-permute-start | bytes 442376 | tf_op jit(solution)/shard_map/ppermute | solution.py:553
  312.2 31.0 %collective-permute-start.58 = (bf16[192,768]{1,0:T(8,128)(2,1)S(1)}, bf16[192,768]{1,0:T(8,128)(2,1)S(1)}, u32[]{:S(2)}, u32[]{:S(2)}) collective-permute-start(bf16[192,768]{1,0:T(8,128)(2,1)S(1)} %maximum_select_fusion.10), channel_id=1, source_target_pairs={{0,2},{1,3},{2,0},{3,1},{4,6},{5,7},{6,4},{7,5},{8,10},{9,11},{10,... | collective-permute-start | bytes 884744 | tf_op jit(solution)/shard_map/ppermute | solution.py:553
  315.5 28.0 %collective-permute-start.57 = (bf16[192,768]{1,0:T(8,128)(2,1)S(1)}, bf16[192,768]{1,0:T(8,128)(2,1)S(1)}, u32[]{:S(2)}, u32[]{:S(2)}) collective-permute-start(bf16[192,768]{1,0:T(8,128)(2,1)S(1)} %maximum_select_fusion.11), channel_id=1, source_target_pairs={{0,2},{1,3},{2,0},{3,1},{4,6},{5,7},{6,4},{7,5},{8,10},{9,11},{10,... | collective-permute-start | bytes 884744 | tf_op jit(solution)/shard_map/ppermute | solution.py:553
  317.4 20.5 %collective-permute-start.50 = (bf16[144,768]{1,0:T(8,128)(2,1)S(1)}, bf16[144,768]{1,0:T(8,128)(2,1)S(1)}, u32[]{:S(2)}, u32[]{:S(2)}) collective-permute-start(bf16[144,768]{1,0:T(8,128)(2,1)S(1)} %constant_dynamic-slice_fusion.3), channel_id=1, source_target_pairs={{0,2},{1,3},{2,0},{3,1},{4,6},{5,7},{6,4},{7,5},{8,10},{9,11},{10,... | collective-permute-start | bytes 663560 | tf_op jit(solution)/shard_map/ppermute | solution.py:553
  318.1 23.4 %collective-permute-start.49 = (bf16[112,768]{1,0:T(8,128)(2,1)S(1)}, bf16[112,768]{1,0:T(8,128)(2,1)S(1)}, u32[]{:S(2)}, u32[]{:S(2)}) collective-permute-start(bf16[112,768]{1,0:T(8,128)(2,1)S(1)} %constant_dynamic-slice_fusion.4), channel_id=1, source_target_pairs={{0,2},{1,3},{2,0},{3,1},{4,6},{5,7},{6,4},{7,5},{8,10},{9,11},{10,... | collective-permute-start | bytes 516104 | tf_op jit(solution)/shard_map/ppermute | solution.py:553
  319.6 24.0 %collective-permute-start.56 = (bf16[96,768]{1,0:T(8,128)(2,1)S(1)}, bf16[96,768]{1,0:T(8,128)(2,1)S(1)}, u32[]{:S(2)}, u32[]{:S(2)}) collective-permute-start(bf16[96,768]{1,0:T(8,128)(2,1)S(1)} %add_convert_fusion.15), channel_id=1, source_target_pairs={{0,4},{1,5},{2,6},{3,7},{4,0},{5,1},{6,2},{7,3},{8,12},{9,13},{10,... | collective-permute-start | bytes 442376 | tf_op jit(solution)/shard_map/ppermute | solution.py:553
  345.7 28.4 %collective-permute-start.68 = (bf16[384,768]{1,0:T(8,128)(2,1)S(1)}, bf16[384,768]{1,0:T(8,128)(2,1)S(1)}, u32[]{:S(2)}, u32[]{:S(2)}) collective-permute-start(bf16[384,768]{1,0:T(8,128)(2,1)S(1)} %maximum_select_fusion.5), channel_id=1, source_target_pairs={{0,1},{1,0},{2,3},{3,2},{4,5},{5,4},{6,7},{7,6},{8,9},{9,8},{10,11... | collective-permute-start | bytes 1769480 | tf_op jit(solution)/shard_map/ppermute | solution.py:553
  347.1 30.5 %collective-permute-start.67 = (bf16[384,768]{1,0:T(8,128)(2,1)S(1)}, bf16[384,768]{1,0:T(8,128)(2,1)S(1)}, u32[]{:S(2)}, u32[]{:S(2)}) collective-permute-start(bf16[384,768]{1,0:T(8,128)(2,1)S(1)} %maximum_select_fusion.6), channel_id=1, source_target_pairs={{0,1},{1,0},{2,3},{3,2},{4,5},{5,4},{6,7},{7,6},{8,9},{9,8},{10,11... | collective-permute-start | bytes 1769480 | tf_op jit(solution)/shard_map/ppermute | solution.py:553
  354.6 23.6 %collective-permute-start.64 = (bf16[384,768]{1,0:T(8,128)(2,1)S(1)}, bf16[384,768]{1,0:T(8,128)(2,1)S(1)}, u32[]{:S(2)}, u32[]{:S(2)}) collective-permute-start(bf16[384,768]{1,0:T(8,128)(2,1)S(1)} %maximum_select_fusion.7), channel_id=1, source_target_pairs={{0,2},{1,3},{2,0},{3,1},{4,6},{5,7},{6,4},{7,5},{8,10},{9,11},{10,... | collective-permute-start | bytes 1769480 | tf_op jit(solution)/shard_map/ppermute | solution.py:553
  (128 other events, 1149.7 us)

commit v3 on v2

--- a/solution.py
+++ b/solution.py
@@ -25,6 +25,12 @@
 TIME_QV, SPACE_QV, MLP_IN_B = 10, 12, 14
 VECTOR_ROWS = 18
 EXTRA = 64
+LIMITS = {
+    "place_forward": 10, "frame_forward": 14, "mlp_both": 28, "space_back": 19, "time_back": 13,
+    "mlp_out_grad": 8, "mlp_in_grad": 8, "space_grad": 7, "pack_rest": 8, "time_projections": 6,
+}
+ORDERS = {"o": "xyuw", "i": "yuxw", "s": "uxyw", "p": "yxuw", "t": "yxuw"}
+SCHEDULE = ("oi", "", "oi", "spi", "", "iptosip", "oistposi" + "tpotsop" + "tsptst")
 
 TIME_QKV_PARTS = ((0, 0, 192, 0, 0), (0, 192, 192, 0, 1), (1, 0, 192, 0, 2))
 TIME_PROJ_PARTS = ((1, 192, 192, 0, 0),)
@@ -127,14 +133,18 @@
     return jnp.where(allowed, 0.0, -1e30).astype(f32)
 
 
-def probs_of(key_pair, query_pair, mask, second):
-    scores = nt(masked(key_pair, second), query_pair) + mask
-    weights = jnp.exp(scores - jnp.max(scores, axis=0, keepdims=True))
-    return weights * (1.0 / jnp.sum(weights, axis=0, keepdims=True))
-
-
-def merged_rows(first, second):
-    return jnp.concatenate([first[:64], second[64:]], axis=0)
+def both_heads(pair):
+    return jnp.concatenate([masked(pair, False), masked(pair, True)], axis=0)
+
+
+def probs_of(keys, query_pair, mask):
+    scores = nt(keys, query_pair).reshape(2, HALF, HALF) + mask[None]
+    weights = jnp.exp(scores - jnp.max(scores, axis=1, keepdims=True))
+    return weights * (1.0 / jnp.sum(weights, axis=1, keepdims=True))
+
+
+def flat_heads(values):
+    return values.astype(bf16).reshape(2 * HALF, HALF)
 
 
 def attend(qkv_ref, mask, out_ref):
@@ -145,39 +155,42 @@
             query = qkv_ref[rows, pl.ds(column, 128)] * bf16(HEAD_DIM**-0.5)
             key_part = qkv_ref[rows, pl.ds(D + column, 128)]
             value_part = qkv_ref[rows, pl.ds(2 * D + column, 128)]
-            mixed = [
-                tn(value_part, probs_of(key_part, query, mask, second).astype(bf16))
-                for second in (False, True)
-            ]
-            out_ref[rows, pl.ds(column, 128)] = merged_rows(*mixed).T.astype(bf16)
+            mixed = []
+            for second in (False, True):
+                scores = nt(masked(key_part, second), query) + mask
+                weights = jnp.exp(scores - jnp.max(scores, axis=0, keepdims=True))
+                probs = weights * (1.0 / jnp.sum(weights, axis=0, keepdims=True))
+                mixed.append(tn(value_part, probs.astype(bf16)))
+            mixed = jnp.concatenate([mixed[0][:64], mixed[1][64:]], axis=0)
+            out_ref[rows, pl.ds(column, 128)] = mixed.T.astype(bf16)
         return carry
 
     lax.fori_loop(0, HEADS // 2, pair_step, 0)
 
 
 def attend_back(qkv_ref, mask, grad_ref, out_ref):
+    first = lane_half(False)
+
     def pair_step(pair, carry):
         column = pl.multiple_of(pair * 128, 128)
         for part in range(2):
             rows = pl.ds(part * HALF, HALF)
             query = qkv_ref[rows, pl.ds(column, 128)] * bf16(HEAD_DIM**-0.5)
-            key_part = qkv_ref[rows, pl.ds(D + column, 128)]
-            value_part = qkv_ref[rows, pl.ds(2 * D + column, 128)]
+            keys = both_heads(qkv_ref[rows, pl.ds(D + column, 128)])
+            values = both_heads(qkv_ref[rows, pl.ds(2 * D + column, 128)])
             grad = grad_ref[rows, pl.ds(column, 128)]
-            grads = ([], [], [])
-            for second in (False, True):
-                probs = probs_of(key_part, query, mask, second)
-                grad_probs = nt(masked(value_part, second), grad)
-                centre = jnp.sum(grad_probs * probs, axis=0, keepdims=True)
-                grad_scores = (probs * (grad_probs - centre)).astype(bf16)
-                grads[0].append(tn(key_part, grad_scores))
-                grads[1].append(nn(grad_scores, query))
-                grads[2].append(nn(probs.astype(bf16), grad))
-            grad_query = merged_rows(*grads[0]).T * HEAD_DIM**-0.5
+            probs = probs_of(keys, query, mask)
+            grad_probs = nt(values, grad).reshape(2, HALF, HALF)
+            centre = jnp.sum(grad_probs * probs, axis=1, keepdims=True)
+            grad_scores = flat_heads(probs * (grad_probs - centre))
+            grad_query = tn(keys, grad_scores).T * HEAD_DIM**-0.5
             out_ref[rows, pl.ds(column, 128)] = grad_query.astype(bf16)
-            first = lane_half(False)
-            out_ref[rows, pl.ds(D + column, 128)] = jnp.where(first, *grads[1]).astype(bf16)
-            out_ref[rows, pl.ds(2 * D + column, 128)] = jnp.where(first, *grads[2]).astype(bf16)
+            grad_key = nn(grad_scores, query)
+            grad_key = jnp.where(first, grad_key[:HALF], grad_key[HALF:])
+            out_ref[rows, pl.ds(D + column, 128)] = grad_key.astype(bf16)
+            grad_value = nn(flat_heads(probs), grad)
+            grad_value = jnp.where(first, grad_value[:HALF], grad_value[HALF:])
+            out_ref[rows, pl.ds(2 * D + column, 128)] = grad_value.astype(bf16)
         return carry
 
     lax.fori_loop(0, HEADS // 2, pair_step, 0)
@@ -351,18 +364,14 @@
     sums[5:8, :] = jnp.zeros((3, D), f32)
 
 
-def time_back_kernel(scalars, vec, tokens, qkv, r0, r1, r2, r3, *refs):
-    own_fc, own_proj, own_qkv, packed, *pieces = refs[:12]
+def time_projections_kernel(scalars, r0, r1, r2, r3, *refs):
+    own_fc, own_proj, packed, *pieces = refs[:11]
+    dt1, do1, da1, sums, w_fc, w_proj, sem_a, sem_b = refs[11:]
     fc_pieces, pieces = [packed] + pieces[:4], [packed] + pieces[4:]
-    (
-        dqkv, dt1, do1, sums, s0, s1, s2, s3, w_fc, w_proj, w_qkv, da, sem_a, sem_b, sem_c,
-    ) = refs[12:]
     fc_copy = Weights(scalars, own_fc, fc_pieces, TIME_FC_PARTS, SPACE_CHUNK, w_fc, sem_a)
     proj_copy = Weights(scalars, own_proj, pieces, TIME_PROJ_PARTS, TIME_CHUNK, w_proj, sem_b)
-    qkv_copy = Weights(scalars, own_qkv, pieces, TIME_QKV_PARTS, TIME_CHUNK, w_qkv, sem_c)
     fc_copy.start()
     proj_copy.start()
-    qkv_copy.start()
     branch = sum(
         tn(place_to_send(source), ref[...]) for source, ref in enumerate((r0, r1, r2, r3))
     ).astype(bf16)
@@ -371,8 +380,17 @@
     projected = nt(branch, w_fc[...]).astype(bf16)
     do1[...] = projected
     proj_copy.wait()
-    da[...] = nt(projected, w_proj[...]).astype(bf16)
-    attend_back(qkv, key_mask(True), da, dqkv)
+    da1[...] = nt(projected, w_proj[...]).astype(bf16)
+    sums[0:1, :] = column_sum(projected)
+    sums[1:2, :] = column_sum(branch)
+    sums[2:8, :] = jnp.zeros((6, D), f32)
+
+
+def time_back_kernel(scalars, vec, tokens, qkv, da1, early_sums, own_qkv, *refs):
+    pieces, (dqkv, sums, s0, s1, s2, s3, w_qkv, sem) = refs[:5], refs[5:]
+    qkv_copy = Weights(scalars, own_qkv, pieces, TIME_QKV_PARTS, TIME_CHUNK, w_qkv, sem)
+    qkv_copy.start()
+    attend_back(qkv, key_mask(True), da1, dqkv)
     qkv_copy.wait()
     back = nt(dqkv[...], w_qkv[...])
     grad, gain_grad, shift_grad = norm_back(
@@ -383,15 +401,14 @@
         ref[...] = nn(place_to_send(dest), rounded).astype(bf16)
     sums[0:1, :] = gain_grad
     sums[1:2, :] = shift_grad
-    sums[2:3, :] = column_sum(projected)
-    sums[3:4, :] = column_sum(branch)
+    sums[2:4, :] = early_sums[0:2, :]
     sums[4:5, :] = column_sum(dqkv[:, :D])
     sums[5:6, :] = column_sum(dqkv[:, 2 * D :])
     sums[6:8, :] = jnp.zeros((2, D), f32)
 
 
 def weight_grad_kernel(scalars, *refs, count, tables):
-    inputs, (kept, sent) = refs[:-2], refs[-2:]
+    inputs, (kept, sent, turned, ordered) = refs[:-4], refs[-4:]
     core = scalars[0] % 2
 
     def store(shard, rows, columns, values):
@@ -406,13 +423,32 @@
     at = 0
     for index in range(count):
         left, right = inputs[2 * index : 2 * index + 2]
-        shard_rows = left.shape[1] // 4
+        width = left.shape[1]
+        shard_rows = width // 4
+        if shard_rows % 128 == 0:
+            for spot in range(4):
+                shard = 2 * (spot % 2) + (core if spot < 2 else 1 - core)
+                source = pl.ds(pl.multiple_of(shard * shard_rows, shard_rows), shard_rows)
+                target = kept if spot < 2 else sent
+                for block in range(right.shape[1] // D):
+                    total = tn(left[:, source], right[:, block * D : (block + 1) * D])
+                    rows = slice(at + block * shard_rows, at + (block + 1) * shard_rows)
+                    target[spot % 2, rows, :] = total.astype(bf16)
+            at += shard_rows * (right.shape[1] // D)
+            continue
+        turned[0:width, :] = left[...].T
+        for spot in range(4):
+            shard = 2 * (spot % 2) + (core if spot < 2 else 1 - core)
+            source = pl.ds(pl.multiple_of(shard * shard_rows, shard_rows), shard_rows)
+            ordered[spot * shard_rows : (spot + 1) * shard_rows, :] = turned[source, :]
         for block in range(right.shape[1] // D):
             columns = slice(block * D, (block + 1) * D)
-            total = tn(left[...], right[:, columns]).astype(bf16)
-            for shard in range(4):
-                values = total[shard * shard_rows : (shard + 1) * shard_rows, :]
-                store(shard, slice(at, at + shard_rows), slice(0, D), values)
+            total = nn(ordered[...], right[:, columns]).astype(bf16)
+            for spot in range(4):
+                target = kept if spot < 2 else sent
+                target[spot % 2, at : at + shard_rows, :] = total[
+                    spot * shard_rows : (spot + 1) * shard_rows, :
+                ]
             at += shard_rows
     if tables:
         time, space, mlp = (ref[...] for ref in inputs[2 * count :])
@@ -444,10 +480,10 @@
 
 VMEM = pl.BlockSpec(memory_space=pltpu.MemorySpace.VMEM)
 SMEM = pl.BlockSpec(memory_space=pltpu.MemorySpace.SMEM)
-ANY = pl.BlockSpec(memory_space=pl.ANY)
-
-
-def call(kernel, name, outs, specs, scratch, operands, microseconds, limit=48):
+ANY = pl.BlockSpec(memory_space=pltpu.MemorySpace.HBM)
+
+
+def call(kernel, name, outs, specs, scratch, operands, microseconds):
     return pl.pallas_call(
         kernel,
         name=name,
@@ -455,7 +491,7 @@
         in_specs=specs,
         out_specs=[VMEM] * len(outs),
         scratch_shapes=scratch,
-        compiler_params=pltpu.CompilerParams(vmem_limit_bytes=limit << 20),
+        compiler_params=pltpu.CompilerParams(vmem_limit_bytes=LIMITS.get(name, 5) << 20),
         cost_estimate=pl.CostEstimate(
             flops=int(microseconds * 1.1e9), transcendentals=0, bytes_accessed=1 << 20
         ),
@@ -501,7 +537,7 @@
     return call(
         mlp_kernel, "mlp_both", outs, [SMEM, SMEM] + [VMEM] * 4 + [ANY] * 11,
         [vmem(D, FF), vmem(FF, D), dma_sems(MLP_IN_PARTS), dma_sems(MLP_OUT_PARTS)],
-        (scalars, live, vec, x2, h3, out_grad, *owns, *in_pieces, *out_pieces[1:]), 18, 56,
+        (scalars, live, vec, x2, h3, out_grad, *owns, *in_pieces, *out_pieces[1:]), 18,
     )
 
 
@@ -518,16 +554,21 @@
     )
 
 
-def time_back(scalars, vec, tokens, qkv, received, owns, fc_pieces, pieces):
-    outs = [shape(ROWS, 3 * D, bf16), shape(ROWS, D, bf16), shape(ROWS, D, bf16)]
-    outs += [shape(8, D, f32)] + [shape(CHUNK, D, bf16)] * 4
+def time_projections(scalars, received, owns, fc_pieces, pieces):
+    outs = [shape(ROWS, D, bf16)] * 3 + [shape(8, D, f32)]
     return call(
-        time_back_kernel, "time_back", outs, [SMEM] + [VMEM] * 7 + [ANY] * 12,
-        [
-            vmem(D, D), vmem(D, D), vmem(D, 3 * D), vmem(ROWS, D),
-            dma_sems(TIME_FC_PARTS), dma_sems(TIME_PROJ_PARTS), dma_sems(TIME_QKV_PARTS),
-        ],
-        (scalars, vec, tokens, qkv, *received, *owns, *fc_pieces, *pieces[1:]), 21,
+        time_projections_kernel, "time_projections", outs, [SMEM] + [VMEM] * 4 + [ANY] * 11,
+        [vmem(D, D), vmem(D, D), dma_sems(TIME_FC_PARTS), dma_sems(TIME_PROJ_PARTS)],
+        (scalars, *received, *owns, *fc_pieces, *pieces[1:]), 4,
+    )
+
+
+def time_back(scalars, vec, tokens, qkv, da1, early_sums, own, pieces):
+    outs = [shape(ROWS, 3 * D, bf16), shape(8, D, f32)] + [shape(CHUNK, D, bf16)] * 4
+    return call(
+        time_back_kernel, "time_back", outs, [SMEM] + [VMEM] * 5 + [ANY] * 6,
+        [vmem(D, 3 * D), dma_sems(TIME_QKV_PARTS)],
+        (scalars, vec, tokens, qkv, da1, early_sums, own, *pieces), 16,
     )
 
 
@@ -538,8 +579,143 @@
     kernel = functools.partial(weight_grad_kernel, count=len(groups), tables=len(tables))
     return call(
         kernel, name, [jax.ShapeDtypeStruct((2, rows, D), bf16)] * 2, [SMEM] + [VMEM] * len(flat),
-        [], (scalars, *flat), rows / 128,
-    )
+        [vmem(D, ROWS)] * 2, (scalars, *flat), rows / 150,
+    )
+
+
+def copy_all(copies):
+    for copy in copies:
+        copy.start()
+    for copy in copies:
+        copy.wait()
+
+
+def columns_of(ref, at):
+    return ref.at[:, pl.ds(pl.multiple_of(at * D, D), D)]
+
+
+def pack_time_kernel(scalars, time_qkv, time_proj, vectors, out, sems):
+    first, second = out.at[pl.ds(0, BLOCK), :], out.at[pl.ds(BLOCK, BLOCK), :]
+    tail = pltpu.make_async_copy(vectors, out.at[pl.ds(2 * BLOCK, 8), :], sems.at[2])
+    tail.start()
+
+    @pl.when(scalars[1] == 0)
+    def _():
+        pltpu.make_async_copy(columns_of(time_qkv, 0), first, sems.at[0]).start()
+        pltpu.make_async_copy(columns_of(time_qkv, 1), second, sems.at[1]).start()
+
+    @pl.when(scalars[1] != 0)
+    def _():
+        pltpu.make_async_copy(columns_of(time_qkv, 2), first, sems.at[0]).start()
+        pltpu.make_async_copy(time_proj, second, sems.at[1]).start()
+
+    pltpu.make_async_copy(time_proj, first, sems.at[0]).wait()
+    pltpu.make_async_copy(time_proj, second, sems.at[1]).wait()
+    tail.wait()
+
+
+def pack_rest_kernel(
+    scalars, time_qkv, time_proj, time_fc, space_qkv, space_proj, mlp_in, mlp_out, vectors,
+    packed, space_half, in_half, out_half, sems,
+):
+    half = scalars[1]
+    copies = []
+
+    def add(source, target, row, rows):
+        target = target.at[pl.ds(row, rows), :]
+        copies.append(pltpu.make_async_copy(source, target, sems.at[len(copies)]))
+
+    halves = pl.ds(pl.multiple_of(half * 2 * BLOCK, 2 * BLOCK), 2 * BLOCK)
+    add(columns_of(mlp_in, 2 * half), in_half, 0, BLOCK)
+    add(columns_of(mlp_in, 2 * half + 1), in_half, BLOCK, BLOCK)
+    add(mlp_out.at[halves, :], out_half, 0, 2 * BLOCK)
+    blocks = [columns_of(time_qkv, at) for at in range(3)] + [time_proj]
+    blocks += [columns_of(space_qkv, 0), columns_of(space_qkv, 1), time_fc]
+    blocks += [columns_of(space_qkv, 2), space_proj]
+    blocks += [columns_of(mlp_in, at) for at in range(4)]
+    for at, source in enumerate(blocks):
+        add(source, packed, at * BLOCK, BLOCK)
+    add(mlp_out, packed, 13 * BLOCK, 4 * BLOCK)
+    add(vectors, packed, VECTOR_AT, 8)
+    at = len(copies)
+    middle = BLOCK // 2
+
+    def space(source, row, rows, sem):
+        return pltpu.make_async_copy(source, space_half.at[pl.ds(row, rows), :], sems.at[sem])
+
+    @pl.when(half == 0)
+    def _():
+        space(columns_of(space_qkv, 0), 0, BLOCK, at).start()
+        space(columns_of(space_qkv, 1), BLOCK, BLOCK, at + 1).start()
+        space(time_fc.at[pl.ds(0, middle), :], 2 * BLOCK, middle, at + 2).start()
+
+    @pl.when(half != 0)
+    def _():
+        space(time_fc.at[pl.ds(middle, middle), :], 0, middle, at + 2).start()
+        space(columns_of(space_qkv, 2), middle, BLOCK, at).start()
+        space(space_proj, BLOCK + middle, BLOCK, at + 1).start()
+
+    copy_all(copies)
+    space(space_proj, 0, BLOCK, at).wait()
+    space(space_proj, BLOCK, BLOCK, at + 1).wait()
+    space(time_fc.at[pl.ds(0, middle), :], 2 * BLOCK, middle, at + 2).wait()
+
+
+def pack_time(*operands):
+    return pl.pallas_call(
+        pack_time_kernel, name="pack_time",
+        compiler_params=pltpu.CompilerParams(vmem_limit_bytes=LIMITS.get("pack_time", 5) << 20), out_shape=shape(392, D, bf16),
+        in_specs=[SMEM, ANY, ANY, ANY], out_specs=VMEM,
+        scratch_shapes=[pltpu.SemaphoreType.DMA((3,))],
+        cost_estimate=pl.CostEstimate(flops=10**9, transcendentals=0, bytes_accessed=1 << 20),
+    )(*operands)
+
+
+def pack_rest(*operands):
+    return pl.pallas_call(
+        pack_rest_kernel, name="pack_rest",
+        compiler_params=pltpu.CompilerParams(vmem_limit_bytes=LIMITS.get("pack_rest", 5) << 20),
+        out_shape=[
+            shape(VECTOR_AT + 8, D, bf16), shape(480, D, bf16), shape(384, D, bf16),
+            shape(384, D, bf16),
+        ],
+        in_specs=[SMEM] + [ANY] * 8, out_specs=[VMEM] * 4,
+        scratch_shapes=[pltpu.SemaphoreType.DMA((21,))],
+        cost_estimate=pl.CostEstimate(flops=3 * 10**9, transcendentals=0, bytes_accessed=1 << 20),
+    )(*operands)
+
+
+def unpack_kernel(scalars, mine, other, *outs, bit, parts):
+    own_first = (scalars[2] // bit) % 2 == 0
+    for half, row, rows, index, out_row, column in parts:
+        rows = pl.ds(row, rows)
+        near, far = mine[rows, :], other[rows, :]
+        pair = (near, far) if half == 0 else (far, near)
+        outs[index][out_row : out_row + rows.size, column * D : (column + 1) * D] = jnp.where(
+            own_first, *pair
+        ).astype(f32)
+
+
+def unpack(scalars, mine, other, bit, parts, outs):
+    kernel = functools.partial(unpack_kernel, bit=bit, parts=parts)
+    return call(
+        kernel, "unpack", [shape(*out, f32) for out in outs], [SMEM, VMEM, VMEM], [],
+        (scalars, mine, other), 2,
+    )
+
+
+OUT_PARTS = ((0, 0, 384, 0, 0, 0), (1, 0, 384, 0, 384, 0))
+IN_PARTS = (
+    (0, 0, 192, 0, 0, 0), (0, 192, 192, 0, 0, 1), (1, 0, 192, 0, 0, 2), (1, 192, 192, 0, 0, 3),
+)
+SPACE_PARTS = (
+    (0, 0, 192, 0, 0, 0), (0, 192, 192, 0, 0, 1), (1, 0, 192, 0, 0, 2), (1, 192, 192, 1, 0, 0),
+)
+SMALL_PARTS = ((0, 0, 192, 0, 0, 0), (1, 0, 192, 1, 0, 0))
+TIME_PARTS = (
+    (0, 0, 192, 0, 0, 0), (0, 192, 128, 0, 0, 1), (1, 0, 64, 0, 128, 1), (1, 64, 192, 0, 0, 2),
+    (1, 256, 16, 1, 0, 0),
+)
 
 
 def last_sum(scalars, e1, received):
@@ -569,54 +745,123 @@
     return lax.dynamic_slice_in_dim(own, half_at * (own.shape[0] // 2), own.shape[0] // 2, 0)
 
 
+def step_rows(rows):
+    return next(step for step in (96, 80, 48, 16) if rows % step == 0)
+
+
+def sum_split_kernel(scalars, kept, got, keep, send, *, bit):
+    rows = keep.shape[-2]
+    step = step_rows(rows)
+    if bit == 0:
+        mine = scalars[0] // 2
+    else:
+        mine = (scalars[2] // bit) % 2
+    for target, at in ((keep, mine), (send, 1 - mine)):
+
+        def body(index, carry, target=target, at=at):
+            row = pl.multiple_of(index * step, 16)
+            if bit == 0:
+                total = kept[at, pl.ds(row, step), :].astype(f32)
+                total = total + got[at, pl.ds(row, step), :].astype(f32)
+                target[pl.ds(row, step), :] = total.astype(bf16)
+            else:
+                source = pl.ds(pl.multiple_of(at * rows + row, 16), step)
+                for chip in range(2) if len(keep.shape) == 3 else [None]:
+                    here = (source, slice(None)) if chip is None else (chip, source, slice(None))
+                    there = (pl.ds(row, step), slice(None))
+                    there = there if chip is None else (chip,) + there
+                    total = kept[here].astype(f32) + got[here].astype(f32)
+                    target[there] = total.astype(bf16)
+            return carry
+
+        lax.fori_loop(0, rows // step, body, 0)
+
+
+def sum_split(scalars, kept, got, bit):
+    dims = kept.shape
+    out = dims[1:] if bit == 0 else dims[:-2] + (dims[-2] // 2, D)
+    kernel = functools.partial(sum_split_kernel, bit=bit)
+    outs = [jax.ShapeDtypeStruct(out, bf16)] * 2
+    return call(kernel, "sum_split", outs, [SMEM, VMEM, VMEM], [], (scalars, kept, got), 1.5)
+
+
+def join_kernel(scalars, mine, other, out, *, bit):
+    rows = mine.shape[0]
+    at = (scalars[2] // bit) % 2
+    out[pl.ds(pl.multiple_of(at * rows, 16), rows), :] = mine[...]
+    out[pl.ds(pl.multiple_of((1 - at) * rows, 16), rows), :] = other[...]
+
+
+def join(scalars, mine, other, bit):
+    kernel = functools.partial(join_kernel, bit=bit)
+    outs = [shape(2 * mine.shape[0], D, bf16)]
+    return call(kernel, "join", outs, [SMEM, VMEM, VMEM], [], (scalars, mine, other), 1)[0]
+
+
 class Reduce:
-    def __init__(self, parts, order, group_at, replica_at, ring_size):
+    def __init__(self, parts, order, scalars, replica_at, ring_size):
         self.kept, sent = parts
-        self.group_at, self.replica_at = group_at, replica_at
-        self.ring_size = ring_size
-        self.steps = [("sum", -1)] + [("sum", bit) for bit in order]
+        self.scalars, self.replica_at, self.ring_size = scalars, replica_at, ring_size
+        self.steps = [("sum", bit) for bit in order]
         self.steps += [("gather", bit) for bit in reversed(order) if bit]
         self.flying = flip(sent, "group", 1, 4)
-
-    def place(self, bit):
-        return (self.replica_at // bit) % 2
-
-    def start(self, *others):
-        kind, bit = self.steps[0]
-        if kind == "gather":
+        self.halve = lambda array: array
+
+    def split(self, bit):
+        if bit == 0:
+            chip = self.scalars[0] // 2
+            return (lambda a: pick(a, chip)), (lambda a: pick(a, 1 - chip))
+        mine = (self.replica_at // bit) % 2
+
+        def half(at):
+            def take(array):
+                rows = array.shape[-2] // 2
+                return lax.dynamic_slice_in_dim(array, at * rows, rows, array.ndim - 2)
+
+            return take
+
+        return half(mine), half(1 - mine)
+
+    def flip(self, array, bit):
+        axis = ("group", 2, 4) if bit == 0 else ("replica", bit, self.ring_size)
+        return flip(array, *axis)
+
+    def advance(self, *others):
+        got = after(self.flying, *others) if others else self.flying
+        if self.kept is not None:
+            if self.steps[0][0] == "sum":
+                bit = self.steps.pop(0)[1]
+                if self.kept.shape[-2] % 32 == 0:
+                    self.kept, sent = sum_split(self.scalars, self.kept, got, bit)
+                else:
+                    keep, send = self.split(bit)
+                    sent = add_rounded(send(self.kept), send(got))
+                    self.kept = add_rounded(keep(self.kept), keep(got))
+            else:
+                sent = self.current = add_rounded(self.kept, got)
+                self.kept = None
+                bit = self.steps[0][1]
+        else:
+            bit = self.steps.pop(0)[1]
+            mine = (self.replica_at // bit) % 2
+            if not self.steps:
+                self.got, self.bit = got, bit
+                return got
+            if got.shape[0] % 16 == 0:
+                self.current = join(self.scalars, self.current, got, bit)
+            else:
+                self.current = jnp.where(
+                    mine == 0,
+                    jnp.concatenate([self.current, got], 0),
+                    jnp.concatenate([got, self.current], 0),
+                )
             sent = self.current
-        elif bit == 0:
-            chip = self.group_at // 2
-            sent, self.kept = pick(self.current, 1 - chip), pick(self.current, chip)
-        else:
-            rows = self.current.shape[-2] // 2
-            mine = self.place(bit)
-            sent = lax.dynamic_slice_in_dim(self.current, (1 - mine) * rows, rows, -2 % self.current.ndim)
-            self.kept = lax.dynamic_slice_in_dim(self.current, mine * rows, rows, -2 % self.current.ndim)
-        if others:
-            sent = after(sent, *others)
-        axis = ("group", 2, 4) if bit == 0 else ("replica", bit, self.ring_size)
-        self.flying = flip(sent, *axis)
-
-    def finish(self, *others):
-        kind, bit = self.steps.pop(0)
-        got = after(self.flying, *others) if others else self.flying
-        if kind == "sum":
-            self.current = add_rounded(self.kept, got)
-        else:
-            mine = self.place(bit)
-            self.current = jnp.where(
-                mine == 0,
-                jnp.concatenate([self.current, got], 0),
-                jnp.concatenate([got, self.current], 0),
-            )
-        return self.current
-
-    def advance(self, *others):
-        result = self.finish(*others)
-        if self.steps:
-            self.start()
-        return result
+            bit = self.steps[0][1]
+        self.flying = self.flip(sent, bit)
+        return sent
+
+    def unpacked(self, parts, outs):
+        return unpack(self.scalars, self.current, self.got, self.bit, parts, outs)
 
 
 def block(array, at):
@@ -644,7 +889,7 @@
         group_at = lax.axis_index("group")
         replica_at = lax.axis_index("replica")
         half_at = replica_at % 2
-        scalars = jnp.stack([group_at, half_at]).astype(jnp.int32)
+        scalars = jnp.stack([group_at, half_at, replica_at]).astype(jnp.int32)
         live = slot_mask.astype(f32).reshape(1, 1)
         vectors = [
             time_norm_gain, time_norm_shift, time_proj_bias, time_fc_bias, space_norm_gain,
@@ -654,38 +899,28 @@
         cross = functools.partial(flip, axis="group", bit=2, size=4)
         near = functools.partial(flip, axis="group", bit=1, size=4)
         relay = functools.partial(flip, axis="replica", bit=1, size=ring_size)
-        flat = jnp.pad(jnp.concatenate(vectors), (0, 8 * D - VECTOR_ROWS * BLOCK)).reshape(8, D)
-        time_half = jnp.where(
-            half_at == 0,
-            jnp.concatenate([block(time_qkv, 0), block(time_qkv, 1), flat]),
-            jnp.concatenate([block(time_qkv, 2), time_proj, flat]),
-        )
+        ends = [sum(v.shape[0] for v in vectors[: at + 1]) for at in range(len(vectors))]
+        flat = sum(jnp.pad(v, (at - v.shape[0], 8 * D - at)) for v, at in zip(vectors, ends))
+        flat = flat.reshape(8, D)
+        time_half = pack_time(scalars, time_qkv, time_proj, flat)
         time_direct = cross(time_half)
-        token_pieces = tokens[0].transpose(1, 0, 2).reshape(4, 49, 2, D)
+        token_pieces = after(tokens[0], time_half).transpose(1, 0, 2).reshape(4, 49, 2, D)
         got = exchange([pick(token_pieces, group_at ^ d) for d in range(4)])
         place_tokens = jnp.pad(jnp.concatenate(got, axis=1), ((0, 3), (0, 0), (0, 0)))
         place_tokens = place_tokens.reshape(ROWS, D)
 
-        packed = jnp.concatenate(
-            [
-                block(time_qkv, 0), block(time_qkv, 1), block(time_qkv, 2), time_proj,
-                block(space_qkv, 0), block(space_qkv, 1), time_fc, block(space_qkv, 2), space_proj,
-                block(mlp_in, 0), block(mlp_in, 1), block(mlp_in, 2), block(mlp_in, 3), mlp_out,
-                flat,
-            ]
-        )
-
-        def half_of(chunk):
-            first, rows = chunk
-            return lax.dynamic_slice_in_dim(packed, first + half_at * (rows // 2), rows // 2, 0)
-
+        packed, space_half, in_half, out_half = pack_rest(
+            scalars, time_qkv, time_proj, time_fc, space_qkv, space_proj, mlp_in, mlp_out,
+            after(flat, got[1]),
+        )
         partner = near(packed)
+        time_direct, space_half = lax.optimization_barrier((time_direct, space_half))
         time_across = near(time_direct)
         time_relayed = relay(time_direct)
         time_pieces = (partner, time_direct, time_relayed, time_across, near(time_relayed))
-        space_direct = cross(after(half_of(SPACE_CHUNK), time_direct, got[2], got[3]))
-        in_direct = cross(after(half_of(IN_CHUNK), space_direct))
-        out_direct = cross(after(half_of(OUT_CHUNK), in_direct))
+        space_direct = cross(after(space_half, got[2], got[3]))
+        in_direct = cross(after(in_half, space_direct))
+        out_direct = cross(after(out_half, space_direct))
 
         held = [flat, partner[VECTOR_AT:], time_direct[384:], time_across[384:]]
         held = jnp.stack(held).reshape(4, 8 * D)[:, : VECTOR_ROWS * BLOCK]
@@ -714,81 +949,101 @@
             near(after(space_relayed, o1)),
         )
         x1, h2, qkv2, a2, x2, h3 = frame_forward(
-            scalars, after(frame_tokens, in_direct), vec, received,
+            scalars, after(frame_tokens, in_direct, out_direct), vec, received,
             (time_fc, space_qkv, space_proj), space_pieces,
         )
         in_relayed = relay(in_direct)
         in_pieces = (
             partner, in_direct, in_relayed, near(after(in_direct, x2)), near(after(in_relayed, x2)),
         )
-        out_direct = after(out_direct, x2)
         out_relayed = relay(out_direct)
-        out_pieces = (partner, out_direct, out_relayed, near(out_direct), near(out_relayed))
+        out_pieces = (
+            partner, out_direct, out_relayed, near(after(out_direct, x2)),
+            near(after(out_relayed, x2)),
+        )
         layer_out, act, du, dm, e2, sums3 = mlp_both(
             scalars, live, vec, x2, h3, frame_grad, (mlp_in, mlp_out), in_pieces, out_pieces
         )
         layer_out = layer_out.reshape(2, HALF, D)[None, :, :PLACES]
 
         chunk = functools.partial(
-            Reduce, group_at=group_at, replica_at=replica_at, ring_size=ring_size
+            Reduce, scalars=scalars, replica_at=replica_at, ring_size=ring_size
         )
         bits = [1 << at for at in range(ring_size.bit_length() - 1)]
         along = [0] + bits
-        first_y = bits[:1] + [0] + bits[1:]
-        first_z = bits[1:2] + [0] + bits[:1] + bits[2:]
-
-        way_out = chunk(weight_grads("mlp_out_grad", scalars, [(act, dm)]), along)
-        way_in = chunk(
-            weight_grads("mlp_in_grad", scalars, [(h3, after(du, way_out.kept))]), first_y
-        )
-        one = way_out.advance(way_in.kept)
-        two = way_in.advance(one)
+        names = {"x": 0, "y": bits[0], "u": bits[1], "w": bits[2]}
+
+        def way(parts, order):
+            return chunk(parts, [names[name] for name in order] + bits[3:])
+
+        ways = {}
+        last = ()
+
+        def advance(steps):
+            nonlocal last
+            for name in steps:
+                if ways[name].steps:
+                    last = (ways[name].advance(*last),)
+
+        ways["o"] = way(weight_grads("mlp_out_grad", scalars, [(act, dm)]), ORDERS["o"])
+        ways["i"] = way(
+            weight_grads("mlp_in_grad", scalars, [(h3, after(du, ways["o"].kept))]), ORDERS["i"]
+        )
+        last = (ways["i"].kept,)
+        advance(SCHEDULE[0])
         dqkv2, e1, dt2, sums2, *sends = space_back(
-            scalars, vec, after(e2, one, two), x1, qkv2, (space_proj, space_qkv), space_pieces
+            scalars, vec, after(e2, *last), x1, qkv2, (space_proj, space_qkv), space_pieces
         )
         received = exchange(sends)
-        one = way_out.advance(e1)
-        two = way_in.advance(one)
-        way_space = chunk(
-            weight_grads("space_grad", scalars, [(h2, after(dqkv2, two)), (a2, dt2)]), first_z
-        )
-        three = way_space.advance(two)
-        dqkv1, dt1, do1, sums1, *sends = time_back(
-            scalars, vec, after(place_tokens, three), qkv1, received,
-            (time_fc, time_proj, time_qkv), space_pieces, time_pieces,
+        last = (e1,)
+        advance(SCHEDULE[1])
+        ways["s"] = way(
+            weight_grads("space_grad", scalars, [(h2, after(dqkv2, *last)), (a2, dt2)]),
+            ORDERS["s"],
+        )
+        last = (ways["s"].kept,)
+        advance(SCHEDULE[2])
+        dt1, do1, da1, early = time_projections(
+            scalars, [after(received[0], *last)] + received[1:], (time_fc, time_proj),
+            space_pieces, time_pieces,
+        )
+        ways["p"] = way(
+            weight_grads("time_small_grad", scalars, [(a1, do1), (o1, dt1)]), ORDERS["p"]
+        )
+        last = (ways["p"].kept,)
+        advance(SCHEDULE[3])
+        dqkv1, sums1, *sends = time_back(
+            scalars, vec, place_tokens, qkv1, after(da1, *last), early, time_qkv, time_pieces
         )
         received = exchange(sends)
-        one = way_out.advance(dqkv1)
-        two = way_in.advance(one)
-        three = way_space.advance(two)
-        way_time = chunk(weight_grads("time_grad", scalars, [(h1, after(dqkv1, three))]), along)
-        way_small = chunk(
+        last = (dqkv1,)
+        advance(SCHEDULE[4])
+        ways["t"] = way(
             weight_grads(
-                "time_small_grad", scalars, [(a1, after(do1, way_time.kept)), (o1, dt1)],
-                (sums1, sums2, sums3),
+                "time_grad", scalars, [(h1, after(dqkv1, *last))], (sums1, sums2, sums3)
             ),
-            first_y,
-        )
-        last = way_time.advance(way_small.kept)
-        last = way_small.advance(last)
-        tokens_grad = last_sum(scalars, after(e1, last), received)
-        last = tokens_grad
+            ORDERS["t"],
+        )
+        last = (ways["t"].kept,)
+        advance(SCHEDULE[5])
+        tokens_grad = last_sum(scalars, after(e1, *last), received)
+        last = (tokens_grad,)
         tokens_grad = tokens_grad.reshape(2, HALF, D)[None, :, :PLACES]
-        ways = [way_out, way_in, way_space, way_time, way_small]
-        while any(way.steps for way in ways):
-            for way in ways:
-                if way.steps:
-                    last = way.advance(last)
-        sum_out, sum_in, sum_space, sum_time, sum_small = (way.current for way in ways)
-        vectors = sum_small[384:].astype(f32)
+        advance(SCHEDULE[6])
+        while any(each.steps for each in ways.values()):
+            advance([name for name in ways])
+        way_out, way_in, way_space, way_small, way_time = (ways[name] for name in "oispt")
+        (d_out,) = way_out.unpacked(OUT_PARTS, [(D, D)])
+        (d_in,) = way_in.unpacked(IN_PARTS, [(BLOCK, FF)])
+        d_space_qkv, d_space_proj = way_space.unpacked(SPACE_PARTS, [(BLOCK, 3 * D), (BLOCK, D)])
+        d_proj, d_fc = way_small.unpacked(SMALL_PARTS, [(BLOCK, D), (BLOCK, D)])
+        d_time_qkv, vectors = way_time.unpacked(TIME_PARTS, [(BLOCK, 3 * D), (16, D)])
         ones = vectors[:10, :BLOCK]
         return (
-            layer_out, tokens_grad, ones[0], ones[1], unpack_grad(sum_time, 3),
-            vectors[10, : D // 2], sum_small[:192].astype(f32), ones[2],
-            sum_small[192:384].astype(f32), ones[3],
-            ones[4], ones[5], unpack_grad(sum_space[:576], 3), vectors[11, : D // 2],
-            sum_space[576:768].astype(f32), ones[6], ones[7], ones[8], unpack_grad(sum_in, 4),
-            vectors[12], sum_out.astype(f32), ones[9],
+            layer_out, tokens_grad, ones[0], ones[1], d_time_qkv, vectors[10, : D // 2],
+            d_proj, ones[2], d_fc, ones[3], ones[4], ones[5], d_space_qkv,
+            vectors[11, : D // 2], d_space_proj, ones[6], ones[7], ones[8], d_in, vectors[12],
+            d_out, ones[9],
         )
 
     return on_device

time: 407 us -> 375 us (0.921)
  other arithmetic: 28.9 us -> 1.94 us
  local copies, waits for them, and re-layouts: 44.5 us -> 26.6 us
  waiting for transfers between devices: 150 us -> 159 us
  Pallas kernels: 110 us -> 116 us
  starting transfers between devices: 66.4 us -> 61.4 us
    convert_element_type x25 -> x5, other arithmetic: 19.9 us -> 0.17 us  [add_rounded(): return (left.astype(f32) + right.astype(f32)).astype(bf16)]
    ppermute x69, waiting for transfers between devices: 150 us -> 159 us  [flip(): return lax.ppermute(array, axis, [(at, at ^ bit) for at in range(size)])]
    unnamed x192 -> x86, local copies, waits for them, and re-layouts: 27.7 us -> 21.8 us
    dynamic_slice x17 -> x0, local copies, waits for them, and re-layouts: 5.83 us -> none  [the longest x2 3.49 us: half_of(): lax.dynamic_slice_in_dim(packed, first + half_at * (rows // 2), rows // 2...]
    ppermute x69, starting transfers between devices: 66.4 us -> 61.4 us  [flip(): return lax.ppermute(array, axis, [(at, at ^ bit) for at in range(size)])]
    pallas_call x11 -> x47, Pallas kernels: 110 us -> 113 us  [call(): pl.pallas_call(kernel, name=name, out_shape=outs, in_specs=specs, out_spe...]
  transfers between devices with their start and end apart: 69 -> 69, of which waited for: 29 -> 37; matrix products, arithmetic and copies ran while one was open for 11% -> 1% of each run, Pallas kernels for 19% -> 21%
where the time goes in v3:
time: 375 us; the launch traced here: 368 us
  waiting for transfers between devices  159 us (42%)
  Pallas kernels  116 us (31%)
  starting transfers between devices  61.4 us (16%)
  local copies, waits for them, and re-layouts  26.6 us (7%)
    ppermute x69, waiting for transfers between devices, flip(): return lax.ppermute(array, axis, [(at, at ^ bit) for at in range(size)])  159 us
    pallas_call x47, Pallas kernels, call(): pl.pallas_call(kernel, name=name, out_shape=outs, in_specs=specs, out_spe...  113 us
    ppermute x69, starting transfers between devices, flip(): return lax.ppermute(array, axis, [(at, at ^ bit) for at in range(size)])  61.4 us
    unnamed x86, local copies, waits for them, and re-layouts  21.8 us
  transfers between devices with their start and end apart: 69, of which 37 were waited for; matrix products, arithmetic and copies ran while one was open for 1% of the time, Pallas kernels for 21%

profile of v3, /device:TPU:0, one launch (start us, length us, event | category | flops | bytes accessed | tf_op | source)
XLA Modules:
  0.0 368.1 jit_solution(248353791768461018)
XLA Ops:
  19.6 12.7 %collective-permute-done.2.refs_3_.refs_7_.refs_1_ = bf16[392,768]{1,0:T(8,128)(2,1)S(1)} collective-permute-done((bf16[392,768]{1,0:T(8,128)(2,1)S(1)}, bf16[392,768]{1,0:T(8,128)(2,1)S(1)}, u32[]{:S(2)}, u32[]{:S(2)}) %collective-permute-start.2) | collective-permute-done | bytes 602144 | tf_op jit(solution)/shard_map/ppermute | solution.py:729
  42.5 12.5 %collective-permute-done.9.refs_4_.refs_8_.refs_2_ = bf16[392,768]{1,0:T(8,128)(2,1)} collective-permute-done((bf16[392,768]{1,0:T(8,128)(2,1)S(1)}, bf16[392,768]{1,0:T(8,128)(2,1)}, u32[]{:S(2)}, u32[]{:S(2)}) %collective-permute-start.9) | collective-permute-done | bytes 602144 | tf_op jit(solution)/shard_map/ppermute | solution.py:729
  68.4 10.1 %place_forward.1 = (bf16[416,768]{1,0:T(8,128)(2,1)S(1)}, bf16[416,2304]{1,0:T(8,128)(2,1)S(1)}, bf16[416,768]{1,0:T(8,128)(2,1)S(1)}, bf16[416,768]{1,0:T(8,128...) custom-call(s32[3]{0:T(128)S(1)} %pad_add_fusion.1.scalars, ...), custom_call_target="tpu_custom_call" | custom-call | flops 12099999744 | bytes 1048576 | tf_op jit(solution)/shard_map/place_forward/pallas_call | solution.py:487
  90.4 11.8 %frame_forward.1 = (f32[416,768]{1,0:T(8,128)S(1)}, bf16[416,768]{1,0:T(8,128)(2,1)S(1)}, bf16[416,2304]{1,0:T(8,128)(2,1)S(1)}, bf16[416,768]{1,0:T(8,128)(2,1)...) custom-call(s32[3]{0:T(128)S(1)} %pad_add_fusion.1.scalars, bf16[416,768]{1,0:T(8,128)(2,1)S(1)} %bitcast.54, ...), custom_call_target="tpu_custom_call" | custom-call | flops 14300000256 | bytes 1048576 | tf_op jit(solution)/shard_map/frame_forward/pallas_call | solution.py:487
  104.5 8.3 %collective-permute-done.20.refs_8_ = bf16[384,768]{1,0:T(8,128)(2,1)S(1)} collective-permute-done((bf16[384,768]{1,0:T(8,128)(2,1)}, bf16[384,768]{1,0:T(8,128)(2,1)S(1)}, u32[]{:S(2)}, u32[]{:S(2)}) %collective-permute-start.20) | collective-permute-done | bytes 589856 | tf_op jit(solution)/shard_map/ppermute | solution.py:729
  117.4 12.2 %mlp_both.1 = (bf16[416,768]{1,0:T(8,128)(2,1)S(1)}, bf16[416,3072]{1,0:T(8,128)(2,1)S(1)}, bf16[416,3072]{1,0:T(8,128)(2,1)S(1)}, bf16[416,768]{1,0:T(8,128)(2,...) custom-call(s32[3]{0:T(128)S(1)} %pad_add_fusion.1.scalars, f32[1,1]{1,0:T(1,128)} %bitcast.3.live, ...), custom_call_target="tpu_custom_call" | custom-call | flops 19800000512 | bytes 1048576 | tf_op jit(solution)/shard_map/mlp_both/pallas_call | solution.py:487
  133.2 3.5 mlp_in_grad.1
  144.8 13.5 %space_back.1 = (bf16[416,2304]{1,0:T(8,128)(2,1)S(1)}, f32[416,768]{1,0:T(8,128)S(1)}, bf16[416,768]{1,0:T(8,128)(2,1)S(1)}, f32[8,768]{1,0:T(8,128)S(1)}, bf16...) custom-call(s32[3]{0:T(128)S(1)} %pad_add_fusion.1.scalars, ...), custom_call_target="tpu_custom_call" | custom-call | flops 22000001024 | bytes 1048576 | tf_op jit(solution)/shard_map/space_back/pallas_call | solution.py:487
  163.6 4.0 %collective-permute-done.26.got = bf16[768,768]{1,0:T(8,128)(2,1)S(1)} collective-permute-done((bf16[768,768]{1,0:T(8,128)(2,1)S(1)}, bf16[768,768]{1,0:T(8,128)(2,1)S(1)}, u32[]{:S(2)}, u32[]{:S(2)}) %collective-permute-start.26) | collective-permute-done | bytes 1179680 | tf_op jit(solution)/shard_map/ppermute | solution.py:729
  173.8 4.6 %time_projections.1 = (bf16[416,768]{1,0:T(8,128)(2,1)S(1)}, bf16[416,768]{1,0:T(8,128)(2,1)S(1)}, bf16[416,768]{1,0:T(8,128)(2,1)S(1)}, f32[8,768]{1,0:T(8,128)S(1)}) custom-call(s32[3]{0:T(128)S(1)} %pad_add_fusion.1.scalars, bf16[104,768]{1,0:T(8,128)(2,1)S(1)} %get-tuple-element.237.r0, bf16[104,768]{1,0:T(8,128)(2,1)S(1)} %collective-permute-done.27.r1, ...), custom_call_target="tpu_custom_call" | custom-call | flops 4400000000 | bytes 1048576 | tf_op jit(solution)/shard_map/time_projections/pallas_call | solution.py:487
  184.3 12.0 %collective-permute-done.33.got = bf16[2,192,768]{2,1,0:T(8,128)(2,1)S(1)} collective-permute-done((bf16[2,192,768]{2,1,0:T(8,128)(2,1)S(1)}, bf16[2,192,768]{2,1,0:T(8,128)(2,1)S(1)}, u32[]{:S(2)}, u32[]{:S(2)}) %collective-permute-start.33) | collective-permute-done | bytes 589856 | tf_op jit(solution)/shard_map/ppermute | solution.py:729
  198.2 11.8 %time_back.1 = (bf16[416,2304]{1,0:T(8,128)(2,1)S(1)}, f32[8,768]{1,0:T(8,128)S(1)}, bf16[104,768]{1,0:T(8,128)(2,1)S(1)}, bf16[104,768]{1,0:T(8,128)(2,1)S(1)},...) custom-call(s32[3]{0:T(128)S(1)} %pad_add_fusion.1.scalars, f32[24,768]{1,0:T(8,128)S(1)} %concatenate.8.vec, ...), custom_call_target="tpu_custom_call" | custom-call | flops 17600000000 | bytes 1048576 | tf_op jit(solution)/shard_map/time_back/pallas_call | solution.py:487
  218.7 7.7 %collective-permute-done.34.got = bf16[192,768]{1,0:T(8,128)(2,1)S(1)} collective-permute-done((bf16[192,768]{1,0:T(8,128)(2,1)S(1)}, bf16[192,768]{1,0:T(8,128)(2,1)S(1)}, u32[]{:S(2)}, u32[]{:S(2)}) %collective-permute-start.34) | collective-permute-done | bytes 294944 | tf_op jit(solution)/shard_map/ppermute | solution.py:729
  227.1 4.7 %collective-permute-done.32.got = bf16[2,192,768]{2,1,0:T(8,128)(2,1)S(1)} collective-permute-done((bf16[2,192,768]{2,1,0:T(8,128)(2,1)S(1)}, bf16[2,192,768]{2,1,0:T(8,128)(2,1)S(1)}, u32[]{:S(2)}, u32[]{:S(2)}) %collective-permute-start.32) | collective-permute-done | bytes 589856 | tf_op jit(solution)/shard_map/ppermute | solution.py:729
  234.7 9.2 %collective-permute-done.38.got = bf16[384,768]{1,0:T(8,128)(2,1)S(1)} collective-permute-done((bf16[384,768]{1,0:T(8,128)(2,1)S(1)}, bf16[384,768]{1,0:T(8,128)(2,1)S(1)}, u32[]{:S(2)}, u32[]{:S(2)}) %collective-permute-start.38) | collective-permute-done | bytes 589856 | tf_op jit(solution)/shard_map/ppermute | solution.py:729
  249.3 4.0 %collective-permute-done.36 = bf16[96,768]{1,0:T(8,128)(2,1)S(1)} collective-permute-done((bf16[96,768]{1,0:T(8,128)(2,1)S(1)}, bf16[96,768]{1,0:T(8,128)(2,1)S(1)}, u32[]{:S(2)}, u32[]{:S(2)}) %collective-permute-start.36) | collective-permute-done | bytes 147488 | tf_op jit(solution)/shard_map/ppermute | solution.py:729
  261.2 7.7 %collective-permute-done.46.got = bf16[192,768]{1,0:T(8,128)(2,1)S(1)} collective-permute-done((bf16[192,768]{1,0:T(8,128)(2,1)S(1)}, bf16[192,768]{1,0:T(8,128)(2,1)S(1)}, u32[]{:S(2)}, u32[]{:S(2)}) %collective-permute-start.46) | collective-permute-done | bytes 294944 | tf_op jit(solution)/shard_map/ppermute | solution.py:729
  274.2 3.7 %collective-permute-done.43.got = bf16[2,320,768]{2,1,0:T(8,128)(2,1)S(1)} collective-permute-done((bf16[2,320,768]{2,1,0:T(8,128)(2,1)S(1)}, bf16[2,320,768]{2,1,0:T(8,128)(2,1)S(1)}, u32[]{:S(2)}, u32[]{:S(2)}) %collective-permute-start.43) | collective-permute-done | bytes 983072 | tf_op jit(solution)/shard_map/ppermute | solution.py:729
  284.9 5.2 %collective-permute-done.47.got = bf16[320,768]{1,0:T(8,128)(2,1)S(1)} collective-permute-done((bf16[320,768]{1,0:T(8,128)(2,1)S(1)}, bf16[320,768]{1,0:T(8,128)(2,1)S(1)}, u32[]{:S(2)}, u32[]{:S(2)}) %collective-permute-start.47) | collective-permute-done | bytes 491552 | tf_op jit(solution)/shard_map/ppermute | solution.py:729
  292.0 3.7 %collective-permute-done.53.other = bf16[96,768]{1,0:T(8,128)(2,1)S(1)} collective-permute-done((bf16[96,768]{1,0:T(8,128)(2,1)S(1)}, bf16[96,768]{1,0:T(8,128)(2,1)S(1)}, u32[]{:S(2)}, u32[]{:S(2)}) %collective-permute-start.53) | collective-permute-done | bytes 147488 | tf_op jit(solution)/shard_map/ppermute | solution.py:729
  296.3 8.0 %collective-permute-done.52.got = bf16[160,768]{1,0:T(8,128)(2,1)S(1)} collective-permute-done((bf16[160,768]{1,0:T(8,128)(2,1)S(1)}, bf16[160,768]{1,0:T(8,128)(2,1)S(1)}, u32[]{:S(2)}, u32[]{:S(2)}) %collective-permute-start.52) | collective-permute-done | bytes 245792 | tf_op jit(solution)/shard_map/ppermute | solution.py:729
  324.9 8.2 %collective-permute-done.63.other = bf16[192,768]{1,0:T(8,128)(2,1)S(1)} collective-permute-done((bf16[192,768]{1,0:T(8,128)(2,1)S(1)}, bf16[192,768]{1,0:T(8,128)(2,1)S(1)}, u32[]{:S(2)}, u32[]{:S(2)}) %collective-permute-start.63) | collective-permute-done | bytes 294944 | tf_op jit(solution)/shard_map/ppermute | solution.py:729
  341.6 4.1 %collective-permute-done.67.other = bf16[384,768]{1,0:T(8,128)(2,1)S(1)} collective-permute-done((bf16[384,768]{1,0:T(8,128)(2,1)S(1)}, bf16[384,768]{1,0:T(8,128)(2,1)S(1)}, u32[]{:S(2)}, u32[]{:S(2)}) %collective-permute-start.67) | collective-permute-done | bytes 589856 | tf_op jit(solution)/shard_map/ppermute | solution.py:729
  347.8 12.6 %collective-permute-done.65.other = bf16[192,768]{1,0:T(8,128)(2,1)S(1)} collective-permute-done((bf16[192,768]{1,0:T(8,128)(2,1)S(1)}, bf16[192,768]{1,0:T(8,128)(2,1)S(1)}, u32[]{:S(2)}, u32[]{:S(2)}) %collective-permute-start.65) | collective-permute-done | bytes 294944 | tf_op jit(solution)/shard_map/ppermute | solution.py:729
  (284 shorter events, 169.6 us)
Async XLA Ops:
  14.8 44.0 %collective-permute-start.1 = (bf16[3272,768]{1,0:T(8,128)(2,1)S(1)}, bf16[3272,768]{1,0:T(8,128)(2,1)S(1)}, u32[]{:S(2)}, u32[]{:S(2)}) collective-permute-start(bf16[3272,768]{1,0:T(8,128)(2,1)S(1)} %get-tuple-element.182), channel_id=1, source_target_pairs={{0,8},{8,0},{16,24},{24,16},{1,9},{9,1},{17,25},{25,17},{2,10},{10... | collective-permute-start | bytes 15077384 | tf_op jit(solution)/shard_map/ppermute | solution.py:729
  17.9 20.5 %collective-permute-start.4 = (bf16[49,2,768]{2,1,0:T(2,128)(2,1)S(1)}, bf16[49,2,768]{2,1,0:T(2,128)(2,1)S(1)}, u32[]{:S(2)}, u32[]{:S(2)}) collective-permute-start(bf16[49,2,768]{2,1,0:T(2,128)(2,1)S(1)} %get-tuple-element.346), channel_id=1, source_target_pairs={{0,16},{8,24},{16,0},{24,8},{1,17},{9,25},{17,1},{25,9},{2,18},{10... | collective-permute-start | bytes 451592 | tf_op jit(solution)/shard_map/ppermute | solution.py:729
  56.7 24.5 %collective-permute-start.7 = (bf16[384,768]{1,0:T(8,128)(2,1)}, bf16[384,768]{1,0:T(8,128)(2,1)}, u32[]{:S(2)}, u32[]{:S(2)}) collective-permute-start(bf16[384,768]{1,0:T(8,128)(2,1)} %get-tuple-element.188), channel_id=1, source_target_pairs={{0,16},{8,24},{16,0},{24,8},{1,17},{9,25},{17,1},{25,9},{2,18},{10... | collective-permute-start | bytes 1769480 | tf_op jit(solution)/shard_map/ppermute | solution.py:729
  58.2 25.6 %collective-permute-start.8 = (bf16[384,768]{1,0:T(8,128)(2,1)}, bf16[384,768]{1,0:T(8,128)(2,1)}, u32[]{:S(2)}, u32[]{:S(2)}) collective-permute-start(bf16[384,768]{1,0:T(8,128)(2,1)} %get-tuple-element.190), channel_id=1, source_target_pairs={{0,16},{8,24},{16,0},{24,8},{1,17},{9,25},{17,1},{25,9},{2,18},{10... | collective-permute-start | bytes 1769480 | tf_op jit(solution)/shard_map/ppermute | solution.py:729
  58.8 25.2 %collective-permute-start.15 = (bf16[480,768]{1,0:T(8,128)(2,1)}, bf16[480,768]{1,0:T(8,128)(2,1)}, u32[]{:S(2)}, u32[]{:S(2)}) collective-permute-start(bf16[480,768]{1,0:T(8,128)(2,1)} %collective-permute-done.6.refs_4_.refs_3_), channel_id=1, source_target_pairs={{0,8},{8,0},{16,24},{24,16},{1,9},{9,1},{17,25},{25,17},{2,10},{10... | collective-permute-start | bytes 2211848 | tf_op jit(solution)/shard_map/ppermute | solution.py:729
  58.8 21.8 %collective-permute-start.14 = (bf16[480,768]{1,0:T(8,128)(2,1)}, bf16[480,768]{1,0:T(8,128)(2,1)}, u32[]{:S(2)}, u32[]{:S(2)}) collective-permute-start(bf16[480,768]{1,0:T(8,128)(2,1)} %collective-permute-done.6.refs_4_.refs_3_), channel_id=1, source_target_pairs={{0,1},{1,0},{2,3},{3,2},{4,5},{5,4},{6,7},{7,6},{8,9},{9,8},{10,11... | collective-permute-start | bytes 2211848 | tf_op jit(solution)/shard_map/ppermute | solution.py:729
  84.0 28.9 %collective-permute-start.17 = (bf16[384,768]{1,0:T(8,128)(2,1)}, bf16[384,768]{1,0:T(8,128)(2,1)S(1)}, u32[]{:S(2)}, u32[]{:S(2)}) collective-permute-start(bf16[384,768]{1,0:T(8,128)(2,1)} %collective-permute-done.7.refs_3_), channel_id=1, source_target_pairs={{0,1},{1,0},{2,3},{3,2},{4,5},{5,4},{6,7},{7,6},{8,9},{9,8},{10,11... | collective-permute-start | bytes 1769480 | tf_op jit(solution)/shard_map/ppermute | solution.py:729
  86.3 26.6 %collective-permute-start.20 = (bf16[384,768]{1,0:T(8,128)(2,1)}, bf16[384,768]{1,0:T(8,128)(2,1)S(1)}, u32[]{:S(2)}, u32[]{:S(2)}) collective-permute-start(bf16[384,768]{1,0:T(8,128)(2,1)} %collective-permute-done.8.refs_7_), channel_id=1, source_target_pairs={{0,1},{1,0},{2,3},{3,2},{4,5},{5,4},{6,7},{7,6},{8,9},{9,8},{10,11... | collective-permute-start | bytes 1769480 | tf_op jit(solution)/shard_map/ppermute | solution.py:729
  138.7 28.9 %collective-permute-start.26 = (bf16[768,768]{1,0:T(8,128)(2,1)S(1)}, bf16[768,768]{1,0:T(8,128)(2,1)S(1)}, u32[]{:S(2)}, u32[]{:S(2)}) collective-permute-start(bf16[768,768]{1,0:T(8,128)(2,1)S(1)} %get-tuple-element.216), channel_id=1, source_target_pairs={{0,16},{8,24},{16,0},{24,8},{1,17},{9,25},{17,1},{25,9},{2,18},{10... | collective-permute-start | bytes 3538952 | tf_op jit(solution)/shard_map/ppermute | solution.py:729
  142.4 28.8 %collective-permute-start.25 = (bf16[2,384,768]{2,1,0:T(8,128)(2,1)S(1)}, bf16[2,384,768]{2,1,0:T(8,128)(2,1)S(1)}, u32[]{:S(2)}, u32[]{:S(2)}) collective-permute-start(bf16[2,384,768]{2,1,0:T(8,128)(2,1)S(1)} %get-tuple-element.218), channel_id=1, source_target_pairs={{0,1},{1,0},{2,3},{3,2},{4,5},{5,4},{6,7},{7,6},{8,9},{9,8},{10,11... | collective-permute-start | bytes 3538952 | tf_op jit(solution)/shard_map/ppermute | solution.py:729
  161.7 20.6 %collective-permute-start.31 = (bf16[2,768,768]{2,1,0:T(8,128)(2,1)S(1)}, bf16[2,768,768]{2,1,0:T(8,128)(2,1)S(1)}, u32[]{:S(2)}, u32[]{:S(2)}) collective-permute-start(bf16[2,768,768]{2,1,0:T(8,128)(2,1)S(1)} %get-tuple-element.245), channel_id=1, source_target_pairs={{0,8},{8,0},{16,24},{24,16},{1,9},{9,1},{17,25},{25,17},{2,10},{10... | collective-permute-start | bytes 7077896 | tf_op jit(solution)/shard_map/ppermute | solution.py:729
  213.4 33.8 %collective-permute-start.37 = (bf16[2,384,768]{2,1,0:T(8,128)(2,1)S(1)}, bf16[2,384,768]{2,1,0:T(8,128)(2,1)S(1)}, u32[]{:S(2)}, u32[]{:S(2)}) collective-permute-start(bf16[2,384,768]{2,1,0:T(8,128)(2,1)S(1)} %get-tuple-element.247), channel_id=1, source_target_pairs={{0,2},{1,3},{2,0},{3,1},{4,6},{5,7},{6,4},{7,5},{8,10},{9,11},{10,... | collective-permute-start | bytes 3538952 | tf_op jit(solution)/shard_map/ppermute | solution.py:729
  218.7 25.2 %collective-permute-start.38 = (bf16[384,768]{1,0:T(8,128)(2,1)S(1)}, bf16[384,768]{1,0:T(8,128)(2,1)S(1)}, u32[]{:S(2)}, u32[]{:S(2)}) collective-permute-start(bf16[384,768]{1,0:T(8,128)(2,1)S(1)} %get-tuple-element.234), channel_id=1, source_target_pairs={{0,1},{1,0},{2,3},{3,2},{4,5},{5,4},{6,7},{7,6},{8,9},{9,8},{10,11... | collective-permute-start | bytes 1769480 | tf_op jit(solution)/shard_map/ppermute | solution.py:729
  226.4 29.6 %collective-permute-start.40 = (bf16[104,768]{1,0:T(8,128)(2,1)S(1)}, bf16[104,768]{1,0:T(8,128)(2,1)S(1)}, u32[]{:S(2)}, u32[]{:S(2)}) collective-permute-start(bf16[104,768]{1,0:T(8,128)(2,1)S(1)} %get-tuple-element.285), channel_id=1, source_target_pairs={{0,8},{8,0},{16,24},{24,16},{1,9},{9,1},{17,25},{25,17},{2,10},{10... | collective-permute-start | bytes 479240 | tf_op jit(solution)/shard_map/ppermute | solution.py:729
  231.7 26.0 %collective-permute-start.41 = (bf16[104,768]{1,0:T(8,128)(2,1)S(1)}, bf16[104,768]{1,0:T(8,128)(2,1)S(1)}, u32[]{:S(2)}, u32[]{:S(2)}) collective-permute-start(bf16[104,768]{1,0:T(8,128)(2,1)S(1)} %get-tuple-element.286), channel_id=1, source_target_pairs={{0,16},{8,24},{16,0},{24,8},{1,17},{9,25},{17,1},{25,9},{2,18},{10... | collective-permute-start | bytes 479240 | tf_op jit(solution)/shard_map/ppermute | solution.py:729
  233.5 25.9 %collective-permute-start.42 = (bf16[104,768]{1,0:T(8,128)(2,1)S(1)}, bf16[104,768]{1,0:T(8,128)(2,1)S(1)}, u32[]{:S(2)}, u32[]{:S(2)}) collective-permute-start(bf16[104,768]{1,0:T(8,128)(2,1)S(1)} %get-tuple-element.287), channel_id=1, source_target_pairs={{0,24},{8,16},{16,8},{24,0},{1,25},{9,17},{17,9},{25,1},{2,26},{10... | collective-permute-start | bytes 479240 | tf_op jit(solution)/shard_map/ppermute | solution.py:729
  253.3 24.6 %collective-permute-start.43 = (bf16[2,320,768]{2,1,0:T(8,128)(2,1)S(1)}, bf16[2,320,768]{2,1,0:T(8,128)(2,1)S(1)}, u32[]{:S(2)}, u32[]{:S(2)}) collective-permute-start(bf16[2,320,768]{2,1,0:T(8,128)(2,1)S(1)} %get-tuple-element.275), channel_id=1, source_target_pairs={{0,1},{1,0},{2,3},{3,2},{4,5},{5,4},{6,7},{7,6},{8,9},{9,8},{10,11... | collective-permute-start | bytes 2949128 | tf_op jit(solution)/shard_map/ppermute | solution.py:729
  257.8 22.1 %collective-permute-start.51 = (bf16[96,768]{1,0:T(8,128)(2,1)S(1)}, bf16[96,768]{1,0:T(8,128)(2,1)S(1)}, u32[]{:S(2)}, u32[]{:S(2)}) collective-permute-start(bf16[96,768]{1,0:T(8,128)(2,1)S(1)} %get-tuple-element.282), channel_id=1, source_target_pairs={{0,2},{1,3},{2,0},{3,1},{4,6},{5,7},{6,4},{7,5},{8,10},{9,11},{10,... | collective-permute-start | bytes 442376 | tf_op jit(solution)/shard_map/ppermute | solution.py:729
  284.2 20.8 %collective-permute-start.58 = (bf16[96,768]{1,0:T(8,128)(2,1)S(1)}, bf16[96,768]{1,0:T(8,128)(2,1)S(1)}, u32[]{:S(2)}, u32[]{:S(2)}) collective-permute-start(bf16[96,768]{1,0:T(8,128)(2,1)S(1)} %get-tuple-element.306), channel_id=1, source_target_pairs={{0,4},{1,5},{2,6},{3,7},{4,0},{5,1},{6,2},{7,3},{8,12},{9,13},{10,... | collective-permute-start | bytes 442376 | tf_op jit(solution)/shard_map/ppermute | solution.py:729
  291.0 21.0 %collective-permute-start.56 = (bf16[48,768]{1,0:T(8,128)(2,1)S(1)}, bf16[48,768]{1,0:T(8,128)(2,1)S(1)}, u32[]{:S(2)}, u32[]{:S(2)}) collective-permute-start(bf16[48,768]{1,0:T(8,128)(2,1)S(1)} %add_convert_fusion.4.mine), channel_id=1, source_target_pairs={{0,4},{1,5},{2,6},{3,7},{4,0},{5,1},{6,2},{7,3},{8,12},{9,13},{10,... | collective-permute-start | bytes 221192 | tf_op jit(solution)/shard_map/ppermute | solution.py:729
  310.4 29.1 %collective-permute-start.68 = (bf16[384,768]{1,0:T(8,128)(2,1)S(1)}, bf16[384,768]{1,0:T(8,128)(2,1)S(1)}, u32[]{:S(2)}, u32[]{:S(2)}) collective-permute-start(bf16[384,768]{1,0:T(8,128)(2,1)S(1)} %join.13.mine), channel_id=1, source_target_pairs={{0,1},{1,0},{2,3},{3,2},{4,5},{5,4},{6,7},{7,6},{8,9},{9,8},{10,11... | collective-permute-start | bytes 1769480 | tf_op jit(solution)/shard_map/ppermute | solution.py:729
  323.7 22.0 %collective-permute-start.67 = (bf16[384,768]{1,0:T(8,128)(2,1)S(1)}, bf16[384,768]{1,0:T(8,128)(2,1)S(1)}, u32[]{:S(2)}, u32[]{:S(2)}) collective-permute-start(bf16[384,768]{1,0:T(8,128)(2,1)S(1)} %join.11.mine), channel_id=1, source_target_pairs={{0,1},{1,0},{2,3},{3,2},{4,5},{5,4},{6,7},{7,6},{8,9},{9,8},{10,11... | collective-permute-start | bytes 1769480 | tf_op jit(solution)/shard_map/ppermute | solution.py:729
  334.4 26.0 %collective-permute-start.64 = (bf16[320,768]{1,0:T(8,128)(2,1)S(1)}, bf16[320,768]{1,0:T(8,128)(2,1)S(1)}, u32[]{:S(2)}, u32[]{:S(2)}) collective-permute-start(bf16[320,768]{1,0:T(8,128)(2,1)S(1)} %join.19.mine), channel_id=1, source_target_pairs={{0,1},{1,0},{2,3},{3,2},{4,5},{5,4},{6,7},{7,6},{8,9},{9,8},{10,11... | collective-permute-start | bytes 1474568 | tf_op jit(solution)/shard_map/ppermute | solution.py:729
  338.9 21.5 %collective-permute-start.65 = (bf16[192,768]{1,0:T(8,128)(2,1)S(1)}, bf16[192,768]{1,0:T(8,128)(2,1)S(1)}, u32[]{:S(2)}, u32[]{:S(2)}) collective-permute-start(bf16[192,768]{1,0:T(8,128)(2,1)S(1)} %join.16.mine), channel_id=1, source_target_pairs={{0,1},{1,0},{2,3},{3,2},{4,5},{5,4},{6,7},{7,6},{8,9},{9,8},{10,11... | collective-permute-start | bytes 884744 | tf_op jit(solution)/shard_map/ppermute | solution.py:729
  (83 other events, 721.1 us)

commit v4 on v3

--- a/solution.py
+++ b/solution.py
@@ -29,8 +29,8 @@
     "place_forward": 10, "frame_forward": 14, "mlp_both": 28, "space_back": 19, "time_back": 13,
     "mlp_out_grad": 8, "mlp_in_grad": 8, "space_grad": 7, "pack_rest": 8, "time_projections": 6,
 }
-ORDERS = {"o": "xyuw", "i": "yuxw", "s": "uxyw", "p": "yxuw", "t": "yxuw"}
-SCHEDULE = ("oi", "", "oi", "spi", "", "iptosip", "oistposi" + "tpotsop" + "tsptst")
+ORDERS = {"o": "uyxw", "i": "yuxw", "s": "xyuw", "p": "uyxw", "t": "xyuw"}
+SCHEDULE = ("", "", "io", "", "s", "", "i", "opisotiospispotipsitptsipotpsatapoatasot")
 
 TIME_QKV_PARTS = ((0, 0, 192, 0, 0), (0, 192, 192, 0, 1), (1, 0, 192, 0, 2))
 TIME_PROJ_PARTS = ((1, 192, 192, 0, 0),)
@@ -41,6 +41,7 @@
 MLP_OUT_PARTS = ((0, 0, 384, 0, 0), (1, 0, 384, 384, 0))
 TIME_CHUNK, SPACE_CHUNK, IN_CHUNK, OUT_CHUNK = (0, 768), (768, 960), (1728, 768), (2496, 768)
 VECTOR_AT = 3264
+VECTOR_PAD = 24
 
 
 def nn(left, right):
@@ -483,6 +484,10 @@
 ANY = pl.BlockSpec(memory_space=pltpu.MemorySpace.HBM)
 
 
+def in_hbm(array):
+    return pltpu.with_memory_space_constraint(array, pltpu.MemorySpace.HBM)
+
+
 def call(kernel, name, outs, specs, scratch, operands, microseconds):
     return pl.pallas_call(
         kernel,
@@ -493,7 +498,8 @@
         scratch_shapes=scratch,
         compiler_params=pltpu.CompilerParams(vmem_limit_bytes=LIMITS.get(name, 5) << 20),
         cost_estimate=pl.CostEstimate(
-            flops=int(microseconds * 1.1e9), transcendentals=0, bytes_accessed=1 << 20
+            flops=int((microseconds + 10) * 1.1e9), transcendentals=0,
+            bytes_accessed=1024,
         ),
     )(*operands)
 
@@ -596,7 +602,7 @@
 
 def pack_time_kernel(scalars, time_qkv, time_proj, vectors, out, sems):
     first, second = out.at[pl.ds(0, BLOCK), :], out.at[pl.ds(BLOCK, BLOCK), :]
-    tail = pltpu.make_async_copy(vectors, out.at[pl.ds(2 * BLOCK, 8), :], sems.at[2])
+    tail = pltpu.make_async_copy(vectors, out.at[pl.ds(2 * BLOCK, VECTOR_PAD), :], sems.at[2])
     tail.start()
 
     @pl.when(scalars[1] == 0)
@@ -636,7 +642,7 @@
     for at, source in enumerate(blocks):
         add(source, packed, at * BLOCK, BLOCK)
     add(mlp_out, packed, 13 * BLOCK, 4 * BLOCK)
-    add(vectors, packed, VECTOR_AT, 8)
+    add(vectors, packed, VECTOR_AT, VECTOR_PAD)
     at = len(copies)
     middle = BLOCK // 2
 
@@ -662,27 +668,61 @@
 
 
 def pack_time(*operands):
+    operands = [operands[0], *map(in_hbm, operands[1:])]
     return pl.pallas_call(
         pack_time_kernel, name="pack_time",
-        compiler_params=pltpu.CompilerParams(vmem_limit_bytes=LIMITS.get("pack_time", 5) << 20), out_shape=shape(392, D, bf16),
+        compiler_params=pltpu.CompilerParams(vmem_limit_bytes=LIMITS.get("pack_time", 5) << 20), out_shape=shape(2 * BLOCK + VECTOR_PAD, D, bf16),
         in_specs=[SMEM, ANY, ANY, ANY], out_specs=VMEM,
         scratch_shapes=[pltpu.SemaphoreType.DMA((3,))],
-        cost_estimate=pl.CostEstimate(flops=10**9, transcendentals=0, bytes_accessed=1 << 20),
+        cost_estimate=pl.CostEstimate(flops=11 * 10**9, transcendentals=0, bytes_accessed=1024),
     )(*operands)
 
 
 def pack_rest(*operands):
+    operands = [operands[0], *map(in_hbm, operands[1:])]
     return pl.pallas_call(
         pack_rest_kernel, name="pack_rest",
         compiler_params=pltpu.CompilerParams(vmem_limit_bytes=LIMITS.get("pack_rest", 5) << 20),
         out_shape=[
-            shape(VECTOR_AT + 8, D, bf16), shape(480, D, bf16), shape(384, D, bf16),
+            shape(VECTOR_AT + VECTOR_PAD, D, bf16), shape(480, D, bf16), shape(384, D, bf16),
             shape(384, D, bf16),
         ],
         in_specs=[SMEM] + [ANY] * 8, out_specs=[VMEM] * 4,
         scratch_shapes=[pltpu.SemaphoreType.DMA((21,))],
-        cost_estimate=pl.CostEstimate(flops=3 * 10**9, transcendentals=0, bytes_accessed=1 << 20),
+        cost_estimate=pl.CostEstimate(flops=11 * 10**9, transcendentals=0, bytes_accessed=1024),
     )(*operands)
+
+
+def table_kernel(scalars, own, packed, direct, across, out, pieces, sems):
+    copies = [
+        pltpu.make_async_copy(source.at[pl.ds(row, VECTOR_PAD), :], pieces.at[at], sems.at[at])
+        for at, (source, row) in enumerate(
+            ((own, 0), (packed, VECTOR_AT), (direct, 2 * BLOCK), (across, 2 * BLOCK))
+        )
+    ]
+    copy_all(copies)
+    group_at = scalars[0]
+    out[...] = jnp.zeros((VECTOR_PAD, D), f32)
+    for shard in range(4):
+        rows = pieces[group_at ^ shard].astype(f32)[:, :BLOCK]
+        lanes = slice(shard * BLOCK, (shard + 1) * BLOCK)
+        out[0:10, lanes] = rows[0:10]
+        for row in range(2):
+            lanes = slice((shard % 2) * 384 + row * BLOCK, (shard % 2) * 384 + (row + 1) * BLOCK)
+            for first in (TIME_QV, SPACE_QV):
+                source = rows[first + row : first + row + 1]
+                out[first + shard // 2 : first + shard // 2 + 1, lanes] = source
+        for row in range(4):
+            lanes = slice(row * BLOCK, (row + 1) * BLOCK)
+            source = rows[MLP_IN_B + row : MLP_IN_B + row + 1]
+            out[MLP_IN_B + shard : MLP_IN_B + shard + 1, lanes] = source
+
+
+def vector_table(*operands):
+    return call(
+        table_kernel, "table", [shape(VECTOR_PAD, D, f32)], [SMEM] + [ANY] * 4,
+        [pltpu.VMEM((4, VECTOR_PAD, D), bf16), pltpu.SemaphoreType.DMA((4,))], operands, 1,
+    )[0]
 
 
 def unpack_kernel(scalars, mine, other, *outs, bit, parts):
@@ -782,7 +822,7 @@
     out = dims[1:] if bit == 0 else dims[:-2] + (dims[-2] // 2, D)
     kernel = functools.partial(sum_split_kernel, bit=bit)
     outs = [jax.ShapeDtypeStruct(out, bf16)] * 2
-    return call(kernel, "sum_split", outs, [SMEM, VMEM, VMEM], [], (scalars, kept, got), 1.5)
+    return call(kernel, "sum_split", outs, [SMEM, VMEM, VMEM], [], (scalars, kept, got), 0)
 
 
 def join_kernel(scalars, mine, other, out, *, bit):
@@ -795,7 +835,7 @@
 def join(scalars, mine, other, bit):
     kernel = functools.partial(join_kernel, bit=bit)
     outs = [shape(2 * mine.shape[0], D, bf16)]
-    return call(kernel, "join", outs, [SMEM, VMEM, VMEM], [], (scalars, mine, other), 1)[0]
+    return call(kernel, "join", outs, [SMEM, VMEM, VMEM], [], (scalars, mine, other), 0)[0]
 
 
 class Reduce:
@@ -900,52 +940,44 @@
         near = functools.partial(flip, axis="group", bit=1, size=4)
         relay = functools.partial(flip, axis="replica", bit=1, size=ring_size)
         ends = [sum(v.shape[0] for v in vectors[: at + 1]) for at in range(len(vectors))]
-        flat = sum(jnp.pad(v, (at - v.shape[0], 8 * D - at)) for v, at in zip(vectors, ends))
-        flat = flat.reshape(8, D)
-        time_half = pack_time(scalars, time_qkv, time_proj, flat)
-        time_direct = cross(time_half)
-        token_pieces = after(tokens[0], time_half).transpose(1, 0, 2).reshape(4, 49, 2, D)
-        got = exchange([pick(token_pieces, group_at ^ d) for d in range(4)])
+        room = VECTOR_PAD * BLOCK
+        flat = sum(jnp.pad(v, (at - v.shape[0], room - at)) for v, at in zip(vectors, ends))
+        flat = jnp.pad(flat.reshape(VECTOR_PAD, BLOCK), ((0, 0), (0, D - BLOCK)))
+        token_pieces = tokens[0].transpose(1, 0, 2).reshape(4, 49, 2, D)
+        token_pieces = [pick(token_pieces, group_at ^ d) for d in range(4)]
+        got = exchange(token_pieces)
+        time_half = pack_time(scalars, time_qkv, time_proj, after(flat, *token_pieces))
+        time_direct = cross(after(time_half, *got[1:]))
         place_tokens = jnp.pad(jnp.concatenate(got, axis=1), ((0, 3), (0, 0), (0, 0)))
         place_tokens = place_tokens.reshape(ROWS, D)
 
         packed, space_half, in_half, out_half = pack_rest(
             scalars, time_qkv, time_proj, time_fc, space_qkv, space_proj, mlp_in, mlp_out,
-            after(flat, got[1]),
+            after(flat, *got[1:]),
         )
         partner = near(packed)
-        time_direct, space_half = lax.optimization_barrier((time_direct, space_half))
         time_across = near(time_direct)
         time_relayed = relay(time_direct)
-        time_pieces = (partner, time_direct, time_relayed, time_across, near(time_relayed))
-        space_direct = cross(after(space_half, got[2], got[3]))
+        space_direct = cross(after(space_half, time_direct))
         in_direct = cross(after(in_half, space_direct))
         out_direct = cross(after(out_half, space_direct))
 
-        held = [flat, partner[VECTOR_AT:], time_direct[384:], time_across[384:]]
-        held = jnp.stack(held).reshape(4, 8 * D)[:, : VECTOR_ROWS * BLOCK]
-        tables = jnp.stack([pick(held, group_at ^ shard) for shard in range(4)]).astype(f32)
-        tables = tables.reshape(4, VECTOR_ROWS, BLOCK)
-        vec = jnp.concatenate(
-            [
-                tables[:, :10].transpose(1, 0, 2).reshape(10, D),
-                tables[:, 10:12].reshape(2, D),
-                tables[:, 12:14].reshape(2, D),
-                tables[:, 14:18].reshape(4, D),
-                jnp.zeros((6, D), f32),
-            ]
+        vec = vector_table(scalars, flat, partner, time_direct, time_across)
+        time_pieces = (
+            partner, time_direct, time_relayed, time_across, near(after(time_relayed, vec)),
         )
         pads = ((0, 0), (0, HALF - PLACES), (0, 0))
         frame_tokens = jnp.pad(tokens[0], pads).reshape(ROWS, D)
         frame_grad = jnp.pad(out_grad[0], pads).reshape(ROWS, D)
 
+        space_across = near(space_direct)
         h1, qkv1, a1, o1, *sends = place_forward(
             scalars, after(place_tokens, space_direct), vec, (time_qkv, time_proj), time_pieces
         )
         received = exchange(sends)
         space_relayed = relay(space_direct)
         space_pieces = (
-            partner, space_direct, space_relayed, near(space_direct),
+            partner, space_direct, space_relayed, space_across,
             near(after(space_relayed, o1)),
         )
         x1, h2, qkv2, a2, x2, h3 = frame_forward(
@@ -954,7 +986,7 @@
         )
         in_relayed = relay(in_direct)
         in_pieces = (
-            partner, in_direct, in_relayed, near(after(in_direct, x2)), near(after(in_relayed, x2)),
+            partner, in_direct, in_relayed, near(in_direct), near(after(in_relayed, x2)),
         )
         out_relayed = relay(out_direct)
         out_pieces = (
@@ -979,45 +1011,68 @@
         ways = {}
         last = ()
 
+        back = {"sent": None, "got": [], "flying": None, "out": None}
+
+        def move_back():
+            nonlocal last
+            sends, got = back["sent"], back["got"]
+            if back["flying"] is not None:
+                got.append(after(back["flying"], *last))
+                last = (got[-1],)
+            at = len(got) + 1
+            if at < 4:
+                back["flying"] = flip(after(sends[at], *last), "group", at, 4)
+            else:
+                back["out"] = last_sum(scalars, e1, [sends[0]] + got)
+                back["flying"] = None
+                last = (back["out"],)
+
         def advance(steps):
             nonlocal last
             for name in steps:
-                if ways[name].steps:
+                if name == "a":
+                    move_back()
+                elif ways[name].steps:
                     last = (ways[name].advance(*last),)
 
         ways["o"] = way(weight_grads("mlp_out_grad", scalars, [(act, dm)]), ORDERS["o"])
+        last = (ways["o"].kept,)
+        advance(SCHEDULE[0])
         ways["i"] = way(
-            weight_grads("mlp_in_grad", scalars, [(h3, after(du, ways["o"].kept))]), ORDERS["i"]
+            weight_grads("mlp_in_grad", scalars, [(h3, after(du, *last))]), ORDERS["i"]
         )
         last = (ways["i"].kept,)
-        advance(SCHEDULE[0])
+        advance(SCHEDULE[1])
         dqkv2, e1, dt2, sums2, *sends = space_back(
             scalars, vec, after(e2, *last), x1, qkv2, (space_proj, space_qkv), space_pieces
         )
         received = exchange(sends)
         last = (e1,)
-        advance(SCHEDULE[1])
+        advance(SCHEDULE[2])
         ways["s"] = way(
             weight_grads("space_grad", scalars, [(h2, after(dqkv2, *last)), (a2, dt2)]),
             ORDERS["s"],
         )
         last = (ways["s"].kept,)
-        advance(SCHEDULE[2])
+        advance(SCHEDULE[3])
         dt1, do1, da1, early = time_projections(
             scalars, [after(received[0], *last)] + received[1:], (time_fc, time_proj),
             space_pieces, time_pieces,
         )
+        last = (do1,)
+        advance(SCHEDULE[4])
         ways["p"] = way(
-            weight_grads("time_small_grad", scalars, [(a1, do1), (o1, dt1)]), ORDERS["p"]
+            weight_grads("time_small_grad", scalars, [(a1, after(do1, *last)), (o1, dt1)]),
+            ORDERS["p"],
         )
         last = (ways["p"].kept,)
-        advance(SCHEDULE[3])
+        advance(SCHEDULE[5])
         dqkv1, sums1, *sends = time_back(
             scalars, vec, place_tokens, qkv1, after(da1, *last), early, time_qkv, time_pieces
         )
-        received = exchange(sends)
+        back["sent"] = sends
         last = (dqkv1,)
-        advance(SCHEDULE[4])
+        advance(SCHEDULE[6])
         ways["t"] = way(
             weight_grads(
                 "time_grad", scalars, [(h1, after(dqkv1, *last))], (sums1, sums2, sums3)
@@ -1025,11 +1080,10 @@
             ORDERS["t"],
         )
         last = (ways["t"].kept,)
-        advance(SCHEDULE[5])
-        tokens_grad = last_sum(scalars, after(e1, *last), received)
-        last = (tokens_grad,)
-        tokens_grad = tokens_grad.reshape(2, HALF, D)[None, :, :PLACES]
-        advance(SCHEDULE[6])
+        advance(SCHEDULE[7])
+        while back["out"] is None:
+            move_back()
+        tokens_grad = back["out"].reshape(2, HALF, D)[None, :, :PLACES]
         while any(each.steps for each in ways.values()):
             advance([name for name in ways])
         way_out, way_in, way_space, way_small, way_time = (ways[name] for name in "oispt")

time: 375 us -> 338 us (0.901)
  waiting for transfers between devices: 159 us -> 130 us
  local copies, waits for them, and re-layouts: 26.6 us -> 8.36 us
  starting transfers between devices: 61.4 us -> 69.8 us
  Pallas kernels: 116 us -> 120 us
    ppermute x69, waiting for transfers between devices: 159 us -> 130 us  [flip(): return lax.ppermute(array, axis, [(at, at ^ bit) for at in range(size)])]
    unnamed x86 -> x64, local copies, waits for them, and re-layouts: 21.8 us -> 4.08 us
    ppermute x69, starting transfers between devices: 61.4 us -> 69.8 us  [flip(): return lax.ppermute(array, axis, [(at, at ^ bit) for at in range(size)])]
    pallas_call x47 -> x48, Pallas kernels: 113 us -> 114 us  [call(): pl.pallas_call(kernel, name=name, out_shape=outs, in_specs=specs, out_spe...]
  transfers between devices with their start and end apart: 69 -> 69, of which waited for: 37 -> 31; matrix products, arithmetic and copies ran while one was open for 1% -> 2% of each run, Pallas kernels for 21% -> 27%
where the time goes in v4:
time: 338 us; the launch traced here: 332 us
  waiting for transfers between devices  130 us (38%)
  Pallas kernels  120 us (36%)
  starting transfers between devices  69.8 us (21%)
  local copies, waits for them, and re-layouts  8.36 us (2%)
    ppermute x69, waiting for transfers between devices, flip(): return lax.ppermute(array, axis, [(at, at ^ bit) for at in range(size)])  130 us
    pallas_call x48, Pallas kernels, call(): pl.pallas_call(kernel, name=name, out_shape=outs, in_specs=specs, out_spe...  114 us
    ppermute x69, starting transfers between devices, flip(): return lax.ppermute(array, axis, [(at, at ^ bit) for at in range(size)])  69.8 us
  transfers between devices with their start and end apart: 69, of which 31 were waited for; matrix products, arithmetic and copies ran while one was open for 2% of the time, Pallas kernels for 27%

profile of v4, /device:TPU:0, one launch (start us, length us, event | category | flops | bytes accessed | tf_op | source)
XLA Modules:
  0.0 331.9 jit_solution(15101294122924911940)
XLA Ops:
  9.0 3.4 %collective-permute-done.1 = bf16[49,2,768]{2,1,0:T(2,128)(2,1)S(1)} collective-permute-done((bf16[49,2,768]{2,1,0:T(2,128)(2,1)S(1)}, bf16[49,2,768]{2,1,0:T(2,128)(2,1)S(1)}, u32[]{:S(2)}, u32[]{:S(2)}) %collective-permute-start.1) | collective-permute-done | bytes 150560 | tf_op jit(solution)/shard_map/ppermute | solution.py:769
  12.4 3.8 %pack_rest.1 = (bf16[3288,768]{1,0:T(8,128)(2,1)S(1)}, bf16[480,768]{1,0:T(8,128)(2,1)S(1)}, bf16[384,768]{1,0:T(8,128)(2,1)S(1)}, bf16[384,768]{1,0:T(8,128)(2,1)S(1)}) custom-call(s32[3]{0:T(128)S(1)} %pad_add_fusion.1.scalars, bf16[192,2304]{1,0:T(8,128)(2,1)} %own_qkv.1, bf16[192,768]{1,0:T(8,128)(2,1)} %refs_1_.9, bf16[192,768]{1,0:T(8,128)(2,1)} %refs_0_.9, ...), custom_call_target="tpu_custom_call" | custom-call | flops 11000000512 | bytes 1024 | tf_op jit(solution)/shard_map/pack_rest/pallas_call | solution.py:683
  20.3 14.7 %collective-permute-done.4.direct.refs_3_.refs_7_.refs_1_ = bf16[408,768]{1,0:T(8,128)(2,1)S(1)} collective-permute-done((bf16[408,768]{1,0:T(8,128)(2,1)S(1)}, bf16[408,768]{1,0:T(8,128)(2,1)S(1)}, u32[]{:S(2)}, u32[]{:S(2)}) %collective-permute-start.4) | collective-permute-done | bytes 626720 | tf_op jit(solution)/shard_map/ppermute | solution.py:769
  39.3 13.7 %collective-permute-done.9.refs_4_.refs_8_.refs_2_ = bf16[408,768]{1,0:T(8,128)(2,1)S(1)} collective-permute-done((bf16[408,768]{1,0:T(8,128)(2,1)S(1)}, bf16[408,768]{1,0:T(8,128)(2,1)S(1)}, u32[]{:S(2)}, u32[]{:S(2)}) %collective-permute-start.9) | collective-permute-done | bytes 626720 | tf_op jit(solution)/shard_map/ppermute | solution.py:769
  57.8 9.4 %place_forward.1 = (bf16[416,768]{1,0:T(8,128)(2,1)S(1)}, bf16[416,2304]{1,0:T(8,128)(2,1)S(1)}, bf16[416,768]{1,0:T(8,128)(2,1)S(1)}, bf16[416,768]{1,0:T(8,128...) custom-call(s32[3]{0:T(128)S(1)} %pad_add_fusion.1.scalars, ...), custom_call_target="tpu_custom_call" | custom-call | flops 23100000256 | bytes 1024 | tf_op jit(solution)/shard_map/place_forward/pallas_call | solution.py:492
  67.3 7.6 %collective-permute-done.14.refs_5_.refs_4_ = bf16[480,768]{1,0:T(8,128)(2,1)S(1)} collective-permute-done((bf16[480,768]{1,0:T(8,128)(2,1)S(1)}, bf16[480,768]{1,0:T(8,128)(2,1)S(1)}, u32[]{:S(2)}, u32[]{:S(2)}) %collective-permute-start.14) | collective-permute-done | bytes 737312 | tf_op jit(solution)/shard_map/ppermute | solution.py:769
  77.2 5.6 %collective-permute-done.8.refs_7_ = bf16[384,768]{1,0:T(8,128)(2,1)S(1)} collective-permute-done((bf16[384,768]{1,0:T(8,128)(2,1)S(1)}, bf16[384,768]{1,0:T(8,128)(2,1)S(1)}, u32[]{:S(2)}, u32[]{:S(2)}) %collective-permute-start.8) | collective-permute-done | bytes 589856 | tf_op jit(solution)/shard_map/ppermute | solution.py:769
  88.9 12.6 %frame_forward.1 = (f32[416,768]{1,0:T(8,128)S(1)}, bf16[416,768]{1,0:T(8,128)(2,1)S(1)}, bf16[416,2304]{1,0:T(8,128)(2,1)S(1)}, bf16[416,768]{1,0:T(8,128)(2,1)...) custom-call(s32[3]{0:T(128)S(1)} %pad_add_fusion.1.scalars, bf16[416,768]{1,0:T(8,128)(2,1)S(1)} %bitcast.41, ...), custom_call_target="tpu_custom_call" | custom-call | flops 25300000768 | bytes 1024 | tf_op jit(solution)/shard_map/frame_forward/pallas_call | solution.py:492
  102.4 10.5 %collective-permute-done.20.refs_8_ = bf16[384,768]{1,0:T(8,128)(2,1)S(1)} collective-permute-done((bf16[384,768]{1,0:T(8,128)(2,1)S(1)}, bf16[384,768]{1,0:T(8,128)(2,1)S(1)}, u32[]{:S(2)}, u32[]{:S(2)}) %collective-permute-start.20) | collective-permute-done | bytes 589856 | tf_op jit(solution)/shard_map/ppermute | solution.py:769
  116.6 12.4 %mlp_both.1 = (bf16[416,768]{1,0:T(8,128)(2,1)S(1)}, bf16[416,3072]{1,0:T(8,128)(2,1)S(1)}, bf16[416,3072]{1,0:T(8,128)(2,1)S(1)}, bf16[416,768]{1,0:T(8,128)(2,...) custom-call(s32[3]{0:T(128)S(1)} %pad_add_fusion.1.scalars, f32[1,1]{1,0:T(1,128)} %bitcast.3.live, ...), custom_call_target="tpu_custom_call" | custom-call | flops 30799998976 | bytes 1024 | tf_op jit(solution)/shard_map/mlp_both/pallas_call | solution.py:492
  132.3 3.5 %mlp_in_grad.1 = (bf16[2,768,768]{2,1,0:T(8,128)(2,1)S(1)}, bf16[2,768,768]{2,1,0:T(8,128)(2,1)S(1)}) custom-call(s32[3]{0:T(128)S(1)} %pad_add_fusion.1.scalars, bf16[416,768]{1,0:T(8,128)(2,1)S(1)} %get-tuple-element.206.h3.refs_0_, bf16[416,3072]{1,0:T(8,128)(2,1)S(1)} %get-tuple-element.216.refs_1_), custom_call_target="tpu_custom_call" | custom-call | flops 16632000512 | bytes 1024 | tf_op jit(solution)/shard_map/mlp_in_grad/pallas_call | solution.py:492
  136.4 13.1 %space_back.1 = (bf16[416,2304]{1,0:T(8,128)(2,1)S(1)}, f32[416,768]{1,0:T(8,128)S(1)}, bf16[416,768]{1,0:T(8,128)(2,1)S(1)}, f32[8,768]{1,0:T(8,128)S(1)}, bf16...) custom-call(s32[3]{0:T(128)S(1)} %pad_add_fusion.1.scalars, ...), custom_call_target="tpu_custom_call" | custom-call | flops 32999999488 | bytes 1024 | tf_op jit(solution)/shard_map/space_back/pallas_call | solution.py:492
  152.0 3.3 %space_grad.1 = (bf16[2,768,768]{2,1,0:T(8,128)(2,1)S(1)}, bf16[2,768,768]{2,1,0:T(8,128)(2,1)S(1)}) custom-call(s32[3]{0:T(128)S(1)} %pad_add_fusion.1.scalars, bf16[416,768]{1,0:T(8,128)(2,1)S(1)} %copy-done.21, bf16[416,2304]{1,0:T(8,128)(2,1)S(1)} %get-tuple-element.232.refs_1_, bf16[416,768]{1,0:T(8,128)(2,1)S(1)} %copy-done.23, ...), custom_call_target="tpu_custom_call" | custom-call | flops 16632000512 | bytes 1024 | tf_op jit(solution)/shard_map/space_grad/pallas_call | solution.py:492
  164.6 5.3 %time_projections.1 = (bf16[416,768]{1,0:T(8,128)(2,1)S(1)}, bf16[416,768]{1,0:T(8,128)(2,1)S(1)}, bf16[416,768]{1,0:T(8,128)(2,1)S(1)}, f32[8,768]{1,0:T(8,128)S(1)}) custom-call(s32[3]{0:T(128)S(1)} %pad_add_fusion.1.scalars, bf16[104,768]{1,0:T(8,128)(2,1)S(1)} %get-tuple-element.236.r0, bf16[104,768]{1,0:T(8,128)(2,1)S(1)} %collective-permute-done.25.r1, ...), custom_call_target="tpu_custom_call" | custom-call | flops 15399999488 | bytes 1024 | tf_op jit(solution)/shard_map/time_projections/pallas_call | solution.py:492
  173.4 12.0 %time_back.1 = (bf16[416,2304]{1,0:T(8,128)(2,1)S(1)}, f32[8,768]{1,0:T(8,128)S(1)}, bf16[104,768]{1,0:T(8,128)(2,1)S(1)}, bf16[104,768]{1,0:T(8,128)(2,1)S(1)},...) custom-call(s32[3]{0:T(128)S(1)} %pad_add_fusion.1.scalars, f32[24,768]{1,0:T(8,128)S(1)} %table.1.vec, ...), custom_call_target="tpu_custom_call" | custom-call | flops 28600000512 | bytes 1024 | tf_op jit(solution)/shard_map/time_back/pallas_call | solution.py:492
  188.8 3.3 %time_grad.1 = (bf16[2,640,768]{2,1,0:T(8,128)(2,1)S(1)}, bf16[2,640,768]{2,1,0:T(8,128)(2,1)S(1)}) custom-call(s32[3]{0:T(128)S(1)} %pad_add_fusion.1.scalars, bf16[416,768]{1,0:T(8,128)(2,1)S(1)} %get-tuple-element.261.refs_0_, bf16[416,2304]{1,0:T(8,128)(2,1)S(1)} %get-tuple-element.262.refs_1_, f32[8,768]{1,0:T(8,128)S(1)} %get-tuple-element.263.refs_2_, ...), custom_call_target="tpu_custom_call" | custom-call | flops 15693333504 | bytes 1024 | tf_op jit(solution)/shard_map/time_grad/pallas_call | solution.py:492
  196.2 6.7 %collective-permute-done.31.got = bf16[2,192,768]{2,1,0:T(8,128)(2,1)S(1)} collective-permute-done((bf16[2,192,768]{2,1,0:T(8,128)(2,1)S(1)}, bf16[2,192,768]{2,1,0:T(8,128)(2,1)S(1)}, u32[]{:S(2)}, u32[]{:S(2)}) %collective-permute-start.31) | collective-permute-done | bytes 589856 | tf_op jit(solution)/shard_map/ppermute | solution.py:769
  204.1 13.1 %collective-permute-done.29.got = bf16[768,768]{1,0:T(8,128)(2,1)S(1)} collective-permute-done((bf16[768,768]{1,0:T(8,128)(2,1)S(1)}, bf16[768,768]{1,0:T(8,128)(2,1)S(1)}, u32[]{:S(2)}, u32[]{:S(2)}) %collective-permute-start.29) | collective-permute-done | bytes 1179680 | tf_op jit(solution)/shard_map/ppermute | solution.py:769
  227.0 3.4 %collective-permute-done.36.got = bf16[192,768]{1,0:T(8,128)(2,1)S(1)} collective-permute-done((bf16[192,768]{1,0:T(8,128)(2,1)S(1)}, bf16[192,768]{1,0:T(8,128)(2,1)S(1)}, u32[]{:S(2)}, u32[]{:S(2)}) %collective-permute-start.36) | collective-permute-done | bytes 294944 | tf_op jit(solution)/shard_map/ppermute | solution.py:769
  238.2 8.5 %collective-permute-done.39.got = bf16[192,768]{1,0:T(8,128)(2,1)S(1)} collective-permute-done((bf16[192,768]{1,0:T(8,128)(2,1)S(1)}, bf16[192,768]{1,0:T(8,128)(2,1)S(1)}, u32[]{:S(2)}, u32[]{:S(2)}) %collective-permute-start.39) | collective-permute-done | bytes 294944 | tf_op jit(solution)/shard_map/ppermute | solution.py:769
  257.8 5.0 %collective-permute-done.50.other = bf16[192,768]{1,0:T(8,128)(2,1)S(1)} collective-permute-done((bf16[192,768]{1,0:T(8,128)(2,1)S(1)}, bf16[192,768]{1,0:T(8,128)(2,1)S(1)}, u32[]{:S(2)}, u32[]{:S(2)}) %collective-permute-start.50) | collective-permute-done | bytes 294944 | tf_op jit(solution)/shard_map/ppermute | solution.py:769
  276.3 10.0 %collective-permute-done.48.other = bf16[96,768]{1,0:T(8,128)(2,1)S(1)} collective-permute-done((bf16[96,768]{1,0:T(8,128)(2,1)S(1)}, bf16[96,768]{1,0:T(8,128)(2,1)S(1)}, u32[]{:S(2)}, u32[]{:S(2)}) %collective-permute-start.48) | collective-permute-done | bytes 147488 | tf_op jit(solution)/shard_map/ppermute | solution.py:769
  292.4 3.5 %collective-permute-start.60 = (bf16[80,768]{1,0:T(8,128)(2,1)S(1)}, bf16[80,768]{1,0:T(8,128)(2,1)S(1)}, u32[]{:S(2)}, u32[]{:S(2)}) collective-permute-start(bf16[80,768]{1,0:T(8,128)(2,1)S(1)} %add_convert_fusion.3.mine), channel_id=1, source_target_pairs={{0,4},{1,5},{2,6},{3,7},{4,0},{5,1},{6,2},{7,3},{8,12},{9,13},{10,... | collective-permute-start | bytes 368648 | tf_op jit(solution)/shard_map/ppermute | solution.py:769
  312.3 5.1 %collective-permute-done.64.r3 = bf16[104,768]{1,0:T(8,128)(2,1)S(1)} collective-permute-done((bf16[104,768]{1,0:T(8,128)(2,1)S(1)}, bf16[104,768]{1,0:T(8,128)(2,1)S(1)}, u32[]{:S(2)}, u32[]{:S(2)}) %collective-permute-start.64) | collective-permute-done | bytes 159776 | tf_op jit(solution)/shard_map/ppermute | solution.py:769
  (246 shorter events, 139.7 us)
Async XLA Ops:
  16.2 22.3 %collective-permute-start.3 = (bf16[3288,768]{1,0:T(8,128)(2,1)S(1)}, bf16[3288,768]{1,0:T(8,128)(2,1)S(1)}, u32[]{:S(2)}, u32[]{:S(2)}) collective-permute-start(bf16[3288,768]{1,0:T(8,128)(2,1)S(1)} %get-tuple-element.187), channel_id=1, source_target_pairs={{0,8},{8,0},{16,24},{24,16},{1,9},{9,1},{17,25},{25,17},{2,10},{10... | collective-permute-start | bytes 15151112 | tf_op jit(solution)/shard_map/ppermute | solution.py:769
  35.0 18.9 %collective-permute-start.6 = (bf16[480,768]{1,0:T(8,128)(2,1)S(1)}, bf16[480,768]{1,0:T(8,128)(2,1)S(1)}, u32[]{:S(2)}, u32[]{:S(2)}) collective-permute-start(bf16[480,768]{1,0:T(8,128)(2,1)S(1)} %get-tuple-element.192), channel_id=1, source_target_pairs={{0,16},{8,24},{16,0},{24,8},{1,17},{9,25},{17,1},{25,9},{2,18},{10... | collective-permute-start | bytes 2211848 | tf_op jit(solution)/shard_map/ppermute | solution.py:769
  54.0 21.5 %collective-permute-start.7 = (bf16[384,768]{1,0:T(8,128)(2,1)S(1)}, bf16[384,768]{1,0:T(8,128)(2,1)S(1)}, u32[]{:S(2)}, u32[]{:S(2)}) collective-permute-start(bf16[384,768]{1,0:T(8,128)(2,1)S(1)} %get-tuple-element.193), channel_id=1, source_target_pairs={{0,16},{8,24},{16,0},{24,8},{1,17},{9,25},{17,1},{25,9},{2,18},{10... | collective-permute-start | bytes 1769480 | tf_op jit(solution)/shard_map/ppermute | solution.py:769
  55.7 27.0 %collective-permute-start.8 = (bf16[384,768]{1,0:T(8,128)(2,1)S(1)}, bf16[384,768]{1,0:T(8,128)(2,1)S(1)}, u32[]{:S(2)}, u32[]{:S(2)}) collective-permute-start(bf16[384,768]{1,0:T(8,128)(2,1)S(1)} %get-tuple-element.195), channel_id=1, source_target_pairs={{0,16},{8,24},{16,0},{24,8},{1,17},{9,25},{17,1},{25,9},{2,18},{10... | collective-permute-start | bytes 1769480 | tf_op jit(solution)/shard_map/ppermute | solution.py:769
  56.0 26.9 %collective-permute-start.15 = (bf16[480,768]{1,0:T(8,128)(2,1)S(1)}, bf16[480,768]{1,0:T(8,128)(2,1)S(1)}, u32[]{:S(2)}, u32[]{:S(2)}) collective-permute-start(bf16[480,768]{1,0:T(8,128)(2,1)S(1)} %collective-permute-done.6.refs_4_.refs_3_), channel_id=1, source_target_pairs={{0,8},{8,0},{16,24},{24,16},{1,9},{9,1},{17,25},{25,17},{2,10},{10... | collective-permute-start | bytes 2211848 | tf_op jit(solution)/shard_map/ppermute | solution.py:769
  56.0 18.9 %collective-permute-start.14 = (bf16[480,768]{1,0:T(8,128)(2,1)S(1)}, bf16[480,768]{1,0:T(8,128)(2,1)S(1)}, u32[]{:S(2)}, u32[]{:S(2)}) collective-permute-start(bf16[480,768]{1,0:T(8,128)(2,1)S(1)} %collective-permute-done.6.refs_4_.refs_3_), channel_id=1, source_target_pairs={{0,1},{1,0},{2,3},{3,2},{4,5},{5,4},{6,7},{7,6},{8,9},{9,8},{10,11... | collective-permute-start | bytes 2211848 | tf_op jit(solution)/shard_map/ppermute | solution.py:769
  82.9 31.3 %collective-permute-start.18 = (bf16[384,768]{1,0:T(8,128)(2,1)S(1)}, bf16[384,768]{1,0:T(8,128)(2,1)S(1)}, u32[]{:S(2)}, u32[]{:S(2)}) collective-permute-start(bf16[384,768]{1,0:T(8,128)(2,1)S(1)} %collective-permute-done.7.refs_3_), channel_id=1, source_target_pairs={{0,8},{8,0},{16,24},{24,16},{1,9},{9,1},{17,25},{25,17},{2,10},{10... | collective-permute-start | bytes 1769480 | tf_op jit(solution)/shard_map/ppermute | solution.py:769
  84.9 28.0 %collective-permute-start.17 = (bf16[384,768]{1,0:T(8,128)(2,1)S(1)}, bf16[384,768]{1,0:T(8,128)(2,1)S(1)}, u32[]{:S(2)}, u32[]{:S(2)}) collective-permute-start(bf16[384,768]{1,0:T(8,128)(2,1)S(1)} %collective-permute-done.7.refs_3_), channel_id=1, source_target_pairs={{0,1},{1,0},{2,3},{3,2},{4,5},{5,4},{6,7},{7,6},{8,9},{9,8},{10,11... | collective-permute-start | bytes 1769480 | tf_op jit(solution)/shard_map/ppermute | solution.py:769
  86.5 26.4 %collective-permute-start.20 = (bf16[384,768]{1,0:T(8,128)(2,1)S(1)}, bf16[384,768]{1,0:T(8,128)(2,1)S(1)}, u32[]{:S(2)}, u32[]{:S(2)}) collective-permute-start(bf16[384,768]{1,0:T(8,128)(2,1)S(1)} %collective-permute-done.8.refs_7_), channel_id=1, source_target_pairs={{0,1},{1,0},{2,3},{3,2},{4,5},{5,4},{6,7},{7,6},{8,9},{9,8},{10,11... | collective-permute-start | bytes 1769480 | tf_op jit(solution)/shard_map/ppermute | solution.py:769
  157.4 28.6 %collective-permute-start.30 = (bf16[2,384,768]{2,1,0:T(8,128)(2,1)S(1)}, bf16[2,384,768]{2,1,0:T(8,128)(2,1)S(1)}, u32[]{:S(2)}, u32[]{:S(2)}) collective-permute-start(bf16[2,384,768]{2,1,0:T(8,128)(2,1)S(1)} %get-tuple-element.229), channel_id=1, source_target_pairs={{0,1},{1,0},{2,3},{3,2},{4,5},{5,4},{6,7},{7,6},{8,9},{9,8},{10,11... | collective-permute-start | bytes 3538952 | tf_op jit(solution)/shard_map/ppermute | solution.py:769
  160.1 32.0 %collective-permute-start.33 = (bf16[2,384,768]{2,1,0:T(8,128)(2,1)S(1)}, bf16[2,384,768]{2,1,0:T(8,128)(2,1)S(1)}, u32[]{:S(2)}, u32[]{:S(2)}) collective-permute-start(bf16[2,384,768]{2,1,0:T(8,128)(2,1)S(1)} %get-tuple-element.231), channel_id=1, source_target_pairs={{0,2},{1,3},{2,0},{3,1},{4,6},{5,7},{6,4},{7,5},{8,10},{9,11},{10,... | collective-permute-start | bytes 3538952 | tf_op jit(solution)/shard_map/ppermute | solution.py:769
  188.4 28.8 %collective-permute-start.29 = (bf16[768,768]{1,0:T(8,128)(2,1)S(1)}, bf16[768,768]{1,0:T(8,128)(2,1)S(1)}, u32[]{:S(2)}, u32[]{:S(2)}) collective-permute-start(bf16[768,768]{1,0:T(8,128)(2,1)S(1)} %get-tuple-element.245), channel_id=1, source_target_pairs={{0,16},{8,24},{16,0},{24,8},{1,17},{9,25},{17,1},{25,9},{2,18},{10... | collective-permute-start | bytes 3538952 | tf_op jit(solution)/shard_map/ppermute | solution.py:769
  193.0 26.7 %collective-permute-start.35 = (bf16[2,192,768]{2,1,0:T(8,128)(2,1)S(1)}, bf16[2,192,768]{2,1,0:T(8,128)(2,1)S(1)}, u32[]{:S(2)}, u32[]{:S(2)}) collective-permute-start(bf16[2,192,768]{2,1,0:T(8,128)(2,1)S(1)} %get-tuple-element.268), channel_id=1, source_target_pairs={{0,1},{1,0},{2,3},{3,2},{4,5},{5,4},{6,7},{7,6},{8,9},{9,8},{10,11... | collective-permute-start | bytes 1769480 | tf_op jit(solution)/shard_map/ppermute | solution.py:769
  194.6 26.3 %collective-permute-start.38 = (bf16[2,640,768]{2,1,0:T(8,128)(2,1)S(1)}, bf16[2,640,768]{2,1,0:T(8,128)(2,1)S(1)}, u32[]{:S(2)}, u32[]{:S(2)}) collective-permute-start(bf16[2,640,768]{2,1,0:T(8,128)(2,1)S(1)} %get-tuple-element.281), channel_id=1, source_target_pairs={{0,8},{8,0},{16,24},{24,16},{1,9},{9,1},{17,25},{25,17},{2,10},{10... | collective-permute-start | bytes 5898248 | tf_op jit(solution)/shard_map/ppermute | solution.py:769
  195.7 39.3 %collective-permute-start.41 = (bf16[2,192,768]{2,1,0:T(8,128)(2,1)S(1)}, bf16[2,192,768]{2,1,0:T(8,128)(2,1)S(1)}, u32[]{:S(2)}, u32[]{:S(2)}) collective-permute-start(bf16[2,192,768]{2,1,0:T(8,128)(2,1)S(1)} %get-tuple-element.270), channel_id=1, source_target_pairs={{0,2},{1,3},{2,0},{3,1},{4,6},{5,7},{6,4},{7,5},{8,10},{9,11},{10,... | collective-permute-start | bytes 1769480 | tf_op jit(solution)/shard_map/ppermute | solution.py:769
  203.7 20.0 %collective-permute-start.37 = (bf16[192,768]{1,0:T(8,128)(2,1)S(1)}, bf16[192,768]{1,0:T(8,128)(2,1)S(1)}, u32[]{:S(2)}, u32[]{:S(2)}) collective-permute-start(bf16[192,768]{1,0:T(8,128)(2,1)S(1)} %get-tuple-element.272), channel_id=1, source_target_pairs={{0,16},{8,24},{16,0},{24,8},{1,17},{9,25},{17,1},{25,9},{2,18},{10... | collective-permute-start | bytes 884744 | tf_op jit(solution)/shard_map/ppermute | solution.py:769
  222.0 28.8 %collective-permute-start.46 = (bf16[640,768]{1,0:T(8,128)(2,1)S(1)}, bf16[640,768]{1,0:T(8,128)(2,1)S(1)}, u32[]{:S(2)}, u32[]{:S(2)}) collective-permute-start(bf16[640,768]{1,0:T(8,128)(2,1)S(1)} %get-tuple-element.283), channel_id=1, source_target_pairs={{0,16},{8,24},{16,0},{24,8},{1,17},{9,25},{17,1},{25,9},{2,18},{10... | collective-permute-start | bytes 2949128 | tf_op jit(solution)/shard_map/ppermute | solution.py:769
  265.9 25.8 %collective-permute-start.58 = (bf16[96,768]{1,0:T(8,128)(2,1)S(1)}, bf16[96,768]{1,0:T(8,128)(2,1)S(1)}, u32[]{:S(2)}, u32[]{:S(2)}) collective-permute-start(bf16[96,768]{1,0:T(8,128)(2,1)S(1)} %add_convert_fusion.1.mine), channel_id=1, source_target_pairs={{0,4},{1,5},{2,6},{3,7},{4,0},{5,1},{6,2},{7,3},{8,12},{9,13},{10,... | collective-permute-start | bytes 442376 | tf_op jit(solution)/shard_map/ppermute | solution.py:769
  268.6 17.7 %collective-permute-start.48 = (bf16[96,768]{1,0:T(8,128)(2,1)S(1)}, bf16[96,768]{1,0:T(8,128)(2,1)S(1)}, u32[]{:S(2)}, u32[]{:S(2)}) collective-permute-start(bf16[96,768]{1,0:T(8,128)(2,1)S(1)} %add_convert_fusion.mine), channel_id=1, source_target_pairs={{0,4},{1,5},{2,6},{3,7},{4,0},{5,1},{6,2},{7,3},{8,12},{9,13},{10,... | collective-permute-start | bytes 442376 | tf_op jit(solution)/shard_map/ppermute | solution.py:769
  268.8 18.1 %collective-permute-start.55 = (bf16[384,768]{1,0:T(8,128)(2,1)S(1)}, bf16[384,768]{1,0:T(8,128)(2,1)S(1)}, u32[]{:S(2)}, u32[]{:S(2)}) collective-permute-start(bf16[384,768]{1,0:T(8,128)(2,1)S(1)} %join.11.mine), channel_id=1, source_target_pairs={{0,1},{1,0},{2,3},{3,2},{4,5},{5,4},{6,7},{7,6},{8,9},{9,8},{10,11... | collective-permute-start | bytes 1769480 | tf_op jit(solution)/shard_map/ppermute | solution.py:769
  270.6 18.4 %collective-permute-start.54 = (bf16[48,768]{1,0:T(8,128)(2,1)S(1)}, bf16[48,768]{1,0:T(8,128)(2,1)S(1)}, u32[]{:S(2)}, u32[]{:S(2)}) collective-permute-start(bf16[48,768]{1,0:T(8,128)(2,1)S(1)} %add_convert_fusion.4.mine), channel_id=1, source_target_pairs={{0,4},{1,5},{2,6},{3,7},{4,0},{5,1},{6,2},{7,3},{8,12},{9,13},{10,... | collective-permute-start | bytes 221192 | tf_op jit(solution)/shard_map/ppermute | solution.py:769
  274.7 17.6 %collective-permute-start.57 = (bf16[80,768]{1,0:T(8,128)(2,1)S(1)}, bf16[80,768]{1,0:T(8,128)(2,1)S(1)}, u32[]{:S(2)}, u32[]{:S(2)}) collective-permute-start(bf16[80,768]{1,0:T(8,128)(2,1)S(1)} %get-tuple-element.320), channel_id=1, source_target_pairs={{0,4},{1,5},{2,6},{3,7},{4,0},{5,1},{6,2},{7,3},{8,12},{9,13},{10,... | collective-permute-start | bytes 368648 | tf_op jit(solution)/shard_map/ppermute | solution.py:769
  299.3 21.2 %collective-permute-start.68 = (bf16[384,768]{1,0:T(8,128)(2,1)S(1)}, bf16[384,768]{1,0:T(8,128)(2,1)S(1)}, u32[]{:S(2)}, u32[]{:S(2)}) collective-permute-start(bf16[384,768]{1,0:T(8,128)(2,1)S(1)} %join.16.mine), channel_id=1, source_target_pairs={{0,1},{1,0},{2,3},{3,2},{4,5},{5,4},{6,7},{7,6},{8,9},{9,8},{10,11... | collective-permute-start | bytes 1769480 | tf_op jit(solution)/shard_map/ppermute | solution.py:769
  306.1 17.6 %collective-permute-start.67 = (bf16[384,768]{1,0:T(8,128)(2,1)S(1)}, bf16[384,768]{1,0:T(8,128)(2,1)S(1)}, u32[]{:S(2)}, u32[]{:S(2)}) collective-permute-start(bf16[384,768]{1,0:T(8,128)(2,1)S(1)} %join.18.mine), channel_id=1, source_target_pairs={{0,2},{1,3},{2,0},{3,1},{4,6},{5,7},{6,4},{7,5},{8,10},{9,11},{10,... | collective-permute-start | bytes 1769480 | tf_op jit(solution)/shard_map/ppermute | solution.py:769
  (75 other events, 858.4 us)

commit v5 on v4

--- a/solution.py
+++ b/solution.py
@@ -29,8 +29,8 @@
     "place_forward": 10, "frame_forward": 14, "mlp_both": 28, "space_back": 19, "time_back": 13,
     "mlp_out_grad": 8, "mlp_in_grad": 8, "space_grad": 7, "pack_rest": 8, "time_projections": 6,
 }
-ORDERS = {"o": "uyxw", "i": "yuxw", "s": "xyuw", "p": "uyxw", "t": "xyuw"}
-SCHEDULE = ("", "", "io", "", "s", "", "i", "opisotiospispotipsitptsipotpsatapoatasot")
+ORDERS = {"o": "yuxw", "i": "uxyw", "s": "xyuw", "p": "yxuw", "t": "xyuw"}
+SCHEDULE = ('', '', '', 'ois', '', '', 'ois', 'potsoisoitpostipotsiptoaspatapitspaitp')
 
 TIME_QKV_PARTS = ((0, 0, 192, 0, 0), (0, 192, 192, 0, 1), (1, 0, 192, 0, 2))
 TIME_PROJ_PARTS = ((1, 192, 192, 0, 0),)
@@ -63,7 +63,8 @@
 
 
 class Weights:
-    def __init__(self, scalars, own, pieces, parts, chunk, target, sems):
+    def __init__(self, scalars, own, pieces, parts, chunk, target, sems, half_at=1):
+        self.half_at = half_at
         self.scalars, self.own, self.pieces, self.parts = scalars, own, pieces, parts
         self.chunk, self.target, self.sems = chunk, target, sems
         self.shard_rows = own.shape[0]
@@ -87,7 +88,7 @@
     def start(self):
         packed, direct, relayed, across, across_relayed = self.pieces
         self.own_copy().start()
-        y = self.scalars[1]
+        y = self.scalars[self.half_at]
         first, chunk_rows = self.chunk
         at = 1
         for part in self.parts:
@@ -302,7 +303,7 @@
     in_pieces, out_pieces = [pieces[0]] + pieces[1:5], [pieces[0]] + pieces[5:9]
     layer_out, acts, du, dm, e2, sums, w_in, w_out, sem_a, sem_b = refs[11:]
     in_copy = Weights(scalars, own_in, in_pieces, MLP_IN_PARTS, IN_CHUNK, w_in, sem_a)
-    out_copy = Weights(scalars, own_out, out_pieces, MLP_OUT_PARTS, OUT_CHUNK, w_out, sem_b)
+    out_copy = Weights(scalars, own_out, out_pieces, MLP_OUT_PARTS, OUT_CHUNK, w_out, sem_b, 3)
     in_copy.start()
     out_copy.start()
     e3 = live[0, 0] * out_grad[...].astype(f32)
@@ -631,7 +632,8 @@
         target = target.at[pl.ds(row, rows), :]
         copies.append(pltpu.make_async_copy(source, target, sems.at[len(copies)]))
 
-    halves = pl.ds(pl.multiple_of(half * 2 * BLOCK, 2 * BLOCK), 2 * BLOCK)
+    out_at = scalars[3]
+    halves = pl.ds(pl.multiple_of(out_at * 2 * BLOCK, 2 * BLOCK), 2 * BLOCK)
     add(columns_of(mlp_in, 2 * half), in_half, 0, BLOCK)
     add(columns_of(mlp_in, 2 * half + 1), in_half, BLOCK, BLOCK)
     add(mlp_out.at[halves, :], out_half, 0, 2 * BLOCK)
@@ -929,7 +931,8 @@
         group_at = lax.axis_index("group")
         replica_at = lax.axis_index("replica")
         half_at = replica_at % 2
-        scalars = jnp.stack([group_at, half_at, replica_at]).astype(jnp.int32)
+        far_at = (replica_at // 2) % 2
+        scalars = jnp.stack([group_at, half_at, replica_at, far_at]).astype(jnp.int32)
         live = slot_mask.astype(f32).reshape(1, 1)
         vectors = [
             time_norm_gain, time_norm_shift, time_proj_bias, time_fc_bias, space_norm_gain,
@@ -988,7 +991,7 @@
         in_pieces = (
             partner, in_direct, in_relayed, near(in_direct), near(after(in_relayed, x2)),
         )
-        out_relayed = relay(out_direct)
+        out_relayed = flip(out_direct, "replica", 2, ring_size)
         out_pieces = (
             partner, out_direct, out_relayed, near(after(out_direct, x2)),
             near(after(out_relayed, x2)),

time: 338 us -> 309 us (0.914)
  waiting for transfers between devices: 130 us -> 106 us
  starting transfers between devices: 69.8 us -> 63 us
    ppermute x69, waiting for transfers between devices: 130 us -> 106 us  [flip(): return lax.ppermute(array, axis, [(at, at ^ bit) for at in range(size)])]
    ppermute x69, starting transfers between devices: 69.8 us -> 63 us  [flip(): return lax.ppermute(array, axis, [(at, at ^ bit) for at in range(size)])]
  transfers between devices with their start and end apart: 69 -> 69, of which waited for: 31 -> 26; matrix products, arithmetic and copies ran while one was open for 2% -> 3% of each run, Pallas kernels for 27% -> 31%
where the time goes in v5:
time: 309 us; the launch traced here: 303 us
  Pallas kernels  120 us (39%)
  waiting for transfers between devices  106 us (34%)
  starting transfers between devices  63 us (20%)
  local copies, waits for them, and re-layouts  9.15 us (3%)
    pallas_call x48, Pallas kernels, call(): pl.pallas_call(kernel, name=name, out_shape=outs, in_specs=specs, out_spe...  114 us
    ppermute x69, waiting for transfers between devices, flip(): return lax.ppermute(array, axis, [(at, at ^ bit) for at in range(size)])  106 us
    ppermute x69, starting transfers between devices, flip(): return lax.ppermute(array, axis, [(at, at ^ bit) for at in range(size)])  63 us
  transfers between devices with their start and end apart: 69, of which 26 were waited for; matrix products, arithmetic and copies ran while one was open for 3% of the time, Pallas kernels for 31%

profile of v5, /device:TPU:0, one launch (start us, length us, event | category | flops | bytes accessed | tf_op | source)
XLA Modules:
  0.0 303.2 jit_solution(9708818166011885284)
XLA Ops:
  9.0 3.4 %collective-permute-done.1 = bf16[49,2,768]{2,1,0:T(2,128)(2,1)S(1)} collective-permute-done((bf16[49,2,768]{2,1,0:T(2,128)(2,1)S(1)}, bf16[49,2,768]{2,1,0:T(2,128)(2,1)S(1)}, u32[]{:S(2)}, u32[]{:S(2)}) %collective-permute-start.1) | collective-permute-done | bytes 150560 | tf_op jit(solution)/shard_map/ppermute | solution.py:771
  12.4 3.8 %pack_rest.1 = (bf16[3288,768]{1,0:T(8,128)(2,1)S(1)}, bf16[480,768]{1,0:T(8,128)(2,1)S(1)}, bf16[384,768]{1,0:T(8,128)(2,1)S(1)}, bf16[384,768]{1,0:T(8,128)(2,1)S(1)}) custom-call(s32[4]{0:T(128)S(1)} %pad_add_fusion.1.scalars, bf16[192,2304]{1,0:T(8,128)(2,1)} %own_qkv.1, bf16[192,768]{1,0:T(8,128)(2,1)} %refs_1_.9, bf16[192,768]{1,0:T(8,128)(2,1)} %refs_0_.9, ...), custom_call_target="tpu_custom_call" | custom-call | flops 11000000512 | bytes 1024 | tf_op jit(solution)/shard_map/pack_rest/pallas_call | solution.py:685
  20.3 14.7 %collective-permute-done.4.direct.refs_3_.refs_7_.refs_1_ = bf16[408,768]{1,0:T(8,128)(2,1)S(1)} collective-permute-done((bf16[408,768]{1,0:T(8,128)(2,1)S(1)}, bf16[408,768]{1,0:T(8,128)(2,1)S(1)}, u32[]{:S(2)}, u32[]{:S(2)}) %collective-permute-start.4) | collective-permute-done | bytes 626720 | tf_op jit(solution)/shard_map/ppermute | solution.py:771
  39.3 13.7 %collective-permute-done.9.refs_4_.refs_8_.refs_2_ = bf16[408,768]{1,0:T(8,128)(2,1)S(1)} collective-permute-done((bf16[408,768]{1,0:T(8,128)(2,1)S(1)}, bf16[408,768]{1,0:T(8,128)(2,1)S(1)}, u32[]{:S(2)}, u32[]{:S(2)}) %collective-permute-start.9) | collective-permute-done | bytes 626720 | tf_op jit(solution)/shard_map/ppermute | solution.py:771
  57.8 9.4 %place_forward.1 = (bf16[416,768]{1,0:T(8,128)(2,1)S(1)}, bf16[416,2304]{1,0:T(8,128)(2,1)S(1)}, bf16[416,768]{1,0:T(8,128)(2,1)S(1)}, bf16[416,768]{1,0:T(8,128...) custom-call(s32[4]{0:T(128)S(1)} %pad_add_fusion.1.scalars, ...), custom_call_target="tpu_custom_call" | custom-call | flops 23100000256 | bytes 1024 | tf_op jit(solution)/shard_map/place_forward/pallas_call | solution.py:493
  68.1 6.8 %collective-permute-done.14.refs_5_.refs_4_ = bf16[480,768]{1,0:T(8,128)(2,1)S(1)} collective-permute-done((bf16[480,768]{1,0:T(8,128)(2,1)S(1)}, bf16[480,768]{1,0:T(8,128)(2,1)S(1)}, u32[]{:S(2)}, u32[]{:S(2)}) %collective-permute-start.14) | collective-permute-done | bytes 737312 | tf_op jit(solution)/shard_map/ppermute | solution.py:771
  77.2 5.6 %collective-permute-done.8.refs_7_ = bf16[384,768]{1,0:T(8,128)(2,1)S(1)} collective-permute-done((bf16[384,768]{1,0:T(8,128)(2,1)S(1)}, bf16[384,768]{1,0:T(8,128)(2,1)S(1)}, u32[]{:S(2)}, u32[]{:S(2)}) %collective-permute-start.8) | collective-permute-done | bytes 589856 | tf_op jit(solution)/shard_map/ppermute | solution.py:771
  88.9 12.6 %frame_forward.1 = (f32[416,768]{1,0:T(8,128)S(1)}, bf16[416,768]{1,0:T(8,128)(2,1)S(1)}, bf16[416,2304]{1,0:T(8,128)(2,1)S(1)}, bf16[416,768]{1,0:T(8,128)(2,1)...) custom-call(s32[4]{0:T(128)S(1)} %pad_add_fusion.1.scalars, bf16[416,768]{1,0:T(8,128)(2,1)S(1)} %bitcast.42, ...), custom_call_target="tpu_custom_call" | custom-call | flops 25300000768 | bytes 1024 | tf_op jit(solution)/shard_map/frame_forward/pallas_call | solution.py:493
  106.3 12.4 %mlp_both.1 = (bf16[416,768]{1,0:T(8,128)(2,1)S(1)}, bf16[416,3072]{1,0:T(8,128)(2,1)S(1)}, bf16[416,3072]{1,0:T(8,128)(2,1)S(1)}, bf16[416,768]{1,0:T(8,128)(2,...) custom-call(s32[4]{0:T(128)S(1)} %pad_add_fusion.1.scalars, f32[1,1]{1,0:T(1,128)} %bitcast.4.live, ...), custom_call_target="tpu_custom_call" | custom-call | flops 30799998976 | bytes 1024 | tf_op jit(solution)/shard_map/mlp_both/pallas_call | solution.py:493
  118.7 3.2 %mlp_out_grad.1 = (bf16[2,768,768]{2,1,0:T(8,128)(2,1)S(1)}, bf16[2,768,768]{2,1,0:T(8,128)(2,1)S(1)}) custom-call(s32[4]{0:T(128)S(1)} %pad_add_fusion.1.scalars, bf16[416,3072]{1,0:T(8,128)(2,1)S(1)} %get-tuple-element.212.refs_0_, bf16[416,768]{1,0:T(8,128)(2,1)S(1)} %get-tuple-element.213.refs_1_), custom_call_target="tpu_custom_call" | custom-call | flops 16632000512 | bytes 1024 | tf_op jit(solution)/shard_map/mlp_out_grad/pallas_call | solution.py:493
  121.9 3.5 %mlp_in_grad.1 = (bf16[2,768,768]{2,1,0:T(8,128)(2,1)S(1)}, bf16[2,768,768]{2,1,0:T(8,128)(2,1)S(1)}) custom-call(s32[4]{0:T(128)S(1)} %pad_add_fusion.1.scalars, bf16[416,768]{1,0:T(8,128)(2,1)S(1)} %get-tuple-element.205.h3.refs_0_, bf16[416,3072]{1,0:T(8,128)(2,1)S(1)} %get-tuple-element.215.refs_1_), custom_call_target="tpu_custom_call" | custom-call | flops 16632000512 | bytes 1024 | tf_op jit(solution)/shard_map/mlp_in_grad/pallas_call | solution.py:493
  125.9 13.1 %space_back.1 = (bf16[416,2304]{1,0:T(8,128)(2,1)S(1)}, f32[416,768]{1,0:T(8,128)S(1)}, bf16[416,768]{1,0:T(8,128)(2,1)S(1)}, f32[8,768]{1,0:T(8,128)S(1)}, bf16...) custom-call(s32[4]{0:T(128)S(1)} %pad_add_fusion.1.scalars, ...), custom_call_target="tpu_custom_call" | custom-call | flops 32999999488 | bytes 1024 | tf_op jit(solution)/shard_map/space_back/pallas_call | solution.py:493
  139.3 3.3 %space_grad.1 = (bf16[2,768,768]{2,1,0:T(8,128)(2,1)S(1)}, bf16[2,768,768]{2,1,0:T(8,128)(2,1)S(1)}) custom-call(s32[4]{0:T(128)S(1)} %pad_add_fusion.1.scalars, bf16[416,768]{1,0:T(8,128)(2,1)S(1)} %copy-done.28, bf16[416,2304]{1,0:T(8,128)(2,1)S(1)} %get-tuple-element.225.refs_1_, bf16[416,768]{1,0:T(8,128)(2,1)S(1)} %copy-done.30, ...), custom_call_target="tpu_custom_call" | custom-call | flops 16632000512 | bytes 1024 | tf_op jit(solution)/shard_map/space_grad/pallas_call | solution.py:493
  154.1 5.3 %time_projections.1 = (bf16[416,768]{1,0:T(8,128)(2,1)S(1)}, bf16[416,768]{1,0:T(8,128)(2,1)S(1)}, bf16[416,768]{1,0:T(8,128)(2,1)S(1)}, f32[8,768]{1,0:T(8,128)S(1)}) custom-call(s32[4]{0:T(128)S(1)} %pad_add_fusion.1.scalars, bf16[104,768]{1,0:T(8,128)(2,1)S(1)} %get-tuple-element.238.r0, bf16[104,768]{1,0:T(8,128)(2,1)S(1)} %collective-permute-done.26.r1, ...), custom_call_target="tpu_custom_call" | custom-call | flops 15399999488 | bytes 1024 | tf_op jit(solution)/shard_map/time_projections/pallas_call | solution.py:493
  162.1 11.9 %time_back.1 = (bf16[416,2304]{1,0:T(8,128)(2,1)S(1)}, f32[8,768]{1,0:T(8,128)S(1)}, bf16[104,768]{1,0:T(8,128)(2,1)S(1)}, bf16[104,768]{1,0:T(8,128)(2,1)S(1)},...) custom-call(s32[4]{0:T(128)S(1)} %pad_add_fusion.1.scalars, f32[24,768]{1,0:T(8,128)S(1)} %table.1.vec, ...), custom_call_target="tpu_custom_call" | custom-call | flops 28600000512 | bytes 1024 | tf_op jit(solution)/shard_map/time_back/pallas_call | solution.py:493
  174.1 6.4 %collective-permute-done.29.got = bf16[2,384,768]{2,1,0:T(8,128)(2,1)S(1)} collective-permute-done((bf16[2,384,768]{2,1,0:T(8,128)(2,1)S(1)}, bf16[2,384,768]{2,1,0:T(8,128)(2,1)S(1)}, u32[]{:S(2)}, u32[]{:S(2)}) %collective-permute-start.29) | collective-permute-done | bytes 1179680 | tf_op jit(solution)/shard_map/ppermute | solution.py:771
  186.4 3.3 %time_grad.1 = (bf16[2,640,768]{2,1,0:T(8,128)(2,1)S(1)}, bf16[2,640,768]{2,1,0:T(8,128)(2,1)S(1)}) custom-call(s32[4]{0:T(128)S(1)} %pad_add_fusion.1.scalars, bf16[416,768]{1,0:T(8,128)(2,1)S(1)} %copy-done.26, bf16[416,2304]{1,0:T(8,128)(2,1)S(1)} %get-tuple-element.264.refs_1_, f32[8,768]{1,0:T(8,128)S(1)} %get-tuple-element.265.refs_2_, ...), custom_call_target="tpu_custom_call" | custom-call | flops 15693333504 | bytes 1024 | tf_op jit(solution)/shard_map/time_grad/pallas_call | solution.py:493
  191.1 8.6 %collective-permute-done.30.got = bf16[2,192,768]{2,1,0:T(8,128)(2,1)S(1)} collective-permute-done((bf16[2,192,768]{2,1,0:T(8,128)(2,1)S(1)}, bf16[2,192,768]{2,1,0:T(8,128)(2,1)S(1)}, u32[]{:S(2)}, u32[]{:S(2)}) %collective-permute-start.30) | collective-permute-done | bytes 589856 | tf_op jit(solution)/shard_map/ppermute | solution.py:771
  204.9 5.5 %collective-permute-done.34.got = bf16[192,768]{1,0:T(8,128)(2,1)S(1)} collective-permute-done((bf16[192,768]{1,0:T(8,128)(2,1)S(1)}, bf16[192,768]{1,0:T(8,128)(2,1)S(1)}, u32[]{:S(2)}, u32[]{:S(2)}) %collective-permute-start.34) | collective-permute-done | bytes 294944 | tf_op jit(solution)/shard_map/ppermute | solution.py:771
  217.2 7.7 %collective-permute-done.37 = bf16[96,768]{1,0:T(8,128)(2,1)S(1)} collective-permute-done((bf16[96,768]{1,0:T(8,128)(2,1)S(1)}, bf16[96,768]{1,0:T(8,128)(2,1)S(1)}, u32[]{:S(2)}, u32[]{:S(2)}) %collective-permute-start.37) | collective-permute-done | bytes 147488 | tf_op jit(solution)/shard_map/ppermute | solution.py:771
  244.9 3.0 collective-permute-done.44.other
  248.5 4.9 %collective-permute-done.50.got = bf16[160,768]{1,0:T(8,128)(2,1)S(1)} collective-permute-done((bf16[160,768]{1,0:T(8,128)(2,1)S(1)}, bf16[160,768]{1,0:T(8,128)(2,1)S(1)}, u32[]{:S(2)}, u32[]{:S(2)}) %collective-permute-start.50) | collective-permute-done | bytes 245792 | tf_op jit(solution)/shard_map/ppermute | solution.py:771
  272.1 3.6 %collective-permute-done.58.r2 = bf16[104,768]{1,0:T(8,128)(2,1)S(1)} collective-permute-done((bf16[104,768]{1,0:T(8,128)(2,1)S(1)}, bf16[104,768]{1,0:T(8,128)(2,1)S(1)}, u32[]{:S(2)}, u32[]{:S(2)}) %collective-permute-start.58) | collective-permute-done | bytes 159776 | tf_op jit(solution)/shard_map/ppermute | solution.py:771
  289.2 6.3 %collective-permute-done.67.other = bf16[384,768]{1,0:T(8,128)(2,1)S(1)} collective-permute-done((bf16[384,768]{1,0:T(8,128)(2,1)S(1)}, bf16[384,768]{1,0:T(8,128)(2,1)S(1)}, u32[]{:S(2)}, u32[]{:S(2)}) %collective-permute-start.67) | collective-permute-done | bytes 589856 | tf_op jit(solution)/shard_map/ppermute | solution.py:771
  (260 shorter events, 128.1 us)
Async XLA Ops:
  16.2 22.3 %collective-permute-start.3 = (bf16[3288,768]{1,0:T(8,128)(2,1)S(1)}, bf16[3288,768]{1,0:T(8,128)(2,1)S(1)}, u32[]{:S(2)}, u32[]{:S(2)}) collective-permute-start(bf16[3288,768]{1,0:T(8,128)(2,1)S(1)} %get-tuple-element.186), channel_id=1, source_target_pairs={{0,8},{8,0},{16,24},{24,16},{1,9},{9,1},{17,25},{25,17},{2,10},{10... | collective-permute-start | bytes 15151112 | tf_op jit(solution)/shard_map/ppermute | solution.py:771
  17.9 17.1 %collective-permute-start.4 = (bf16[408,768]{1,0:T(8,128)(2,1)S(1)}, bf16[408,768]{1,0:T(8,128)(2,1)S(1)}, u32[]{:S(2)}, u32[]{:S(2)}) collective-permute-start(bf16[408,768]{1,0:T(8,128)(2,1)S(1)} %pack_time.1), channel_id=1, source_target_pairs={{0,16},{8,24},{16,0},{24,8},{1,17},{9,25},{17,1},{25,9},{2,18},{10... | collective-permute-start | bytes 1880072 | tf_op jit(solution)/shard_map/ppermute | solution.py:771
  35.0 18.9 %collective-permute-start.6 = (bf16[480,768]{1,0:T(8,128)(2,1)S(1)}, bf16[480,768]{1,0:T(8,128)(2,1)S(1)}, u32[]{:S(2)}, u32[]{:S(2)}) collective-permute-start(bf16[480,768]{1,0:T(8,128)(2,1)S(1)} %get-tuple-element.191), channel_id=1, source_target_pairs={{0,16},{8,24},{16,0},{24,8},{1,17},{9,25},{17,1},{25,9},{2,18},{10... | collective-permute-start | bytes 2211848 | tf_op jit(solution)/shard_map/ppermute | solution.py:771
  54.0 21.5 %collective-permute-start.7 = (bf16[384,768]{1,0:T(8,128)(2,1)S(1)}, bf16[384,768]{1,0:T(8,128)(2,1)S(1)}, u32[]{:S(2)}, u32[]{:S(2)}) collective-permute-start(bf16[384,768]{1,0:T(8,128)(2,1)S(1)} %get-tuple-element.192), channel_id=1, source_target_pairs={{0,16},{8,24},{16,0},{24,8},{1,17},{9,25},{17,1},{25,9},{2,18},{10... | collective-permute-start | bytes 1769480 | tf_op jit(solution)/shard_map/ppermute | solution.py:771
  55.7 27.0 %collective-permute-start.8 = (bf16[384,768]{1,0:T(8,128)(2,1)S(1)}, bf16[384,768]{1,0:T(8,128)(2,1)S(1)}, u32[]{:S(2)}, u32[]{:S(2)}) collective-permute-start(bf16[384,768]{1,0:T(8,128)(2,1)S(1)} %get-tuple-element.194), channel_id=1, source_target_pairs={{0,16},{8,24},{16,0},{24,8},{1,17},{9,25},{17,1},{25,9},{2,18},{10... | collective-permute-start | bytes 1769480 | tf_op jit(solution)/shard_map/ppermute | solution.py:771
  56.0 26.9 %collective-permute-start.15 = (bf16[480,768]{1,0:T(8,128)(2,1)S(1)}, bf16[480,768]{1,0:T(8,128)(2,1)S(1)}, u32[]{:S(2)}, u32[]{:S(2)}) collective-permute-start(bf16[480,768]{1,0:T(8,128)(2,1)S(1)} %collective-permute-done.6.refs_4_.refs_3_), channel_id=1, source_target_pairs={{0,8},{8,0},{16,24},{24,16},{1,9},{9,1},{17,25},{25,17},{2,10},{10... | collective-permute-start | bytes 2211848 | tf_op jit(solution)/shard_map/ppermute | solution.py:771
  56.0 18.9 %collective-permute-start.14 = (bf16[480,768]{1,0:T(8,128)(2,1)S(1)}, bf16[480,768]{1,0:T(8,128)(2,1)S(1)}, u32[]{:S(2)}, u32[]{:S(2)}) collective-permute-start(bf16[480,768]{1,0:T(8,128)(2,1)S(1)} %collective-permute-done.6.refs_4_.refs_3_), channel_id=1, source_target_pairs={{0,1},{1,0},{2,3},{3,2},{4,5},{5,4},{6,7},{7,6},{8,9},{9,8},{10,11... | collective-permute-start | bytes 2211848 | tf_op jit(solution)/shard_map/ppermute | solution.py:771
  82.9 21.7 %collective-permute-start.18 = (bf16[384,768]{1,0:T(8,128)(2,1)S(1)}, bf16[384,768]{1,0:T(8,128)(2,1)S(1)}, u32[]{:S(2)}, u32[]{:S(2)}) collective-permute-start(bf16[384,768]{1,0:T(8,128)(2,1)S(1)} %collective-permute-done.7.refs_3_), channel_id=1, source_target_pairs={{0,8},{8,0},{16,24},{24,16},{1,9},{9,1},{17,25},{25,17},{2,10},{10... | collective-permute-start | bytes 1769480 | tf_op jit(solution)/shard_map/ppermute | solution.py:771
  84.9 17.5 %collective-permute-start.17 = (bf16[384,768]{1,0:T(8,128)(2,1)S(1)}, bf16[384,768]{1,0:T(8,128)(2,1)S(1)}, u32[]{:S(2)}, u32[]{:S(2)}) collective-permute-start(bf16[384,768]{1,0:T(8,128)(2,1)S(1)} %collective-permute-done.7.refs_3_), channel_id=1, source_target_pairs={{0,1},{1,0},{2,3},{3,2},{4,5},{5,4},{6,7},{7,6},{8,9},{9,8},{10,11... | collective-permute-start | bytes 1769480 | tf_op jit(solution)/shard_map/ppermute | solution.py:771
  125.4 20.2 %collective-permute-start.25 = (bf16[2,768,768]{2,1,0:T(8,128)(2,1)S(1)}, bf16[2,768,768]{2,1,0:T(8,128)(2,1)S(1)}, u32[]{:S(2)}, u32[]{:S(2)}) collective-permute-start(bf16[2,768,768]{2,1,0:T(8,128)(2,1)S(1)} %get-tuple-element.231), channel_id=1, source_target_pairs={{0,8},{8,0},{16,24},{24,16},{1,9},{9,1},{17,25},{25,17},{2,10},{10... | collective-permute-start | bytes 7077896 | tf_op jit(solution)/shard_map/ppermute | solution.py:771
  148.7 32.7 %collective-permute-start.33 = (bf16[2,384,768]{2,1,0:T(8,128)(2,1)S(1)}, bf16[2,384,768]{2,1,0:T(8,128)(2,1)S(1)}, u32[]{:S(2)}, u32[]{:S(2)}) collective-permute-start(bf16[2,384,768]{2,1,0:T(8,128)(2,1)S(1)} %get-tuple-element.235), channel_id=1, source_target_pairs={{0,2},{1,3},{2,0},{3,1},{4,6},{5,7},{6,4},{7,5},{8,10},{9,11},{10,... | collective-permute-start | bytes 3538952 | tf_op jit(solution)/shard_map/ppermute | solution.py:771
  151.8 30.4 %collective-permute-start.32 = (bf16[768,768]{1,0:T(8,128)(2,1)S(1)}, bf16[768,768]{1,0:T(8,128)(2,1)S(1)}, u32[]{:S(2)}, u32[]{:S(2)}) collective-permute-start(bf16[768,768]{1,0:T(8,128)(2,1)S(1)} %get-tuple-element.237), channel_id=1, source_target_pairs={{0,16},{8,24},{16,0},{24,8},{1,17},{9,25},{17,1},{25,9},{2,18},{10... | collective-permute-start | bytes 3538952 | tf_op jit(solution)/shard_map/ppermute | solution.py:771
  152.5 27.9 %collective-permute-start.29 = (bf16[2,384,768]{2,1,0:T(8,128)(2,1)S(1)}, bf16[2,384,768]{2,1,0:T(8,128)(2,1)S(1)}, u32[]{:S(2)}, u32[]{:S(2)}) collective-permute-start(bf16[2,384,768]{2,1,0:T(8,128)(2,1)S(1)} %get-tuple-element.233), channel_id=1, source_target_pairs={{0,1},{1,0},{2,3},{3,2},{4,5},{5,4},{6,7},{7,6},{8,9},{9,8},{10,11... | collective-permute-start | bytes 3538952 | tf_op jit(solution)/shard_map/ppermute | solution.py:771
  161.7 28.1 %collective-permute-start.31 = (bf16[2,384,768]{2,1,0:T(8,128)(2,1)S(1)}, bf16[2,384,768]{2,1,0:T(8,128)(2,1)S(1)}, u32[]{:S(2)}, u32[]{:S(2)}) collective-permute-start(bf16[2,384,768]{2,1,0:T(8,128)(2,1)S(1)} %get-tuple-element.256), channel_id=1, source_target_pairs={{0,8},{8,0},{16,24},{24,16},{1,9},{9,1},{17,25},{25,17},{2,10},{10... | collective-permute-start | bytes 3538952 | tf_op jit(solution)/shard_map/ppermute | solution.py:771
  183.1 20.5 %collective-permute-start.35 = (bf16[384,768]{1,0:T(8,128)(2,1)S(1)}, bf16[384,768]{1,0:T(8,128)(2,1)S(1)}, u32[]{:S(2)}, u32[]{:S(2)}) collective-permute-start(bf16[384,768]{1,0:T(8,128)(2,1)S(1)} %get-tuple-element.263), channel_id=1, source_target_pairs={{0,1},{1,0},{2,3},{3,2},{4,5},{5,4},{6,7},{7,6},{8,9},{9,8},{10,11... | collective-permute-start | bytes 1769480 | tf_op jit(solution)/shard_map/ppermute | solution.py:771
  184.7 29.0 %collective-permute-start.39 = (bf16[384,768]{1,0:T(8,128)(2,1)S(1)}, bf16[384,768]{1,0:T(8,128)(2,1)S(1)}, u32[]{:S(2)}, u32[]{:S(2)}) collective-permute-start(bf16[384,768]{1,0:T(8,128)(2,1)S(1)} %get-tuple-element.261), channel_id=1, source_target_pairs={{0,16},{8,24},{16,0},{24,8},{1,17},{9,25},{17,1},{25,9},{2,18},{10... | collective-permute-start | bytes 1769480 | tf_op jit(solution)/shard_map/ppermute | solution.py:771
  190.7 39.7 %collective-permute-start.41 = (bf16[2,192,768]{2,1,0:T(8,128)(2,1)S(1)}, bf16[2,192,768]{2,1,0:T(8,128)(2,1)S(1)}, u32[]{:S(2)}, u32[]{:S(2)}) collective-permute-start(bf16[2,192,768]{2,1,0:T(8,128)(2,1)S(1)} %get-tuple-element.270), channel_id=1, source_target_pairs={{0,1},{1,0},{2,3},{3,2},{4,5},{5,4},{6,7},{7,6},{8,9},{9,8},{10,11... | collective-permute-start | bytes 1769480 | tf_op jit(solution)/shard_map/ppermute | solution.py:771
  202.5 26.1 %collective-permute-start.42 = (bf16[640,768]{1,0:T(8,128)(2,1)S(1)}, bf16[640,768]{1,0:T(8,128)(2,1)S(1)}, u32[]{:S(2)}, u32[]{:S(2)}) collective-permute-start(bf16[640,768]{1,0:T(8,128)(2,1)S(1)} %get-tuple-element.277), channel_id=1, source_target_pairs={{0,16},{8,24},{16,0},{24,8},{1,17},{9,25},{17,1},{25,9},{2,18},{10... | collective-permute-start | bytes 2949128 | tf_op jit(solution)/shard_map/ppermute | solution.py:771
  215.6 17.9 %collective-permute-start.48 = (bf16[96,768]{1,0:T(8,128)(2,1)S(1)}, bf16[96,768]{1,0:T(8,128)(2,1)S(1)}, u32[]{:S(2)}, u32[]{:S(2)}) collective-permute-start(bf16[96,768]{1,0:T(8,128)(2,1)S(1)} %get-tuple-element.288), channel_id=1, source_target_pairs={{0,4},{1,5},{2,6},{3,7},{4,0},{5,1},{6,2},{7,3},{8,12},{9,13},{10,... | collective-permute-start | bytes 442376 | tf_op jit(solution)/shard_map/ppermute | solution.py:771
  233.5 20.6 %collective-permute-start.54 = (bf16[96,768]{1,0:T(8,128)(2,1)S(1)}, bf16[96,768]{1,0:T(8,128)(2,1)S(1)}, u32[]{:S(2)}, u32[]{:S(2)}) collective-permute-start(bf16[96,768]{1,0:T(8,128)(2,1)S(1)} %add_convert_fusion.1.mine), channel_id=1, source_target_pairs={{0,4},{1,5},{2,6},{3,7},{4,0},{5,1},{6,2},{7,3},{8,12},{9,13},{10,... | collective-permute-start | bytes 442376 | tf_op jit(solution)/shard_map/ppermute | solution.py:771
  239.9 16.8 %collective-permute-start.53 = (bf16[96,768]{1,0:T(8,128)(2,1)S(1)}, bf16[96,768]{1,0:T(8,128)(2,1)S(1)}, u32[]{:S(2)}, u32[]{:S(2)}) collective-permute-start(bf16[96,768]{1,0:T(8,128)(2,1)S(1)} %add_convert_fusion.mine), channel_id=1, source_target_pairs={{0,4},{1,5},{2,6},{3,7},{4,0},{5,1},{6,2},{7,3},{8,12},{9,13},{10,... | collective-permute-start | bytes 442376 | tf_op jit(solution)/shard_map/ppermute | solution.py:771
  257.3 20.1 %collective-permute-start.65 = (bf16[192,768]{1,0:T(8,128)(2,1)S(1)}, bf16[192,768]{1,0:T(8,128)(2,1)S(1)}, u32[]{:S(2)}, u32[]{:S(2)}) collective-permute-start(bf16[192,768]{1,0:T(8,128)(2,1)S(1)} %join.13.mine), channel_id=1, source_target_pairs={{0,1},{1,0},{2,3},{3,2},{4,5},{5,4},{6,7},{7,6},{8,9},{9,8},{10,11... | collective-permute-start | bytes 884744 | tf_op jit(solution)/shard_map/ppermute | solution.py:771
  278.1 17.4 %collective-permute-start.67 = (bf16[384,768]{1,0:T(8,128)(2,1)S(1)}, bf16[384,768]{1,0:T(8,128)(2,1)S(1)}, u32[]{:S(2)}, u32[]{:S(2)}) collective-permute-start(bf16[384,768]{1,0:T(8,128)(2,1)S(1)} %join.17.mine), channel_id=1, source_target_pairs={{0,2},{1,3},{2,0},{3,1},{4,6},{5,7},{6,4},{7,5},{8,10},{9,11},{10,... | collective-permute-start | bytes 1769480 | tf_op jit(solution)/shard_map/ppermute | solution.py:771
  281.3 16.3 %collective-permute-start.66 = (bf16[320,768]{1,0:T(8,128)(2,1)S(1)}, bf16[320,768]{1,0:T(8,128)(2,1)S(1)}, u32[]{:S(2)}, u32[]{:S(2)}) collective-permute-start(bf16[320,768]{1,0:T(8,128)(2,1)S(1)} %join.18.mine), channel_id=1, source_target_pairs={{0,1},{1,0},{2,3},{3,2},{4,5},{5,4},{6,7},{7,6},{8,9},{9,8},{10,11... | collective-permute-start | bytes 1474568 | tf_op jit(solution)/shard_map/ppermute | solution.py:771
  (82 other events, 890.0 us)

commit v6 on v5

--- a/solution.py
+++ b/solution.py
@@ -499,7 +499,7 @@
         scratch_shapes=scratch,
         compiler_params=pltpu.CompilerParams(vmem_limit_bytes=LIMITS.get(name, 5) << 20),
         cost_estimate=pl.CostEstimate(
-            flops=int((microseconds + 10) * 1.1e9), transcendentals=0,
+            flops=int((microseconds + 8) * 1.1e9), transcendentals=0,
             bytes_accessed=1024,
         ),
     )(*operands)

time: 309 us -> 319 us (1.032)
  starting transfers between devices: 63 us -> 70.7 us
  local copies, waits for them, and re-layouts: 9.15 us -> 12.5 us
    ppermute x69, starting transfers between devices: 63 us -> 70.7 us  [flip(): return lax.ppermute(array, axis, [(at, at ^ bit) for at in range(size)])]
    unnamed x78 -> x76, local copies, waits for them, and re-layouts: 4.86 us -> 8.2 us
  transfers between devices with their start and end apart: 69 -> 69, of which waited for: 26 -> 24; matrix products, arithmetic and copies ran while one was open for 3% -> 2% of each run, Pallas kernels for 31% -> 31%
where the time goes in v6:
time: 319 us; the launch traced here: 313 us
  Pallas kernels  120 us (38%)
  waiting for transfers between devices  105 us (33%)
  starting transfers between devices  70.7 us (22%)
  local copies, waits for them, and re-layouts  12.5 us (4%)
    pallas_call x48, Pallas kernels, call(): pl.pallas_call(kernel, name=name, out_shape=outs, in_specs=specs, out_spe...  114 us
    ppermute x69, waiting for transfers between devices, flip(): return lax.ppermute(array, axis, [(at, at ^ bit) for at in range(size)])  105 us
    ppermute x69, starting transfers between devices, flip(): return lax.ppermute(array, axis, [(at, at ^ bit) for at in range(size)])  70.7 us
    unnamed x76, local copies, waits for them, and re-layouts  8.2 us
  transfers between devices with their start and end apart: 69, of which 24 were waited for; matrix products, arithmetic and copies ran while one was open for 2% of the time, Pallas kernels for 31%

profile of v6, /device:TPU:0, one launch (start us, length us, event | category | flops | bytes accessed | tf_op | source)
XLA Modules:
  0.0 312.6 jit_solution(8164121419917445307)
XLA Ops:
  9.0 3.4 %collective-permute-done.1 = bf16[49,2,768]{2,1,0:T(2,128)(2,1)S(1)} collective-permute-done((bf16[49,2,768]{2,1,0:T(2,128)(2,1)S(1)}, bf16[49,2,768]{2,1,0:T(2,128)(2,1)S(1)}, u32[]{:S(2)}, u32[]{:S(2)}) %collective-permute-start.1) | collective-permute-done | bytes 150560 | tf_op jit(solution)/shard_map/ppermute | solution.py:771
  12.4 3.8 %pack_rest.1 = (bf16[3288,768]{1,0:T(8,128)(2,1)S(1)}, bf16[480,768]{1,0:T(8,128)(2,1)S(1)}, bf16[384,768]{1,0:T(8,128)(2,1)S(1)}, bf16[384,768]{1,0:T(8,128)(2,1)S(1)}) custom-call(s32[4]{0:T(128)S(1)} %pad_add_fusion.1.scalars, bf16[192,2304]{1,0:T(8,128)(2,1)} %own_qkv.1, bf16[192,768]{1,0:T(8,128)(2,1)} %refs_1_.9, bf16[192,768]{1,0:T(8,128)(2,1)} %refs_0_.9, ...), custom_call_target="tpu_custom_call" | custom-call | flops 11000000512 | bytes 1024 | tf_op jit(solution)/shard_map/pack_rest/pallas_call | solution.py:685
  20.3 14.7 %collective-permute-done.4.direct.refs_3_.refs_7_.refs_1_ = bf16[408,768]{1,0:T(8,128)(2,1)S(1)} collective-permute-done((bf16[408,768]{1,0:T(8,128)(2,1)S(1)}, bf16[408,768]{1,0:T(8,128)(2,1)S(1)}, u32[]{:S(2)}, u32[]{:S(2)}) %collective-permute-start.4) | collective-permute-done | bytes 626720 | tf_op jit(solution)/shard_map/ppermute | solution.py:771
  39.3 13.7 %collective-permute-done.9.refs_4_.refs_8_.refs_2_ = bf16[408,768]{1,0:T(8,128)(2,1)S(1)} collective-permute-done((bf16[408,768]{1,0:T(8,128)(2,1)S(1)}, bf16[408,768]{1,0:T(8,128)(2,1)S(1)}, u32[]{:S(2)}, u32[]{:S(2)}) %collective-permute-start.9) | collective-permute-done | bytes 626720 | tf_op jit(solution)/shard_map/ppermute | solution.py:771
  57.8 9.4 %place_forward.1 = (bf16[416,768]{1,0:T(8,128)(2,1)S(1)}, bf16[416,2304]{1,0:T(8,128)(2,1)S(1)}, bf16[416,768]{1,0:T(8,128)(2,1)S(1)}, bf16[416,768]{1,0:T(8,128...) custom-call(s32[4]{0:T(128)S(1)} %pad_add_fusion.1.scalars, ...), custom_call_target="tpu_custom_call" | custom-call | flops 20899999744 | bytes 1024 | tf_op jit(solution)/shard_map/place_forward/pallas_call | solution.py:493
  69.4 5.5 %collective-permute-done.14.refs_5_.refs_4_ = bf16[480,768]{1,0:T(8,128)(2,1)S(1)} collective-permute-done((bf16[480,768]{1,0:T(8,128)(2,1)S(1)}, bf16[480,768]{1,0:T(8,128)(2,1)S(1)}, u32[]{:S(2)}, u32[]{:S(2)}) %collective-permute-start.14) | collective-permute-done | bytes 737312 | tf_op jit(solution)/shard_map/ppermute | solution.py:771
  77.2 5.6 %collective-permute-done.8.refs_7_ = bf16[384,768]{1,0:T(8,128)(2,1)S(1)} collective-permute-done((bf16[384,768]{1,0:T(8,128)(2,1)S(1)}, bf16[384,768]{1,0:T(8,128)(2,1)S(1)}, u32[]{:S(2)}, u32[]{:S(2)}) %collective-permute-start.8) | collective-permute-done | bytes 589856 | tf_op jit(solution)/shard_map/ppermute | solution.py:771
  88.9 12.6 %frame_forward.1 = (f32[416,768]{1,0:T(8,128)S(1)}, bf16[416,768]{1,0:T(8,128)(2,1)S(1)}, bf16[416,2304]{1,0:T(8,128)(2,1)S(1)}, bf16[416,768]{1,0:T(8,128)(2,1)...) custom-call(s32[4]{0:T(128)S(1)} %pad_add_fusion.1.scalars, bf16[416,768]{1,0:T(8,128)(2,1)S(1)} %bitcast.42, ...), custom_call_target="tpu_custom_call" | custom-call | flops 23100000256 | bytes 1024 | tf_op jit(solution)/shard_map/frame_forward/pallas_call | solution.py:493
  108.1 12.4 %mlp_both.1 = (bf16[416,768]{1,0:T(8,128)(2,1)S(1)}, bf16[416,3072]{1,0:T(8,128)(2,1)S(1)}, bf16[416,3072]{1,0:T(8,128)(2,1)S(1)}, bf16[416,768]{1,0:T(8,128)(2,...) custom-call(s32[4]{0:T(128)S(1)} %pad_add_fusion.1.scalars, f32[1,1]{1,0:T(1,128)} %bitcast.4.live, ...), custom_call_target="tpu_custom_call" | custom-call | flops 28600000512 | bytes 1024 | tf_op jit(solution)/shard_map/mlp_both/pallas_call | solution.py:493
  120.5 3.2 %mlp_out_grad.1 = (bf16[2,768,768]{2,1,0:T(8,128)(2,1)S(1)}, bf16[2,768,768]{2,1,0:T(8,128)(2,1)S(1)}) custom-call(s32[4]{0:T(128)S(1)} %pad_add_fusion.1.scalars, bf16[416,3072]{1,0:T(8,128)(2,1)S(1)} %get-tuple-element.212.refs_0_, bf16[416,768]{1,0:T(8,128)(2,1)S(1)} %get-tuple-element.213.refs_1_), custom_call_target="tpu_custom_call" | custom-call | flops 14432000000 | bytes 1024 | tf_op jit(solution)/shard_map/mlp_out_grad/pallas_call | solution.py:493
  123.8 3.5 %mlp_in_grad.1 = (bf16[2,768,768]{2,1,0:T(8,128)(2,1)S(1)}, bf16[2,768,768]{2,1,0:T(8,128)(2,1)S(1)}) custom-call(s32[4]{0:T(128)S(1)} %pad_add_fusion.1.scalars, bf16[416,768]{1,0:T(8,128)(2,1)S(1)} %get-tuple-element.205.h3.refs_0_, bf16[416,3072]{1,0:T(8,128)(2,1)S(1)} %get-tuple-element.215.refs_1_), custom_call_target="tpu_custom_call" | custom-call | flops 14432000000 | bytes 1024 | tf_op jit(solution)/shard_map/mlp_in_grad/pallas_call | solution.py:493
  127.8 13.1 %space_back.1 = (bf16[416,2304]{1,0:T(8,128)(2,1)S(1)}, f32[416,768]{1,0:T(8,128)S(1)}, bf16[416,768]{1,0:T(8,128)(2,1)S(1)}, f32[8,768]{1,0:T(8,128)S(1)}, bf16...) custom-call(s32[4]{0:T(128)S(1)} %pad_add_fusion.1.scalars, ...), custom_call_target="tpu_custom_call" | custom-call | flops 30799998976 | bytes 1024 | tf_op jit(solution)/shard_map/space_back/pallas_call | solution.py:493
  141.1 3.3 %space_grad.1 = (bf16[2,768,768]{2,1,0:T(8,128)(2,1)S(1)}, bf16[2,768,768]{2,1,0:T(8,128)(2,1)S(1)}) custom-call(s32[4]{0:T(128)S(1)} %pad_add_fusion.1.scalars, bf16[416,768]{1,0:T(8,128)(2,1)S(1)} %copy-done.27, bf16[416,2304]{1,0:T(8,128)(2,1)S(1)} %get-tuple-element.225.refs_1_, bf16[416,768]{1,0:T(8,128)(2,1)S(1)} %copy-done.29, ...), custom_call_target="tpu_custom_call" | custom-call | flops 14432000000 | bytes 1024 | tf_op jit(solution)/shard_map/space_grad/pallas_call | solution.py:493
  154.6 5.3 %time_projections.1 = (bf16[416,768]{1,0:T(8,128)(2,1)S(1)}, bf16[416,768]{1,0:T(8,128)(2,1)S(1)}, bf16[416,768]{1,0:T(8,128)(2,1)S(1)}, f32[8,768]{1,0:T(8,128)S(1)}) custom-call(s32[4]{0:T(128)S(1)} %pad_add_fusion.1.scalars, bf16[104,768]{1,0:T(8,128)(2,1)S(1)} %get-tuple-element.238.r0, bf16[104,768]{1,0:T(8,128)(2,1)S(1)} %collective-permute-done.26.r1, ...), custom_call_target="tpu_custom_call" | custom-call | flops 13200000000 | bytes 1024 | tf_op jit(solution)/shard_map/time_projections/pallas_call | solution.py:493
  162.6 12.0 %time_back.1 = (bf16[416,2304]{1,0:T(8,128)(2,1)S(1)}, f32[8,768]{1,0:T(8,128)S(1)}, bf16[104,768]{1,0:T(8,128)(2,1)S(1)}, bf16[104,768]{1,0:T(8,128)(2,1)S(1)},...) custom-call(s32[4]{0:T(128)S(1)} %pad_add_fusion.1.scalars, f32[24,768]{1,0:T(8,128)S(1)} %table.1.vec, ...), custom_call_target="tpu_custom_call" | custom-call | flops 26400000000 | bytes 1024 | tf_op jit(solution)/shard_map/time_back/pallas_call | solution.py:493
  174.6 6.4 %collective-permute-done.29.got = bf16[2,384,768]{2,1,0:T(8,128)(2,1)S(1)} collective-permute-done((bf16[2,384,768]{2,1,0:T(8,128)(2,1)S(1)}, bf16[2,384,768]{2,1,0:T(8,128)(2,1)S(1)}, u32[]{:S(2)}, u32[]{:S(2)}) %collective-permute-start.29) | collective-permute-done | bytes 1179680 | tf_op jit(solution)/shard_map/ppermute | solution.py:771
  183.8 3.3 %time_grad.1 = (bf16[2,640,768]{2,1,0:T(8,128)(2,1)S(1)}, bf16[2,640,768]{2,1,0:T(8,128)(2,1)S(1)}) custom-call(s32[4]{0:T(128)S(1)} %pad_add_fusion.1.scalars, bf16[416,768]{1,0:T(8,128)(2,1)S(1)} %copy-done.25, bf16[416,2304]{1,0:T(8,128)(2,1)S(1)} %get-tuple-element.264.refs_1_, f32[8,768]{1,0:T(8,128)S(1)} %get-tuple-element.265.refs_2_, ...), custom_call_target="tpu_custom_call" | custom-call | flops 13493332992 | bytes 1024 | tf_op jit(solution)/shard_map/time_grad/pallas_call | solution.py:493
  193.0 13.4 %collective-permute-done.30.got = bf16[2,192,768]{2,1,0:T(8,128)(2,1)S(1)} collective-permute-done((bf16[2,192,768]{2,1,0:T(8,128)(2,1)S(1)}, bf16[2,192,768]{2,1,0:T(8,128)(2,1)S(1)}, u32[]{:S(2)}, u32[]{:S(2)}) %collective-permute-start.30) | collective-permute-done | bytes 589856 | tf_op jit(solution)/shard_map/ppermute | solution.py:771
  211.7 5.5 %collective-permute-done.34.got = bf16[192,768]{1,0:T(8,128)(2,1)S(1)} collective-permute-done((bf16[192,768]{1,0:T(8,128)(2,1)S(1)}, bf16[192,768]{1,0:T(8,128)(2,1)S(1)}, u32[]{:S(2)}, u32[]{:S(2)}) %collective-permute-start.34) | collective-permute-done | bytes 294944 | tf_op jit(solution)/shard_map/ppermute | solution.py:771
  224.3 8.6 %collective-permute-done.37 = bf16[96,768]{1,0:T(8,128)(2,1)S(1)} collective-permute-done((bf16[96,768]{1,0:T(8,128)(2,1)S(1)}, bf16[96,768]{1,0:T(8,128)(2,1)S(1)}, u32[]{:S(2)}, u32[]{:S(2)}) %collective-permute-start.37) | collective-permute-done | bytes 147488 | tf_op jit(solution)/shard_map/ppermute | solution.py:771
  244.0 4.5 %collective-permute-done.47.got = bf16[320,768]{1,0:T(8,128)(2,1)S(1)} collective-permute-done((bf16[320,768]{1,0:T(8,128)(2,1)S(1)}, bf16[320,768]{1,0:T(8,128)(2,1)S(1)}, u32[]{:S(2)}, u32[]{:S(2)}) %collective-permute-start.47) | collective-permute-done | bytes 491552 | tf_op jit(solution)/shard_map/ppermute | solution.py:771
  255.6 4.3 %collective-permute-start.49 = (bf16[384,768]{1,0:T(8,128)(2,1)S(1)}, bf16[384,768]{1,0:T(8,128)(2,1)S(1)}, u32[]{:S(2)}, u32[]{:S(2)}) collective-permute-start(bf16[384,768]{1,0:T(8,128)(2,1)S(1)} %join.11.mine), channel_id=1, source_target_pairs={{0,1},{1,0},{2,3},{3,2},{4,5},{5,4},{6,7},{7,6},{8,9},{9,8},{10,11... | collective-permute-start | bytes 1769480 | tf_op jit(solution)/shard_map/ppermute | solution.py:771
  281.4 4.2 %collective-permute-done.58.r2 = bf16[104,768]{1,0:T(8,128)(2,1)S(1)} collective-permute-done((bf16[104,768]{1,0:T(8,128)(2,1)S(1)}, bf16[104,768]{1,0:T(8,128)(2,1)S(1)}, u32[]{:S(2)}, u32[]{:S(2)}) %collective-permute-start.58) | collective-permute-done | bytes 159776 | tf_op jit(solution)/shard_map/ppermute | solution.py:771
  299.1 5.8 %collective-permute-done.67.other = bf16[384,768]{1,0:T(8,128)(2,1)S(1)} collective-permute-done((bf16[384,768]{1,0:T(8,128)(2,1)S(1)}, bf16[384,768]{1,0:T(8,128)(2,1)S(1)}, u32[]{:S(2)}, u32[]{:S(2)}) %collective-permute-start.67) | collective-permute-done | bytes 589856 | tf_op jit(solution)/shard_map/ppermute | solution.py:771
  (258 shorter events, 132.0 us)
Async XLA Ops:
  16.2 22.3 %collective-permute-start.3 = (bf16[3288,768]{1,0:T(8,128)(2,1)S(1)}, bf16[3288,768]{1,0:T(8,128)(2,1)S(1)}, u32[]{:S(2)}, u32[]{:S(2)}) collective-permute-start(bf16[3288,768]{1,0:T(8,128)(2,1)S(1)} %get-tuple-element.186), channel_id=1, source_target_pairs={{0,8},{8,0},{16,24},{24,16},{1,9},{9,1},{17,25},{25,17},{2,10},{10... | collective-permute-start | bytes 15151112 | tf_op jit(solution)/shard_map/ppermute | solution.py:771
  17.9 17.1 %collective-permute-start.4 = (bf16[408,768]{1,0:T(8,128)(2,1)S(1)}, bf16[408,768]{1,0:T(8,128)(2,1)S(1)}, u32[]{:S(2)}, u32[]{:S(2)}) collective-permute-start(bf16[408,768]{1,0:T(8,128)(2,1)S(1)} %pack_time.1), channel_id=1, source_target_pairs={{0,16},{8,24},{16,0},{24,8},{1,17},{9,25},{17,1},{25,9},{2,18},{10... | collective-permute-start | bytes 1880072 | tf_op jit(solution)/shard_map/ppermute | solution.py:771
  35.0 18.9 %collective-permute-start.6 = (bf16[480,768]{1,0:T(8,128)(2,1)S(1)}, bf16[480,768]{1,0:T(8,128)(2,1)S(1)}, u32[]{:S(2)}, u32[]{:S(2)}) collective-permute-start(bf16[480,768]{1,0:T(8,128)(2,1)S(1)} %get-tuple-element.191), channel_id=1, source_target_pairs={{0,16},{8,24},{16,0},{24,8},{1,17},{9,25},{17,1},{25,9},{2,18},{10... | collective-permute-start | bytes 2211848 | tf_op jit(solution)/shard_map/ppermute | solution.py:771
  54.0 21.5 %collective-permute-start.7 = (bf16[384,768]{1,0:T(8,128)(2,1)S(1)}, bf16[384,768]{1,0:T(8,128)(2,1)S(1)}, u32[]{:S(2)}, u32[]{:S(2)}) collective-permute-start(bf16[384,768]{1,0:T(8,128)(2,1)S(1)} %get-tuple-element.192), channel_id=1, source_target_pairs={{0,16},{8,24},{16,0},{24,8},{1,17},{9,25},{17,1},{25,9},{2,18},{10... | collective-permute-start | bytes 1769480 | tf_op jit(solution)/shard_map/ppermute | solution.py:771
  55.7 27.0 %collective-permute-start.8 = (bf16[384,768]{1,0:T(8,128)(2,1)S(1)}, bf16[384,768]{1,0:T(8,128)(2,1)S(1)}, u32[]{:S(2)}, u32[]{:S(2)}) collective-permute-start(bf16[384,768]{1,0:T(8,128)(2,1)S(1)} %get-tuple-element.194), channel_id=1, source_target_pairs={{0,16},{8,24},{16,0},{24,8},{1,17},{9,25},{17,1},{25,9},{2,18},{10... | collective-permute-start | bytes 1769480 | tf_op jit(solution)/shard_map/ppermute | solution.py:771
  56.0 26.9 %collective-permute-start.15 = (bf16[480,768]{1,0:T(8,128)(2,1)S(1)}, bf16[480,768]{1,0:T(8,128)(2,1)S(1)}, u32[]{:S(2)}, u32[]{:S(2)}) collective-permute-start(bf16[480,768]{1,0:T(8,128)(2,1)S(1)} %collective-permute-done.6.refs_4_.refs_3_), channel_id=1, source_target_pairs={{0,8},{8,0},{16,24},{24,16},{1,9},{9,1},{17,25},{25,17},{2,10},{10... | collective-permute-start | bytes 2211848 | tf_op jit(solution)/shard_map/ppermute | solution.py:771
  56.0 18.9 %collective-permute-start.14 = (bf16[480,768]{1,0:T(8,128)(2,1)S(1)}, bf16[480,768]{1,0:T(8,128)(2,1)S(1)}, u32[]{:S(2)}, u32[]{:S(2)}) collective-permute-start(bf16[480,768]{1,0:T(8,128)(2,1)S(1)} %collective-permute-done.6.refs_4_.refs_3_), channel_id=1, source_target_pairs={{0,1},{1,0},{2,3},{3,2},{4,5},{5,4},{6,7},{7,6},{8,9},{9,8},{10,11... | collective-permute-start | bytes 2211848 | tf_op jit(solution)/shard_map/ppermute | solution.py:771
  82.9 23.6 %collective-permute-start.18 = (bf16[384,768]{1,0:T(8,128)(2,1)S(1)}, bf16[384,768]{1,0:T(8,128)(2,1)S(1)}, u32[]{:S(2)}, u32[]{:S(2)}) collective-permute-start(bf16[384,768]{1,0:T(8,128)(2,1)S(1)} %collective-permute-done.7.refs_3_), channel_id=1, source_target_pairs={{0,8},{8,0},{16,24},{24,16},{1,9},{9,1},{17,25},{25,17},{2,10},{10... | collective-permute-start | bytes 1769480 | tf_op jit(solution)/shard_map/ppermute | solution.py:771
  84.9 19.4 %collective-permute-start.17 = (bf16[384,768]{1,0:T(8,128)(2,1)S(1)}, bf16[384,768]{1,0:T(8,128)(2,1)S(1)}, u32[]{:S(2)}, u32[]{:S(2)}) collective-permute-start(bf16[384,768]{1,0:T(8,128)(2,1)S(1)} %collective-permute-done.7.refs_3_), channel_id=1, source_target_pairs={{0,1},{1,0},{2,3},{3,2},{4,5},{5,4},{6,7},{7,6},{8,9},{9,8},{10,11... | collective-permute-start | bytes 1769480 | tf_op jit(solution)/shard_map/ppermute | solution.py:771
  86.5 17.8 %collective-permute-start.20 = (bf16[384,768]{1,0:T(8,128)(2,1)S(1)}, bf16[384,768]{1,0:T(8,128)(2,1)S(1)}, u32[]{:S(2)}, u32[]{:S(2)}) collective-permute-start(bf16[384,768]{1,0:T(8,128)(2,1)S(1)} %collective-permute-done.8.refs_7_), channel_id=1, source_target_pairs={{0,2},{1,3},{2,0},{3,1},{4,6},{5,7},{6,4},{7,5},{8,10},{9,11},{10,... | collective-permute-start | bytes 1769480 | tf_op jit(solution)/shard_map/ppermute | solution.py:771
  127.3 18.8 %collective-permute-start.25 = (bf16[2,768,768]{2,1,0:T(8,128)(2,1)S(1)}, bf16[2,768,768]{2,1,0:T(8,128)(2,1)S(1)}, u32[]{:S(2)}, u32[]{:S(2)}) collective-permute-start(bf16[2,768,768]{2,1,0:T(8,128)(2,1)S(1)} %get-tuple-element.231), channel_id=1, source_target_pairs={{0,8},{8,0},{16,24},{24,16},{1,9},{9,1},{17,25},{25,17},{2,10},{10... | collective-permute-start | bytes 7077896 | tf_op jit(solution)/shard_map/ppermute | solution.py:771
  149.2 32.7 %collective-permute-start.33 = (bf16[2,384,768]{2,1,0:T(8,128)(2,1)S(1)}, bf16[2,384,768]{2,1,0:T(8,128)(2,1)S(1)}, u32[]{:S(2)}, u32[]{:S(2)}) collective-permute-start(bf16[2,384,768]{2,1,0:T(8,128)(2,1)S(1)} %get-tuple-element.235), channel_id=1, source_target_pairs={{0,2},{1,3},{2,0},{3,1},{4,6},{5,7},{6,4},{7,5},{8,10},{9,11},{10,... | collective-permute-start | bytes 3538952 | tf_op jit(solution)/shard_map/ppermute | solution.py:771
  152.3 30.5 %collective-permute-start.32 = (bf16[768,768]{1,0:T(8,128)(2,1)S(1)}, bf16[768,768]{1,0:T(8,128)(2,1)S(1)}, u32[]{:S(2)}, u32[]{:S(2)}) collective-permute-start(bf16[768,768]{1,0:T(8,128)(2,1)S(1)} %get-tuple-element.237), channel_id=1, source_target_pairs={{0,16},{8,24},{16,0},{24,8},{1,17},{9,25},{17,1},{25,9},{2,18},{10... | collective-permute-start | bytes 3538952 | tf_op jit(solution)/shard_map/ppermute | solution.py:771
  153.0 28.0 %collective-permute-start.29 = (bf16[2,384,768]{2,1,0:T(8,128)(2,1)S(1)}, bf16[2,384,768]{2,1,0:T(8,128)(2,1)S(1)}, u32[]{:S(2)}, u32[]{:S(2)}) collective-permute-start(bf16[2,384,768]{2,1,0:T(8,128)(2,1)S(1)} %get-tuple-element.233), channel_id=1, source_target_pairs={{0,1},{1,0},{2,3},{3,2},{4,5},{5,4},{6,7},{7,6},{8,9},{9,8},{10,11... | collective-permute-start | bytes 3538952 | tf_op jit(solution)/shard_map/ppermute | solution.py:771
  162.1 29.6 %collective-permute-start.31 = (bf16[2,384,768]{2,1,0:T(8,128)(2,1)S(1)}, bf16[2,384,768]{2,1,0:T(8,128)(2,1)S(1)}, u32[]{:S(2)}, u32[]{:S(2)}) collective-permute-start(bf16[2,384,768]{2,1,0:T(8,128)(2,1)S(1)} %get-tuple-element.256), channel_id=1, source_target_pairs={{0,8},{8,0},{16,24},{24,16},{1,9},{9,1},{17,25},{25,17},{2,10},{10... | collective-permute-start | bytes 3538952 | tf_op jit(solution)/shard_map/ppermute | solution.py:771
  187.2 20.9 %collective-permute-start.36 = (bf16[2,640,768]{2,1,0:T(8,128)(2,1)S(1)}, bf16[2,640,768]{2,1,0:T(8,128)(2,1)S(1)}, u32[]{:S(2)}, u32[]{:S(2)}) collective-permute-start(bf16[2,640,768]{2,1,0:T(8,128)(2,1)S(1)} %get-tuple-element.275), channel_id=1, source_target_pairs={{0,8},{8,0},{16,24},{24,16},{1,9},{9,1},{17,25},{25,17},{2,10},{10... | collective-permute-start | bytes 5898248 | tf_op jit(solution)/shard_map/ppermute | solution.py:771
  188.6 21.9 %collective-permute-start.35 = (bf16[384,768]{1,0:T(8,128)(2,1)S(1)}, bf16[384,768]{1,0:T(8,128)(2,1)S(1)}, u32[]{:S(2)}, u32[]{:S(2)}) collective-permute-start(bf16[384,768]{1,0:T(8,128)(2,1)S(1)} %get-tuple-element.263), channel_id=1, source_target_pairs={{0,1},{1,0},{2,3},{3,2},{4,5},{5,4},{6,7},{7,6},{8,9},{9,8},{10,11... | collective-permute-start | bytes 1769480 | tf_op jit(solution)/shard_map/ppermute | solution.py:771
  190.1 30.4 %collective-permute-start.39 = (bf16[384,768]{1,0:T(8,128)(2,1)S(1)}, bf16[384,768]{1,0:T(8,128)(2,1)S(1)}, u32[]{:S(2)}, u32[]{:S(2)}) collective-permute-start(bf16[384,768]{1,0:T(8,128)(2,1)S(1)} %get-tuple-element.261), channel_id=1, source_target_pairs={{0,16},{8,24},{16,0},{24,8},{1,17},{9,25},{17,1},{25,9},{2,18},{10... | collective-permute-start | bytes 1769480 | tf_op jit(solution)/shard_map/ppermute | solution.py:771
  192.6 45.9 %collective-permute-start.41 = (bf16[2,192,768]{2,1,0:T(8,128)(2,1)S(1)}, bf16[2,192,768]{2,1,0:T(8,128)(2,1)S(1)}, u32[]{:S(2)}, u32[]{:S(2)}) collective-permute-start(bf16[2,192,768]{2,1,0:T(8,128)(2,1)S(1)} %get-tuple-element.270), channel_id=1, source_target_pairs={{0,1},{1,0},{2,3},{3,2},{4,5},{5,4},{6,7},{7,6},{8,9},{9,8},{10,11... | collective-permute-start | bytes 1769480 | tf_op jit(solution)/shard_map/ppermute | solution.py:771
  209.2 27.5 %collective-permute-start.42 = (bf16[640,768]{1,0:T(8,128)(2,1)S(1)}, bf16[640,768]{1,0:T(8,128)(2,1)S(1)}, u32[]{:S(2)}, u32[]{:S(2)}) collective-permute-start(bf16[640,768]{1,0:T(8,128)(2,1)S(1)} %get-tuple-element.277), channel_id=1, source_target_pairs={{0,16},{8,24},{16,0},{24,8},{1,17},{9,25},{17,1},{25,9},{2,18},{10... | collective-permute-start | bytes 2949128 | tf_op jit(solution)/shard_map/ppermute | solution.py:771
  222.4 18.8 %collective-permute-start.48 = (bf16[96,768]{1,0:T(8,128)(2,1)S(1)}, bf16[96,768]{1,0:T(8,128)(2,1)S(1)}, u32[]{:S(2)}, u32[]{:S(2)}) collective-permute-start(bf16[96,768]{1,0:T(8,128)(2,1)S(1)} %get-tuple-element.288), channel_id=1, source_target_pairs={{0,4},{1,5},{2,6},{3,7},{4,0},{5,1},{6,2},{7,3},{8,12},{9,13},{10,... | collective-permute-start | bytes 442376 | tf_op jit(solution)/shard_map/ppermute | solution.py:771
  241.3 21.0 %collective-permute-start.54 = (bf16[96,768]{1,0:T(8,128)(2,1)S(1)}, bf16[96,768]{1,0:T(8,128)(2,1)S(1)}, u32[]{:S(2)}, u32[]{:S(2)}) collective-permute-start(bf16[96,768]{1,0:T(8,128)(2,1)S(1)} %add_convert_fusion.1.mine), channel_id=1, source_target_pairs={{0,4},{1,5},{2,6},{3,7},{4,0},{5,1},{6,2},{7,3},{8,12},{9,13},{10,... | collective-permute-start | bytes 442376 | tf_op jit(solution)/shard_map/ppermute | solution.py:771
  265.9 20.6 %collective-permute-start.65 = (bf16[192,768]{1,0:T(8,128)(2,1)S(1)}, bf16[192,768]{1,0:T(8,128)(2,1)S(1)}, u32[]{:S(2)}, u32[]{:S(2)}) collective-permute-start(bf16[192,768]{1,0:T(8,128)(2,1)S(1)} %join.13.mine), channel_id=1, source_target_pairs={{0,1},{1,0},{2,3},{3,2},{4,5},{5,4},{6,7},{7,6},{8,9},{9,8},{10,11... | collective-permute-start | bytes 884744 | tf_op jit(solution)/shard_map/ppermute | solution.py:771
  287.1 17.7 %collective-permute-start.67 = (bf16[384,768]{1,0:T(8,128)(2,1)S(1)}, bf16[384,768]{1,0:T(8,128)(2,1)S(1)}, u32[]{:S(2)}, u32[]{:S(2)}) collective-permute-start(bf16[384,768]{1,0:T(8,128)(2,1)S(1)} %join.17.mine), channel_id=1, source_target_pairs={{0,2},{1,3},{2,0},{3,1},{4,6},{5,7},{6,4},{7,5},{8,10},{9,11},{10,... | collective-permute-start | bytes 1769480 | tf_op jit(solution)/shard_map/ppermute | solution.py:771
  (81 other events, 788.9 us)
